TPU v7x, 32 devices: a whole 2x2x4 slice. The times are simulated.
32 devices in a mesh: dp: 8 (over y, x, core), mp: 4 (over z).
Axes of the slice: x: 2, y: 2, z: 4, core: 2. Of those that a mesh axis runs over, the one named last changes fastest.
Arguments:
- tokens: bfloat16 [8192, 4096], P(('dp', 'mp')), may hold values from -600 to 600
- norm_gain: float32 [4096], replicated, may hold values from 0.5 to 2
- query_weight: bfloat16 [4096, 4096], P(None, 'mp'), may hold values from -0.09375 to 0.09375
- output_weight: bfloat16 [4096, 4096], P('mp'), may hold values from -0.75 to 0.75
- key_cache: bfloat16 [64, 128, 4096], P('dp', None, 'mp'), may hold values from -72 to 72
- value_cache: bfloat16 [64, 128, 4096], P('dp', None, 'mp'), may hold values from -6 to 6
- owners: int32 [128, 2], P('dp'), may hold values from 0 to 7, as said below
- slot_ids: int32 [128, 2], P('dp'), may hold values from 0 to 7
- valid_counts: int32 [128], P('dp'), may hold values from 0 to 2
Outputs:
- cross_out: bfloat16 [8192, 4096], P(('dp', 'mp'))
Inputs may be any that keep to these rules, and one draw needn't show every extreme that they name: `owners`: each index of dp lists 2 x 16 neighbours; at most 4 of them lie with one owner, and one owner holds exactly 4 of the listed neighbours of every index of dp.
All inputs are finite; a program needn't handle non-finite values.
Results may differ from a plain program's by a relative error of at most 0.023.
Values may be sent and summed in bfloat16 or wider, within the bound.
No kernel may reach another device: no remote copies, remote signals or barrier semaphores. Data moves between devices by JAX's collectives and lax.ppermute only.
A program may use at most 128 MiB of HBM per device.

v0:
```python
import math

import jax
import jax.numpy as jnp
from jax import lax
from jax.sharding import PartitionSpec as P

HD = 128
M = 64
NL = 128


def layer_norm(token_rows, norm_gain):
    values = token_rows.astype(jnp.float32)
    row_mean = jnp.mean(values, axis=-1, keepdims=True)
    centered = values - row_mean
    variance = jnp.mean(centered * centered, axis=-1, keepdims=True)
    return (centered * lax.rsqrt(variance + 1e-05) * norm_gain).astype(jnp.bfloat16)


def span_attention(queries, key_blocks, value_blocks, valid_counts, head_count):
    spans, length, local_width = queries.shape
    query_heads = queries.reshape(spans, length, head_count, HD)
    key_heads = key_blocks.reshape(spans, -1, head_count, HD)
    value_heads = value_blocks.reshape(spans, -1, head_count, HD)
    scores = jnp.einsum(
        "cmhd,ckhd->chmk", query_heads, key_heads, preferred_element_type=jnp.float32
    )
    usable = (jnp.arange(key_heads.shape[1], dtype=jnp.int32) // NL)[None, :] < valid_counts[
        :, None
    ]
    usable = usable[:, None, None, :]
    masked = jnp.where(usable, scores, -1e30)
    highest = jnp.max(masked, axis=-1, keepdims=True)
    weights = jnp.where(usable, jnp.exp(masked - highest), 0.0)
    totals = jnp.sum(weights, axis=-1) + (valid_counts == 0).astype(jnp.float32)[:, None, None]
    mixture = jnp.einsum(
        "chmk,ckhd->cmhd",
        weights.astype(jnp.bfloat16),
        value_heads,
        preferred_element_type=jnp.float32,
    )
    mixture = mixture / jnp.transpose(totals, (0, 2, 1))[..., None]
    return mixture.reshape(spans, length, local_width).astype(jnp.bfloat16)


def on_device(
    tokens,
    norm_gain,
    query_weight,
    output_weight,
    key_cache,
    value_cache,
    owners,
    slot_ids,
    valid_counts,
):
    dp_count = lax.axis_size("dp")
    local_width = query_weight.shape[1]
    head_count = local_width // HD
    spans = valid_counts.shape[0]
    neighbours = 2 * spans
    capacity = max(2, (neighbours + dp_count - 1) // dp_count)
    score_scale = 1.0 / math.sqrt(HD)
    normed = layer_norm(tokens, norm_gain)
    queries = (
        jnp.dot(
            lax.all_gather(normed, "mp", axis=0, tiled=True),
            query_weight,
            preferred_element_type=jnp.float32,
        )
        * score_scale
    ).astype(jnp.bfloat16)
    seq_rows = queries.shape[0]
    shifted = jnp.concatenate(
        [queries[M - 1 :], jnp.zeros((M - 1, local_width), jnp.bfloat16)], axis=0
    )
    shifted = shifted.reshape(spans, M, local_width)
    owner_list = owners.reshape(-1)
    slot_list = slot_ids.reshape(-1)
    ordinal = jnp.arange(neighbours, dtype=jnp.int32)
    earlier = (owner_list[:, None] == owner_list[None, :]) & (ordinal[None, :] < ordinal[:, None])
    position = owner_list * capacity + jnp.sum(earlier.astype(jnp.int32), axis=1)
    placed = position[None, :] == jnp.arange(dp_count * capacity, dtype=jnp.int32)[:, None]
    slot_table = jnp.sum(jnp.where(placed, slot_list[None, :], 0), axis=1).reshape(
        dp_count, capacity
    )
    incoming = lax.all_to_all(slot_table, "dp", split_axis=0, concat_axis=0, tiled=True)
    flat_slots = incoming.reshape(-1)
    sent_keys = jnp.take(key_cache, flat_slots, axis=0).reshape(dp_count, capacity, NL, local_width)
    sent_values = jnp.take(value_cache, flat_slots, axis=0).reshape(
        dp_count, capacity, NL, local_width
    )
    got_keys, got_values = (
        lax.all_to_all(sent_keys, "dp", split_axis=0, concat_axis=0, tiled=True),
        lax.all_to_all(sent_values, "dp", split_axis=0, concat_axis=0, tiled=True),
    )
    key_blocks = jnp.take(got_keys.reshape(dp_count * capacity, NL, local_width), position, axis=0)
    value_blocks = jnp.take(
        got_values.reshape(dp_count * capacity, NL, local_width), position, axis=0
    )
    key_blocks = key_blocks.reshape(spans, 2 * NL, local_width)
    value_blocks = value_blocks.reshape(spans, 2 * NL, local_width)
    attended = span_attention(shifted, key_blocks, value_blocks, valid_counts, head_count)
    flat_rows = attended.reshape(seq_rows, local_width)
    attended = jnp.concatenate(
        [jnp.zeros((M - 1, local_width), jnp.bfloat16), flat_rows[: seq_rows - M + 1]], axis=0
    )
    return lax.psum_scatter(
        jnp.dot(attended, output_weight, preferred_element_type=jnp.float32).astype(jnp.bfloat16),
        "mp",
        scatter_dimension=0,
        tiled=True,
    )


def solution(mesh):
    placed = (
        P(("dp", "mp"), None),
        P(),
        P(None, "mp"),
        P("mp", None),
        P("dp", None, "mp"),
        P("dp", None, "mp"),
        P("dp", None),
        P("dp", None),
        P("dp"),
    )
    return jax.shard_map(
        on_device, mesh=mesh, in_specs=placed, out_specs=P(("dp", "mp"), None), check_vma=False
    )
```

profile of v0, /device:TPU:8, one launch (start us, length us, event | category | flops | bytes accessed | tf_op | source)
XLA Modules:
  0.0 482.1 jit_solution(1603596885250871835)
XLA Ops:
  6.5 0.0 copy-start
  6.5 0.9 copy.26
  7.4 0.1 reshape.100
  7.5 0.2 convert_reduce_fusion.1
  7.7 0.8 copy.27
  8.5 0.1 broadcast_in_dim.63
  8.6 0.1 select_reduce_fusion.1
  8.7 0.1 all_to_all.12
  8.8 8.2 %all_to_all.19 = s32[8,1,4]{2,1,0:T(1,128)S(1)} all-to-all(s32[8,1,4]{2,1,0:T(1,128)S(1)} %bitcast.43), channel_id=1, replica_groups=mesh['dp'=8,'mp'=4] {'dp'}, dimensions={0} | all-to-all | bytes 256 | tf_op jit(solution)/shard_map/all_to_all | solution.py:88
  17.0 0.5 broadcast.108
  17.5 0.7 reduce.3
  18.1 0.1 reshape.101
  18.2 0.0 copy-done
  18.3 5.0 %gather_fusion = bf16[32,128,1024]{2,1,0:T(8,128)(2,1)} fusion(bf16[8,128,1024]{2,1,0:T(8,128)(2,1)S(1)} %copy-done, s32[1024]{0:T(1024)S(1)} %pad_clamp_fusion.1), kind=kCustom, calls=%fused_computation.clone | custom fusion | bytes 16777344 | tf_op jit(solution)/shard_map/jit(_take)/gather | solution.py:91
  23.2 6.6 %gather_fusion.2 = bf16[32,128,1024]{2,1,0:T(8,128)(2,1)} fusion(bf16[8,128,1024]{2,1,0:T(8,128)(2,1)} %param.17, s32[1024]{0:T(1024)S(1)} %pad_clamp_fusion.1), kind=kCustom, calls=%fused_computation.2.clone | custom fusion | bytes 16777344 | tf_op jit(solution)/shard_map/jit(_take)/gather | solution.py:90
  29.8 11.6 %broadcast_select_fusion.3 = (bf16[32,128,1024]{2,1,0:T(8,128)(2,1)}, bf16[32,128,1024]{2,1,0:T(8,128)(2,1)}) fusion(bf16[32,128,1024]{2,1,0:T(8,128)(2,1)} %gather_fusion, pred[32]{0:T(512)(128)(4,1)S(1)} %compare_and_fusion.1, bf16[32,128,1024]{2,1,0:T(8,128)(2,1)} %gather_fusion.2), kind=kLoop, calls=%fused_computation.13 | loop fusion | flops 8388608 | bytes 33554464 | tf_op jit(solution)/shard_map/jit(_take)/select_n | solution.py:91
  41.5 0.0 copy-start.3
  41.5 0.0 copy-start.4
  41.5 5.2 %all-to-all-start.2 = ((bf16[8,4,128,1024]{3,2,1,0:T(8,128)(2,1)}), bf16[8,4,128,1024]{3,2,1,0:T(8,128)(2,1)}, u32[]{:S(2)}, u32[]{:S(2)}) async-start(bf16[8,4,128,1024]{3,2,1,0:T(8,128)(2,1)} %bitcast.33), calls=%async_computation.2 | async-start | bytes 16777216 | tf_op jit(solution)/shard_map/all_to_all | solution.py:95
  46.7 0.0 all-gather.2.cloned.1.call-start
  46.7 0.0 copy-done.3
  46.7 0.4 convert_reduce_fusion
  47.1 0.7 fusion.10
  47.8 0.0 copy-done.4
  47.8 2.2 fusion.12
  50.0 0.0 all-gather.2.cloned.1.call-update
  50.0 90.7 %all-to-all-done.2 = bf16[8,4,128,1024]{3,2,1,0:T(8,128)(2,1)} async-done(((bf16[8,4,128,1024]{3,2,1,0:T(8,128)(2,1)}), bf16[8,4,128,1024]{3,2,1,0:T(8,128)(2,1)}, u32[]{:S(2)}, u32[]{:S(2)}) %all-to-all-start.2) | async-done | bytes 8388640 | tf_op jit(solution)/shard_map/all_to_all | solution.py:95
  140.7 0.0 copy-start.5
  140.7 5.2 %all-to-all-start.1 = ((bf16[8,4,128,1024]{3,2,1,0:T(8,128)(2,1)}), bf16[8,4,128,1024]{3,2,1,0:T(8,128)(2,1)}, u32[]{:S(2)}, u32[]{:S(2)}) async-start(bf16[8,4,128,1024]{3,2,1,0:T(8,128)(2,1)} %bitcast.32), calls=%async_computation.1 | async-start | bytes 16777216 | tf_op jit(solution)/shard_map/all_to_all | solution.py:96
  145.9 0.2 reduce-scatter.2.cloned.1.call-start
  146.2 0.0 copy-done.5
  146.2 0.1 broadcast_compare_fusion
  146.3 8.4 %gather_fusion.3 = bf16[32,128,1024]{2,1,0:T(8,128)(2,1)} fusion(bf16[32,128,1024]{2,1,0:T(8,128)(2,1)} %bitcast.4, s32[1024]{0:T(1024)S(1)} %pad_clamp_fusion), kind=kCustom, calls=%fused_computation.3.clone | custom fusion | bytes 16777344 | tf_op jit(solution)/shard_map/jit(_take)/gather | solution.py:98
  154.7 85.3 %all-to-all-done.1 = bf16[8,4,128,1024]{3,2,1,0:T(8,128)(2,1)} async-done(((bf16[8,4,128,1024]{3,2,1,0:T(8,128)(2,1)}), bf16[8,4,128,1024]{3,2,1,0:T(8,128)(2,1)}, u32[]{:S(2)}, u32[]{:S(2)}) %all-to-all-start.1) | async-done | bytes 8388640 | tf_op jit(solution)/shard_map/all_to_all | solution.py:96
  240.0 8.4 %gather_fusion.1 = bf16[32,128,1024]{2,1,0:T(8,128)(2,1)} fusion(bf16[32,128,1024]{2,1,0:T(8,128)(2,1)} %bitcast.2, s32[1024]{0:T(1024)S(1)} %pad_clamp_fusion), kind=kCustom, calls=%fused_computation.1.clone | custom fusion | bytes 16777344 | tf_op jit(solution)/shard_map/jit(_take)/gather | solution.py:99
  248.4 11.6 %broadcast_select_fusion.1 = (bf16[32,128,1024]{2,1,0:T(8,128)(2,1)}, bf16[32,128,1024]{2,1,0:T(8,128)(2,1)}) fusion(bf16[32,128,1024]{2,1,0:T(8,128)(2,1)} %gather_fusion.1, pred[32]{0:T(512)(128)(4,1)S(1)} %get-tuple-element.6, bf16[32,128,1024]{2,1,0:T(8,128)(2,1)} %gather_fusion.3), kind=kLoop, calls=%fused_computation.11 | loop fusion | flops 8388608 | bytes 33554464 | tf_op jit(solution)/shard_map/jit(_take)/select_n | solution.py:99
  260.0 8.8 %copy.35 = bf16[512,8,8,128]{3,2,1,0:T(8,128)(2,1)} copy(bf16[512,8,8,128]{3,1,2,0:T(8,128)(2,1)} %bitcast.35) | data formatting | bytes 16777216
  268.7 8.8 %copy.34 = bf16[512,8,8,128]{3,2,1,0:T(8,128)(2,1)} copy(bf16[512,8,8,128]{3,1,2,0:T(8,128)(2,1)} %bitcast.34) | data formatting | bytes 16777216
  277.5 0.0 all-gather.2.cloned.1.call-done
  277.5 12.8 %fusion.28 = f32[1024,1024]{1,0:T(8,128)S(1)} fusion(bf16[1024,4096]{1,0:T(8,128)(2,1)} %all-gather.2.cloned.1.call-done, bf16[4096,1024]{1,0:T(8,128)(2,1)} %param.15), kind=kOutput, calls=%fused_computation.59 | convolution fusion | flops 8589934592 | bytes 20971520 | tf_op jit(solution)/shard_map/dot_general | solution.py:67
  290.3 0.0 copy-start.2
  290.3 0.6 fusion.17
  290.9 0.2 pad_bitcast_fusion
  291.2 0.6 copy.33
  291.8 1.9 copy-done.2
  293.7 0.0 slice-start
  293.7 6.3 %fusion.3 = f32[16,8,64,256]{3,2,1,0:T(8,128)} fusion(bf16[16,256,8,128]{3,2,1,0:T(8,128)(2,1)S(1)} %bitcast.36, bf16[16,64,8,128]{3,2,1,0:T(8,128)(2,1)S(1)} %bitcast.37), kind=kOutput, calls=%fused_computation.7 | convolution fusion | flops 536870912 | bytes 18874368 | tf_op jit(solution)/shard_map/cmhd,ckhd->chmk/dot_general | solution.py:26
  299.9 0.0 slice-start.1
  299.9 10.8 %fusion.27 = (f32[16,8,64]{2,1,0:T(8,128)S(1)}, bf16[16,8,64,256]{3,2,1,0:T(8,128)(2,1)}) fusion(f32[16,8,64,256]{3,2,1,0:T(8,128)} %fusion.3, pred[16,256]{1,0:T(8,128)(4,1)S(1)} %broadcast_compare_fusion), kind=kOutput, calls=%fused_computation.58 | output fusion | flops 12583167 | bytes 12619776 | tf_op jit(solution)/shard_map/sub | solution.py:35
  310.7 0.1 add_bitcast_fusion
  310.8 0.0 slice-done
  310.8 0.0 slice-done.1
  310.9 3.6 fusion.13
  314.4 1.8 copy.32
  316.2 0.6 copy.46
  316.9 0.2 slice.17
  317.0 0.0 copy-start.1
  317.0 14.6 %convolution_convert_fusion = bf16[1024,4096]{1,0:T(8,128)(2,1)} fusion(bf16[1024,4096]{1,0:T(8,128)(2,1)} %param.16, bf16[961,1024]{1,0:T(8,128)(2,1)S(1)} %slice.17), kind=kOutput, calls=%fused_computation.14 | convolution fusion | flops 8594128896 | bytes 18745344 | tf_op jit(solution)/shard_map/dot_general | solution.py:110
  331.6 0.0 reduce-scatter.2.cloned.1.call-update
  331.6 143.6 %reduce-scatter.2.cloned.1.call-done = bf16[256,4096]{1,0:T(8,128)(2,1)} async-done(((bf16[1024,4096]{1,0:T(8,128)(2,1)}), bf16[256,4096]{1,0:T(8,128)(2,1)}) %reduce-scatter.2.cloned.1.call-update) | async-done | bytes 2097168 | tf_op jit(solution)/shard_map/reduce_scatter | solution.py:109
  475.2 0.0 copy-done.1
  (11 shorter events, 0.1 us)
Async XLA Ops:
  6.5 11.7 %copy-start = (bf16[8,128,1024]{2,1,0:T(8,128)(2,1)S(1)}, bf16[8,128,1024]{2,1,0:T(8,128)(2,1)}, u32[]{:S(2)}) copy-start(bf16[8,128,1024]{2,1,0:T(8,128)(2,1)} %param.18) | copy-start | bytes 6291460
  41.5 5.2 %copy-start.3 = (bf16[256,4096]{1,0:T(8,128)(2,1)S(1)}, bf16[256,4096]{1,0:T(8,128)(2,1)}, u32[]{:S(2)}) copy-start(bf16[256,4096]{1,0:T(8,128)(2,1)} %param.13) | copy-start | bytes 6291460
  41.5 6.3 %copy-start.4 = (f32[4096]{0:T(1024)S(1)}, f32[4096]{0:T(1024)}, u32[]{:S(2)}) copy-start(f32[4096]{0:T(1024)} %param.14) | copy-start | bytes 49156
  41.5 99.2 %all-to-all-start.2 = ((bf16[8,4,128,1024]{3,2,1,0:T(8,128)(2,1)}), bf16[8,4,128,1024]{3,2,1,0:T(8,128)(2,1)}, u32[]{:S(2)}, u32[]{:S(2)}) async-start(bf16[8,4,128,1024]{3,2,1,0:T(8,128)(2,1)} %bitcast.33), calls=%async_computation.2 | async-start | bytes 16777216 | tf_op jit(solution)/shard_map/all_to_all | solution.py:95
  46.7 230.8 %all-gather.2.cloned.1.call-start = ((), (), s32[]{:S(2)}) async-start(), calls=%async_computation.4 | async-start | bytes 10485760 | tf_op jit(solution)/shard_map/all_gather | solution.py:68
  140.7 5.5 %copy-start.5 = (s32[16]{0:T(128)S(1)}, s32[16]{0:T(128)}, u32[]{:S(2)}) copy-start(s32[16]{0:T(128)} %param.21) | copy-start | bytes 196
  140.7 99.3 %all-to-all-start.1 = ((bf16[8,4,128,1024]{3,2,1,0:T(8,128)(2,1)}), bf16[8,4,128,1024]{3,2,1,0:T(8,128)(2,1)}, u32[]{:S(2)}, u32[]{:S(2)}) async-start(bf16[8,4,128,1024]{3,2,1,0:T(8,128)(2,1)} %bitcast.32), calls=%async_computation.1 | async-start | bytes 16777216 | tf_op jit(solution)/shard_map/all_to_all | solution.py:96
  145.9 329.3 %reduce-scatter.2.cloned.1.call-start = ((), (), s32[]{:S(2)}) async-start(), calls=%async_computation.5 | async-start | bytes 10485760 | tf_op jit(solution)/shard_map/reduce_scatter | solution.py:109
  290.3 3.4 copy-start.2
  293.7 17.1 %slice-start = ((s8[8388608]{0:T(1024)(128)(4,1)}), s8[4194304]{0:T(1024)(128)(4,1)S(1)}, s32[]{:S(2)}) async-start(s8[8388608]{0:T(1024)(128)(4,1)} %bitcast.38), calls=%async_computation.6 | async-start | bytes 8388608
  299.9 10.9 %slice-start.1 = ((s8[8388608]{0:T(1024)(128)(4,1)}), s8[4194304]{0:T(1024)(128)(4,1)S(1)}, s32[]{:S(2)}) async-start(s8[8388608]{0:T(1024)(128)(4,1)} %bitcast.38), calls=%async_computation.7 | async-start | bytes 8388608
  317.0 158.2 %copy-start.1 = (bf16[8,128,1024]{2,1,0:T(8,128)(2,1)S(1)}, bf16[8,128,1024]{2,1,0:T(8,128)(2,1)}, u32[]{:S(2)}) copy-start(bf16[8,128,1024]{2,1,0:T(8,128)(2,1)} %param.18) | copy-start | bytes 6291460
Sparse Core Ops, SparseCore 0:
  50.1 148.1 all-gather.1
  331.7 143.4 reduce-scatter.1
where the time goes:
time: 485 us; the launch traced here: 482 us
  waiting for transfers between devices  320 us (66%)
  local copies, waits for them, and re-layouts  53.7 us (11%)
  other arithmetic  39.1 us (8%)
  matrix products  37.2 us (8%)
  between operations  13.6 us (3%)
  starting transfers between devices  10.6 us (2%)
  blocking collectives  8.19 us (2%)
    reduce_scatter x1, waiting for transfers between devices, on_device(): lax.psum_scatter(jnp.dot(attended, output_weight, preferred_element_type=...  144 us
    all_to_all x1, waiting for transfers between devices, on_device(): lax.all_to_all(sent_keys, 'dp', split_axis=0, concat_axis=0, tiled=True)  90.7 us
    all_to_all x1, waiting for transfers between devices, on_device(): lax.all_to_all(sent_values, 'dp', split_axis=0, concat_axis=0, tiled=True)  85.3 us
    unnamed x23, local copies, waits for them, and re-layouts  22.6 us
    dot_general x1, matrix products, on_device(): jnp.dot(attended, output_weight, preferred_element_type=jnp.float32)  14.6 us
    dot_general x1, matrix products, on_device(): jnp.dot(lax.all_gather(normed, 'mp', axis=0, tiled=True), query_weight, p...  12.8 us
    select_n x2, other arithmetic, on_device(): jnp.take(value_cache, flat_slots, axis=0)  11.7 us
    select_n x2, other arithmetic, on_device(): jnp.take(got_values.reshape(dp_count * capacity, NL, local_width), positi...  11.6 us
  transfers between devices with their start and end apart: 4, of which 3 were waited for; matrix products, arithmetic and copies ran while one was open for 10% of the time, Pallas kernels for 0%

commit v1 on v0

--- a/solution.py
+++ b/solution.py
@@ -1,8 +1,11 @@
+import functools
 import math
 
 import jax
 import jax.numpy as jnp
 from jax import lax
+from jax.experimental import pallas as pl
+from jax.experimental.pallas import tpu as pltpu
 from jax.sharding import PartitionSpec as P
 
 HD = 128
@@ -44,7 +47,7 @@
     return mixture.reshape(spans, length, local_width).astype(jnp.bfloat16)
 
 
-def on_device(
+def general_on_device(
     tokens,
     norm_gain,
     query_weight,
@@ -114,6 +117,237 @@
     )
 
 
+SHARD_ORDER = ((3, 2, 1, 0), (3, 2, 0, 1), (0, 1, 3, 2), (0, 1, 2, 3))
+QUERY_ARRAY = {0: 0, -1: 1, 1: 2, 2: 3, -2: 3, 3: 4, -3: 4}
+OUTWARD = ((1, 0), (2, 3))
+INWARD = ((0, 1), (3, 2))
+MIDDLE = ((1, 2), (2, 1))
+
+
+def attention_kernel(step, blocks, steps_ref, relative_ref, slots_ref, counts_ref, *refs):
+    query_refs = refs[:5]
+    key_refs = refs[5:13]
+    value_refs = refs[13:21]
+    out_ref = refs[21]
+    query_buf, key_buf, value_buf, total_buf, query_sem, cache_sem = refs[22:]
+    shard = steps_ref[2 * step]
+    query_array = steps_ref[2 * step + 1]
+    rows, width = query_buf.shape
+    head_count = width // HD
+
+    for index, query_ref in enumerate(query_refs):
+
+        @pl.when(query_array == index)
+        def _():
+            pltpu.make_async_copy(query_ref, query_buf, query_sem).start()
+
+    def entry_of(turn):
+        span = shard * blocks - 1 + turn
+        index = jnp.maximum(span, 0)
+        return index, jnp.where(span < 0, 0, counts_ref[index])
+
+    def copies(turn, neighbour, slot, index):
+        for kind, (source, buf) in enumerate(((key_refs, key_buf), (value_refs, value_buf))):
+            yield pltpu.make_async_copy(
+                source[index].at[slot],
+                buf.at[turn, pl.ds(neighbour * NL, NL)],
+                cache_sem.at[turn, 2 * neighbour + kind],
+            )
+
+    def fetch(turn, carry):
+        entry, count = entry_of(turn)
+
+        @pl.when(count > 0)
+        def _():
+            for neighbour in range(2):
+                relative = relative_ref[entry * 2 + neighbour]
+                slot = slots_ref[entry * 2 + neighbour]
+                for index in range(8):
+
+                    @pl.when(relative == index)
+                    def _():
+                        for copy in copies(turn, neighbour, slot, index):
+                            copy.start()
+
+        return carry
+
+    lax.fori_loop(0, blocks + 1, fetch, 0)
+    pltpu.make_async_copy(query_refs[0], query_buf, query_sem).wait()
+
+    def attend(turn, carry):
+        _, count = entry_of(turn)
+        start = pl.multiple_of(jnp.minimum(turn, blocks - 1) * M, M)
+        before_start = pl.multiple_of(jnp.maximum(turn - 1, 0) * M, M)
+        earlier = pl.ds(pl.multiple_of(before_start + M - 8, 8), 8)
+
+        @pl.when(count > 0)
+        def _():
+            for neighbour in range(2):
+                for copy in copies(turn, neighbour, 0, 0):
+                    copy.wait()
+            real = lax.broadcasted_iota(jnp.int32, (M, 2 * NL), 1) < count * NL
+            row = lax.broadcasted_iota(jnp.int32, (M, HD), 0)
+            for head in range(head_count):
+                columns = pl.ds(head * HD, HD)
+                queries = query_buf[pl.ds(start, M), columns].astype(jnp.float32)
+                before = query_buf[pl.ds(before_start, M), columns].astype(jnp.float32)
+                queries = jnp.where(row == M - 1, before, queries).astype(jnp.bfloat16)
+                scores = lax.dot_general(
+                    queries,
+                    key_buf[turn, :, columns],
+                    (((1,), (1,)), ((), ())),
+                    preferred_element_type=jnp.float32,
+                )
+                scores = jnp.where(real, scores, -1e30)
+                weights = jnp.exp(scores - jnp.max(scores, axis=-1, keepdims=True))
+                totals = jnp.sum(weights, axis=-1, keepdims=True)
+                mixture = jnp.dot(
+                    weights.astype(jnp.bfloat16),
+                    value_buf[turn, :, columns],
+                    preferred_element_type=jnp.float32,
+                )
+                mixture = mixture / totals
+
+                @pl.when(turn < blocks)
+                def _():
+                    total_buf[pl.ds(start, M), columns] = mixture
+
+                total_buf[earlier, columns] = jnp.where(
+                    row[:8] == 7, mixture[M - 8 :], total_buf[earlier, columns]
+                )
+
+        @pl.when(count <= 0)
+        def _():
+            @pl.when(turn < blocks)
+            def _():
+                total_buf[pl.ds(start, M), :] = jnp.zeros((M, width), jnp.float32)
+
+            row = lax.broadcasted_iota(jnp.int32, (8, width), 0)
+            total_buf[earlier, :] = jnp.where(row == 7, 0.0, total_buf[earlier, :])
+
+        return carry
+
+    lax.fori_loop(0, blocks + 1, attend, 0)
+    out_ref[...] = total_buf[...].astype(jnp.bfloat16)
+
+
+def shard_attention(step, steps, relative, slots, counts, queries, keys, values):
+    rows, width = queries[0].shape
+    blocks = rows // M
+    anywhere = pl.BlockSpec(memory_space=pl.ANY)
+    return pl.pallas_call(
+        functools.partial(attention_kernel, step, blocks),
+        out_shape=jax.ShapeDtypeStruct((rows, width), jnp.bfloat16),
+        grid_spec=pltpu.PrefetchScalarGridSpec(
+            num_scalar_prefetch=4,
+            grid=(1,),
+            in_specs=[anywhere] * 21,
+            out_specs=pl.BlockSpec((rows, width), lambda i, *_: (0, 0)),
+            scratch_shapes=[
+                pltpu.VMEM((rows, width), jnp.bfloat16),
+                pltpu.VMEM((blocks + 1, 2 * NL, width), jnp.bfloat16),
+                pltpu.VMEM((blocks + 1, 2 * NL, width), jnp.bfloat16),
+                pltpu.VMEM((rows, width), jnp.float32),
+                pltpu.SemaphoreType.DMA,
+                pltpu.SemaphoreType.DMA((blocks + 1, 4)),
+            ],
+        ),
+        compiler_params=pltpu.CompilerParams(vmem_limit_bytes=24 << 20),
+        cost_estimate=pl.CostEstimate(
+            flops=4 * rows * 2 * NL * width,
+            bytes_accessed=2 * (rows * width * 2 + (blocks + 1) * 2 * NL * width * 2),
+            transcendentals=rows * 2 * NL * (width // HD),
+        ),
+    )(steps, relative, slots, counts, *queries, *keys, *values)
+
+
+def swap(values, bits):
+    return lax.ppermute(values, "dp", [(i, i ^ bits) for i in range(8)])
+
+
+def along(values, pairs):
+    return lax.ppermute(values, "mp", list(pairs))
+
+
+def cube_on_device(
+    tokens,
+    norm_gain,
+    query_weight,
+    output_weight,
+    key_cache,
+    value_cache,
+    owners,
+    slot_ids,
+    valid_counts,
+):
+    score_scale = 1.0 / math.sqrt(HD)
+    place = lax.axis_index("mp")
+
+    def project(rows):
+        return (jnp.dot(rows, query_weight, preferred_element_type=jnp.float32) * score_scale).astype(
+            jnp.bfloat16
+        )
+
+    together = lax.optimization_barrier
+    normed = layer_norm(tokens, norm_gain)
+    below = along(normed, ((0, 1), (1, 2), (2, 3)))
+    above = along(normed, ((1, 0), (2, 1), (3, 2)))
+    keys = [key_cache, swap(key_cache, 1), swap(key_cache, 2)] + [None] * 5
+    values = [value_cache, swap(value_cache, 1), None, None, swap(value_cache, 4)] + [None] * 3
+    below, above, keys[2], values[4], key_cache, value_cache = together(
+        (below, above, keys[2], values[4], key_cache, value_cache)
+    )
+    below_two = along(below, ((1, 2), (2, 3)))
+    above_two = along(above, ((1, 0), (2, 1)))
+    values[2], keys[4] = swap(value_cache, 2), swap(key_cache, 4)
+    keys[3], values[5] = swap(keys[2], 1), swap(values[4], 1)
+    below_two, above_two, values[2], keys[4], keys_x, values_y = together(
+        (below_two, above_two, values[2], keys[4], keys[2], values[4])
+    )
+    two = jnp.where(place >= 2, below_two, above_two)
+    three = along(two, OUTWARD)
+    keys[6], values[6] = swap(keys_x, 4), swap(values_y, 2)
+    values[3], keys[5] = swap(values[2], 1), swap(keys[4], 1)
+    keys[7], values[7] = swap(keys[6], 1), swap(values[6], 1)
+    queries = [project(rows) for rows in (normed, below, above, two, three)]
+
+    table = [
+        [number for shard in order for number in (shard, QUERY_ARRAY[shard - z])]
+        for z, order in enumerate(SHARD_ORDER)
+    ]
+    steps = lax.dynamic_index_in_dim(jnp.array(table, jnp.int32), place, 0, keepdims=False)
+    relative = owners.reshape(-1) ^ lax.axis_index("dp")
+    slots = slot_ids.reshape(-1)
+
+    def part(step):
+        attended = shard_attention(step, steps, relative, slots, valid_counts, queries, keys, values)
+        return jnp.dot(attended, output_weight, preferred_element_type=jnp.float32).astype(jnp.bfloat16)
+
+    def plus(*terms):
+        total = terms[0].astype(jnp.float32)
+        for term in terms[1:]:
+            total = total + term.astype(jnp.float32)
+        return total.astype(jnp.bfloat16)
+
+    first = part(0)
+    first_in = along(first, INWARD)
+    second = part(1)
+    second_in = along(second, INWARD)
+    first_middle = along(plus(first, first_in), MIDDLE)
+    third = part(2)
+    third_in = along(third, INWARD)
+    second_middle = along(plus(second, second_in), MIDDLE)
+    third_out = along(plus(third, first_middle), OUTWARD)
+    own = part(3)
+    return plus(own, third_in, second_middle, third_out)
+
+
+def on_device(*arguments):
+    if lax.axis_size("mp") == 4 and lax.axis_size("dp") == 8:
+        return cube_on_device(*arguments)
+    return general_on_device(*arguments)
+
+
 def solution(mesh):
     placed = (
         P(("dp", "mp"), None),

time: 485 us -> 360 us (0.74)
  the two profiles are of different devices: /device:TPU:8 before, /device:TPU:6 now
where the time goes in v1:
time: 360 us; the launch traced here: 356 us
  waiting for transfers between devices  202 us (56%)
  matrix products  51.7 us (14%)
  Pallas kernels  50.2 us (14%)
  starting transfers between devices  34.2 us (10%)
  other arithmetic  13.8 us (4%)
  local copies, waits for them, and re-layouts  3.79 us (1%)
    ppermute x11, waiting for transfers between devices, along(): return lax.ppermute(values, 'mp', list(pairs))  156 us
    pallas_call x4, Pallas kernels, shard_attention(): pl.pallas_call(functools.partial(attention_kernel, step, blocks), out_sha...  50.2 us
    ppermute x14, waiting for transfers between devices, swap(): return lax.ppermute(values, 'dp', [(i, i ^ bits) for i in range(8)])  46.1 us
    ppermute x11, starting transfers between devices, along(): return lax.ppermute(values, 'mp', list(pairs))  28.4 us
    dot_general x4, matrix products, part(): jnp.dot(attended, output_weight, preferred_element_type=jnp.float32)  26.6 us
    dot_general x5, matrix products, project(): jnp.dot(rows, query_weight, preferred_element_type=jnp.float32)  25 us
  transfers between devices with their start and end apart: 25, of which 13 were waited for; matrix products, arithmetic and copies ran while one was open for 13% of the time, Pallas kernels for 9%

profile of v1, /device:TPU:6, one launch (start us, length us, event | category | flops | bytes accessed | tf_op | source)
XLA Modules:
  0.0 355.7 jit_solution(4007767460814808204)
XLA Ops:
  0.0 2.1 convert_reduce_fusion
  2.1 0.1 copy-done.4
  2.2 0.7 fusion.7
  2.9 0.0 copy-start
  2.9 0.9 fusion.9
  3.9 1.3 collective-permute-start.1
  5.2 5.9 %collective-permute-start = (bf16[256,4096]{1,0:T(8,128)(2,1)S(1)}, bf16[256,4096]{1,0:T(8,128)(2,1)}, u32[]{:S(2)}, u32[]{:S(2)}) collective-permute-start(bf16[256,4096]{1,0:T(8,128)(2,1)S(1)} %fusion.9), channel_id=1, source_target_pairs={{0,1},{1,2},{2,3},{4,5},{5,6},{6,7},{8,9},{9,10},{10,11},{12,13},{... | collective-permute-start | bytes 6291464 | tf_op jit(solution)/shard_map/ppermute | solution.py:269
  11.1 0.5 collective-permute-start.2
  11.7 0.1 collective-permute-start.3
  11.7 41.5 %collective-permute-done.1 = bf16[256,4096]{1,0:T(8,128)(2,1)} collective-permute-done((bf16[256,4096]{1,0:T(8,128)(2,1)S(1)}, bf16[256,4096]{1,0:T(8,128)(2,1)}, u32[]{:S(2)}, u32[]{:S(2)}) %collective-permute-start.1) | collective-permute-done | bytes 2097184 | tf_op jit(solution)/shard_map/ppermute | solution.py:269
  53.3 1.1 collective-permute-done
  54.3 3.7 %collective-permute-done.2.refs_7_ = bf16[8,128,1024]{2,1,0:T(8,128)(2,1)} collective-permute-done((bf16[8,128,1024]{2,1,0:T(8,128)(2,1)S(1)}, bf16[8,128,1024]{2,1,0:T(8,128)(2,1)}, u32[]{:S(2)}, u32[]{:S(2)}) %collective-permute-start.2) | collective-permute-done | bytes 2097184 | tf_op jit(solution)/shard_map/ppermute | solution.py:265
  58.0 0.5 collective-permute-done.3.refs_17_
  58.5 1.5 collective-permute-start.6
  60.0 0.5 collective-permute-start.7
  60.5 2.0 collective-permute-start.4
  62.5 1.3 collective-permute-start.5
  63.8 0.1 collective-permute-start.9
  63.9 40.5 %collective-permute-done.6.refs_15_ = bf16[8,128,1024]{2,1,0:T(8,128)(2,1)} collective-permute-done((bf16[8,128,1024]{2,1,0:T(8,128)(2,1)}, bf16[8,128,1024]{2,1,0:T(8,128)(2,1)}, u32[]{:S(2)}, u32[]{:S(2)}) %collective-permute-start.6) | collective-permute-done | bytes 2097184 | tf_op jit(solution)/shard_map/ppermute | solution.py:265
  104.4 1.0 collective-permute-done.7.refs_9_
  105.4 6.7 %collective-permute-done.5 = bf16[256,4096]{1,0:T(8,128)(2,1)} collective-permute-done((bf16[256,4096]{1,0:T(8,128)(2,1)}, bf16[256,4096]{1,0:T(8,128)(2,1)}, u32[]{:S(2)}, u32[]{:S(2)}) %collective-permute-start.5) | collective-permute-done | bytes 2097184 | tf_op jit(solution)/shard_map/ppermute | solution.py:269
  112.1 3.2 broadcast_select_fusion
  115.3 1.5 collective-permute-start.8
  116.8 1.6 collective-permute-start.12
  118.4 0.5 collective-permute-start.17
  118.9 0.1 copy.13
  119.0 0.1 xor.10.relative_ref
  119.1 0.1 copy.14
  119.2 0.1 reshape.19.slots_ref
  119.3 0.7 dynamic-slice_bitcast_fusion.steps_ref
  120.0 6.5 %fusion.10.refs_0_ = bf16[256,1024]{1,0:T(8,128)(2,1)S(1)} fusion(bf16[256,4096]{1,0:T(8,128)(2,1)} %copy-done.5, bf16[4096,1024]{1,0:T(8,128)(2,1)} %param.12), kind=kOutput, calls=%fused_computation.25 | convolution fusion | flops 2148007936 | bytes 11010048 | tf_op jit(solution)/shard_map/dot_general | solution.py:287
  126.5 0.0 slice-start.1
  126.5 6.5 %fusion.11.refs_1_ = bf16[256,1024]{1,0:T(8,128)(2,1)S(1)} fusion(bf16[256,4096]{1,0:T(8,128)(2,1)} %collective-permute-done, bf16[4096,1024]{1,0:T(8,128)(2,1)} %param.12), kind=kOutput, calls=%fused_computation.26 | convolution fusion | flops 2148007936 | bytes 11010048 | tf_op jit(solution)/shard_map/dot_general | solution.py:287
  133.0 0.1 collective-permute-start.16
  133.1 0.5 collective-permute-start.11
  133.6 28.1 %collective-permute-done.8 = bf16[256,4096]{1,0:T(8,128)(2,1)} collective-permute-done((bf16[256,4096]{1,0:T(8,128)(2,1)}, bf16[256,4096]{1,0:T(8,128)(2,1)}, u32[]{:S(2)}, u32[]{:S(2)}) %collective-permute-start.8) | collective-permute-done | bytes 2097184 | tf_op jit(solution)/shard_map/ppermute | solution.py:269
  161.6 0.5 collective-permute-start.13
  162.2 0.4 collective-permute-done.17.refs_19_
  162.6 4.0 %fusion.12.refs_2_ = bf16[256,1024]{1,0:T(8,128)(2,1)S(1)} fusion(bf16[256,4096]{1,0:T(8,128)(2,1)} %collective-permute-done.1, bf16[4096,1024]{1,0:T(8,128)(2,1)S(1)} %bitcast.21), kind=kOutput, calls=%fused_computation.27 | convolution fusion | flops 2148007936 | bytes 11010048 | tf_op jit(solution)/shard_map/dot_general | solution.py:287
  166.6 4.0 %fusion.13.refs_3_ = bf16[256,1024]{1,0:T(8,128)(2,1)S(1)} fusion(bf16[256,4096]{1,0:T(8,128)(2,1)} %broadcast_select_fusion, bf16[4096,1024]{1,0:T(8,128)(2,1)S(1)} %bitcast.21), kind=kOutput, calls=%fused_computation.28 | convolution fusion | flops 2148007936 | bytes 11010048 | tf_op jit(solution)/shard_map/dot_general | solution.py:287
  170.6 4.0 %fusion.14.refs_4_ = bf16[256,1024]{1,0:T(8,128)(2,1)S(1)} fusion(bf16[256,4096]{1,0:T(8,128)(2,1)} %collective-permute-done.8, bf16[4096,1024]{1,0:T(8,128)(2,1)S(1)} %bitcast.21), kind=kOutput, calls=%fused_computation.29 | convolution fusion | flops 2148007936 | bytes 11010048 | tf_op jit(solution)/shard_map/dot_general | solution.py:287
  174.7 1.3 copy-done.2
  176.0 1.3 copy-done.3
  177.3 17.2 %shard_map.103 = bf16[256,1024]{1,0:T(8,128)(2,1)S(1)} custom-call(s32[8]{0:T(128)S(1)} %dynamic-slice_bitcast_fusion.steps_ref, s32[32]{0:T(128)S(1)} %xor.10.relative_ref, s32[32]{0:T(128)S(1)} %reshape.19.slots_ref, s32[16]{0:T(128)S(1)} %copy-done.1, bf16[256,1024]{1,0:T(8,128)(2,1)S(1)} %fusion.10.refs_0_, bf16[256,1024]{1,0:T(8,128)(2,1)S(1)} %fusion.11.refs_1_, ...), custom_call_target="tpu_custom_call" | custom-call | flops 268435456 | bytes 6291456 | tf_op jit(solution)/shard_map/pallas_call | solution.py:238
  194.5 5.7 %convolution_convert_fusion = bf16[256,4096]{1,0:T(8,128)(2,1)S(1)} fusion(bf16[256,1024]{1,0:T(8,128)(2,1)S(1)} %shard_map.103, bf16[1024,4096]{1,0:T(8,128)(2,1)} %param.13), kind=kOutput, calls=%fused_computation.2 | convolution fusion | flops 2148532224 | bytes 11010048 | tf_op jit(solution)/shard_map/dot_general | solution.py:324
  200.2 5.5 %collective-permute-start.22 = (bf16[256,4096]{1,0:T(8,128)(2,1)S(1)}, bf16[256,4096]{1,0:T(8,128)(2,1)S(1)}, u32[]{:S(2)}, u32[]{:S(2)}) collective-permute-start(bf16[256,4096]{1,0:T(8,128)(2,1)S(1)} %convolution_convert_fusion), channel_id=1, source_target_pairs={{0,1},{3,2},{4,5},{7,6},{8,9},{11,10},{12,13},{15,14},{16,17},{19,... | collective-permute-start | bytes 6291464 | tf_op jit(solution)/shard_map/ppermute | solution.py:269
  205.7 8.2 %shard_map.102 = bf16[256,1024]{1,0:T(8,128)(2,1)S(1)} custom-call(s32[8]{0:T(128)S(1)} %dynamic-slice_bitcast_fusion.steps_ref, s32[32]{0:T(128)S(1)} %xor.10.relative_ref, s32[32]{0:T(128)S(1)} %reshape.19.slots_ref, s32[16]{0:T(128)S(1)} %copy-done.1, bf16[256,1024]{1,0:T(8,128)(2,1)S(1)} %fusion.10.refs_0_, bf16[256,1024]{1,0:T(8,128)(2,1)S(1)} %fusion.11.refs_1_, ...), custom_call_target="tpu_custom_call" | custom-call | flops 268435456 | bytes 6291456 | tf_op jit(solution)/shard_map/pallas_call | solution.py:238
  213.9 5.7 %convolution_convert_fusion.1 = bf16[256,4096]{1,0:T(8,128)(2,1)S(1)} fusion(bf16[256,1024]{1,0:T(8,128)(2,1)S(1)} %shard_map.102, bf16[1024,4096]{1,0:T(8,128)(2,1)} %param.13), kind=kOutput, calls=%fused_computation.3 | convolution fusion | flops 2148532224 | bytes 11010048 | tf_op jit(solution)/shard_map/dot_general | solution.py:324
  219.6 2.7 collective-permute-start.20
  222.3 29.3 %collective-permute-done.22 = bf16[256,4096]{1,0:T(8,128)(2,1)S(1)} collective-permute-done((bf16[256,4096]{1,0:T(8,128)(2,1)S(1)}, bf16[256,4096]{1,0:T(8,128)(2,1)S(1)}, u32[]{:S(2)}, u32[]{:S(2)}) %collective-permute-start.22) | collective-permute-done | bytes 2097184 | tf_op jit(solution)/shard_map/ppermute | solution.py:269
  251.7 2.2 add_convert_fusion.1
  253.8 2.0 collective-permute-start.23
  255.8 13.8 %shard_map.101 = bf16[256,1024]{1,0:T(8,128)(2,1)S(1)} custom-call(s32[8]{0:T(128)S(1)} %dynamic-slice_bitcast_fusion.steps_ref, s32[32]{0:T(128)S(1)} %xor.10.relative_ref, s32[32]{0:T(128)S(1)} %reshape.19.slots_ref, s32[16]{0:T(128)S(1)} %copy-done.1, bf16[256,1024]{1,0:T(8,128)(2,1)S(1)} %fusion.10.refs_0_, bf16[256,1024]{1,0:T(8,128)(2,1)S(1)} %fusion.11.refs_1_, ...), custom_call_target="tpu_custom_call" | custom-call | flops 268435456 | bytes 6291456 | tf_op jit(solution)/shard_map/pallas_call | solution.py:238
  269.7 5.7 %convolution_convert_fusion.2 = bf16[256,4096]{1,0:T(8,128)(2,1)S(1)} fusion(bf16[256,1024]{1,0:T(8,128)(2,1)S(1)} %shard_map.101, bf16[1024,4096]{1,0:T(8,128)(2,1)} %param.13), kind=kOutput, calls=%fused_computation.4 | convolution fusion | flops 2148532224 | bytes 11010048 | tf_op jit(solution)/shard_map/dot_general | solution.py:324
  275.4 2.8 collective-permute-start.19
  278.3 18.3 %collective-permute-done.20 = bf16[256,4096]{1,0:T(8,128)(2,1)} collective-permute-done((bf16[256,4096]{1,0:T(8,128)(2,1)S(1)}, bf16[256,4096]{1,0:T(8,128)(2,1)}, u32[]{:S(2)}, u32[]{:S(2)}) %collective-permute-start.20) | collective-permute-done | bytes 2097184 | tf_op jit(solution)/shard_map/ppermute | solution.py:269
  296.6 2.4 add_convert_fusion.2
  299.0 2.1 collective-permute-start.21
  301.0 2.4 add_convert_fusion
  303.4 1.3 collective-permute-start.24
  304.7 11.0 %shard_map.100 = bf16[256,1024]{1,0:T(8,128)(2,1)S(1)} custom-call(s32[8]{0:T(128)S(1)} %dynamic-slice_bitcast_fusion.steps_ref, s32[32]{0:T(128)S(1)} %xor.10.relative_ref, s32[32]{0:T(128)S(1)} %reshape.19.slots_ref, s32[16]{0:T(128)S(1)} %copy-done.1, bf16[256,1024]{1,0:T(8,128)(2,1)S(1)} %fusion.10.refs_0_, bf16[256,1024]{1,0:T(8,128)(2,1)S(1)} %fusion.11.refs_1_, ...), custom_call_target="tpu_custom_call" | custom-call | flops 268435456 | bytes 6291456 | tf_op jit(solution)/shard_map/pallas_call | solution.py:238
  315.7 22.2 %collective-permute-done.19 = bf16[256,4096]{1,0:T(8,128)(2,1)} collective-permute-done((bf16[256,4096]{1,0:T(8,128)(2,1)S(1)}, bf16[256,4096]{1,0:T(8,128)(2,1)}, u32[]{:S(2)}, u32[]{:S(2)}) %collective-permute-start.19) | collective-permute-done | bytes 2097184 | tf_op jit(solution)/shard_map/ppermute | solution.py:269
  337.9 8.3 %collective-permute-done.24 = bf16[256,4096]{1,0:T(8,128)(2,1)} collective-permute-done((bf16[256,4096]{1,0:T(8,128)(2,1)S(1)}, bf16[256,4096]{1,0:T(8,128)(2,1)}, u32[]{:S(2)}, u32[]{:S(2)}) %collective-permute-start.24) | collective-permute-done | bytes 2097184 | tf_op jit(solution)/shard_map/ppermute | solution.py:269
  346.2 9.5 %fusion.4 = bf16[256,4096]{1,0:T(8,128)(2,1)} fusion(bf16[256,1024]{1,0:T(8,128)(2,1)S(1)} %shard_map.100, bf16[1024,4096]{1,0:T(8,128)(2,1)} %param.13, bf16[256,4096]{1,0:T(8,128)(2,1)} %collective-permute-done.24, bf16[256,4096]{1,0:T(8,128)(2,1)} %collective-permute-done.21, bf16[256,4096]{1,0:T(8,128)(2,1)} %collective-permute-done.19), kind=kOutput, calls=%fused_computation.10 | convolution fusion | flops 2156920832 | bytes 17301504 | tf_op jit(solution)/shard_map/dot_general | solution.py:324
  (37 shorter events, 0.1 us)
Async XLA Ops:
  0.0 2.2 copy-start.4
  0.0 2.9 copy-start.6
  2.9 8.2 %copy-start = (bf16[8,128,1024]{2,1,0:T(8,128)(2,1)S(1)}, bf16[8,128,1024]{2,1,0:T(8,128)(2,1)}, u32[]{:S(2)}) copy-start(bf16[8,128,1024]{2,1,0:T(8,128)(2,1)} %refs_5_.7) | copy-start | bytes 6291460
  3.9 58.6 %copy-start.5 = (bf16[256,4096]{1,0:T(8,128)(2,1)}, bf16[256,4096]{1,0:T(8,128)(2,1)S(1)}, u32[]{:S(2)}) copy-start(bf16[256,4096]{1,0:T(8,128)(2,1)S(1)} %fusion.9) | copy-start | bytes 6291460
  3.9 49.4 %collective-permute-start.1 = (bf16[256,4096]{1,0:T(8,128)(2,1)S(1)}, bf16[256,4096]{1,0:T(8,128)(2,1)}, u32[]{:S(2)}, u32[]{:S(2)}) collective-permute-start(bf16[256,4096]{1,0:T(8,128)(2,1)S(1)} %fusion.9), channel_id=1, source_target_pairs={{1,0},{2,1},{3,2},{5,4},{6,5},{7,6},{9,8},{10,9},{11,10},{13,12},{... | collective-permute-start | bytes 6291464 | tf_op jit(solution)/shard_map/ppermute | solution.py:269
  5.2 49.1 %collective-permute-start = (bf16[256,4096]{1,0:T(8,128)(2,1)S(1)}, bf16[256,4096]{1,0:T(8,128)(2,1)}, u32[]{:S(2)}, u32[]{:S(2)}) collective-permute-start(bf16[256,4096]{1,0:T(8,128)(2,1)S(1)} %fusion.9), channel_id=1, source_target_pairs={{0,1},{1,2},{2,3},{4,5},{5,6},{6,7},{8,9},{9,10},{10,11},{12,13},{... | collective-permute-start | bytes 6291464 | tf_op jit(solution)/shard_map/ppermute | solution.py:269
  11.1 46.9 %collective-permute-start.2 = (bf16[8,128,1024]{2,1,0:T(8,128)(2,1)S(1)}, bf16[8,128,1024]{2,1,0:T(8,128)(2,1)}, u32[]{:S(2)}, u32[]{:S(2)}) collective-permute-start(bf16[8,128,1024]{2,1,0:T(8,128)(2,1)S(1)} %copy-done), channel_id=1, source_target_pairs={{0,8},{4,12},{8,0},{12,4},{16,24},{20,28},{24,16},{28,20},{1,9},{5... | collective-permute-start | bytes 6291464 | tf_op jit(solution)/shard_map/ppermute | solution.py:265
  11.7 46.8 %collective-permute-start.3 = (bf16[8,128,1024]{2,1,0:T(8,128)(2,1)}, bf16[8,128,1024]{2,1,0:T(8,128)(2,1)}, u32[]{:S(2)}, u32[]{:S(2)}) collective-permute-start(bf16[8,128,1024]{2,1,0:T(8,128)(2,1)} %refs_13_.7), channel_id=1, source_target_pairs={{0,16},{4,20},{8,24},{12,28},{16,0},{20,4},{24,8},{28,12},{1,17},{... | collective-permute-start | bytes 6291464 | tf_op jit(solution)/shard_map/ppermute | solution.py:265
  58.5 45.9 %collective-permute-start.6 = (bf16[8,128,1024]{2,1,0:T(8,128)(2,1)}, bf16[8,128,1024]{2,1,0:T(8,128)(2,1)}, u32[]{:S(2)}, u32[]{:S(2)}) collective-permute-start(bf16[8,128,1024]{2,1,0:T(8,128)(2,1)} %refs_13_.7), channel_id=1, source_target_pairs={{0,8},{4,12},{8,0},{12,4},{16,24},{20,28},{24,16},{28,20},{1,9},{5... | collective-permute-start | bytes 6291464 | tf_op jit(solution)/shard_map/ppermute | solution.py:265
  60.0 45.4 %collective-permute-start.7 = (bf16[8,128,1024]{2,1,0:T(8,128)(2,1)S(1)}, bf16[8,128,1024]{2,1,0:T(8,128)(2,1)}, u32[]{:S(2)}, u32[]{:S(2)}) collective-permute-start(bf16[8,128,1024]{2,1,0:T(8,128)(2,1)S(1)} %copy-done), channel_id=1, source_target_pairs={{0,16},{4,20},{8,24},{12,28},{16,0},{20,4},{24,8},{28,12},{1,17},{... | collective-permute-start | bytes 6291464 | tf_op jit(solution)/shard_map/ppermute | solution.py:265
  60.5 44.9 %collective-permute-start.4 = (bf16[256,4096]{1,0:T(8,128)(2,1)}, bf16[256,4096]{1,0:T(8,128)(2,1)}, u32[]{:S(2)}, u32[]{:S(2)}) collective-permute-start(bf16[256,4096]{1,0:T(8,128)(2,1)} %collective-permute-done), channel_id=1, source_target_pairs={{1,2},{2,3},{5,6},{6,7},{9,10},{10,11},{13,14},{14,15},{17,18},{18... | collective-permute-start | bytes 6291464 | tf_op jit(solution)/shard_map/ppermute | solution.py:269
  62.5 49.6 %collective-permute-start.5 = (bf16[256,4096]{1,0:T(8,128)(2,1)}, bf16[256,4096]{1,0:T(8,128)(2,1)}, u32[]{:S(2)}, u32[]{:S(2)}) collective-permute-start(bf16[256,4096]{1,0:T(8,128)(2,1)} %collective-permute-done.1), channel_id=1, source_target_pairs={{1,0},{2,1},{5,4},{6,5},{9,8},{10,9},{13,12},{14,13},{17,16},{18,1... | collective-permute-start | bytes 6291464 | tf_op jit(solution)/shard_map/ppermute | solution.py:269
  63.8 54.6 %collective-permute-start.9 = (bf16[8,128,1024]{2,1,0:T(8,128)(2,1)S(1)}, bf16[8,128,1024]{2,1,0:T(8,128)(2,1)}, u32[]{:S(2)}, u32[]{:S(2)}) collective-permute-start(bf16[8,128,1024]{2,1,0:T(8,128)(2,1)S(1)} %copy-done), channel_id=1, source_target_pairs={{0,4},{4,0},{8,12},{12,8},{16,20},{20,16},{24,28},{28,24},{1,5},{5... | collective-permute-start | bytes 6291464 | tf_op jit(solution)/shard_map/ppermute | solution.py:265
  63.9 55.1 %copy-start.8 = (s32[16,2]{0,1:T(2,128)S(1)}, s32[16,2]{0,1:T(2,128)}, u32[]{:S(2)}) copy-start(s32[16,2]{0,1:T(2,128)} %param.16) | copy-start | bytes 388
  63.9 55.2 %copy-start.7 = (s32[16,2]{0,1:T(2,128)S(1)}, s32[16,2]{0,1:T(2,128)}, u32[]{:S(2)}) copy-start(s32[16,2]{0,1:T(2,128)} %param.17) | copy-start | bytes 388
  104.4 28.6 %collective-permute-start.14 = (bf16[8,128,1024]{2,1,0:T(8,128)(2,1)}, bf16[8,128,1024]{2,1,0:T(8,128)(2,1)}, u32[]{:S(2)}, u32[]{:S(2)}) collective-permute-start(bf16[8,128,1024]{2,1,0:T(8,128)(2,1)} %refs_13_.7), channel_id=1, source_target_pairs={{0,4},{4,0},{8,12},{12,8},{16,20},{20,16},{24,28},{28,24},{1,5},{5... | collective-permute-start | bytes 6291464 | tf_op jit(solution)/shard_map/ppermute | solution.py:265
  105.4 27.7 %collective-permute-start.10 = (bf16[8,128,1024]{2,1,0:T(8,128)(2,1)}, bf16[8,128,1024]{2,1,0:T(8,128)(2,1)}, u32[]{:S(2)}, u32[]{:S(2)}) collective-permute-start(bf16[8,128,1024]{2,1,0:T(8,128)(2,1)} %collective-permute-done.2.refs_7_), channel_id=1, source_target_pairs={{0,4},{4,0},{8,12},{12,8},{16,20},{20,16},{24,28},{28,24},{1,5},{5... | collective-permute-start | bytes 6291464 | tf_op jit(solution)/shard_map/ppermute | solution.py:265
  115.3 46.3 %collective-permute-start.8 = (bf16[256,4096]{1,0:T(8,128)(2,1)}, bf16[256,4096]{1,0:T(8,128)(2,1)}, u32[]{:S(2)}, u32[]{:S(2)}) collective-permute-start(bf16[256,4096]{1,0:T(8,128)(2,1)} %broadcast_select_fusion), channel_id=1, source_target_pairs={{1,0},{2,3},{5,4},{6,7},{9,8},{10,11},{13,12},{14,15},{17,16},{18,... | collective-permute-start | bytes 6291464 | tf_op jit(solution)/shard_map/ppermute | solution.py:269
  116.8 44.9 %collective-permute-start.12 = (bf16[8,128,1024]{2,1,0:T(8,128)(2,1)}, bf16[8,128,1024]{2,1,0:T(8,128)(2,1)}, u32[]{:S(2)}, u32[]{:S(2)}) collective-permute-start(bf16[8,128,1024]{2,1,0:T(8,128)(2,1)} %collective-permute-done.2.refs_7_), channel_id=1, source_target_pairs={{0,16},{4,20},{8,24},{12,28},{16,0},{20,4},{24,8},{28,12},{1,17},{... | collective-permute-start | bytes 6291464 | tf_op jit(solution)/shard_map/ppermute | solution.py:265
  118.4 44.2 %collective-permute-start.17 = (bf16[8,128,1024]{2,1,0:T(8,128)(2,1)}, bf16[8,128,1024]{2,1,0:T(8,128)(2,1)}, u32[]{:S(2)}, u32[]{:S(2)}) collective-permute-start(bf16[8,128,1024]{2,1,0:T(8,128)(2,1)} %collective-permute-done.3.refs_17_), channel_id=1, source_target_pairs={{0,8},{4,12},{8,0},{12,4},{16,24},{20,28},{24,16},{28,20},{1,9},{5... | collective-permute-start | bytes 6291464 | tf_op jit(solution)/shard_map/ppermute | solution.py:265
  120.0 42.6 %slice-start = ((s8[8388608]{0:T(1024)(128)(4,1)}), s8[4194304]{0:T(1024)(128)(4,1)S(1)}, s32[]{:S(2)}) async-start(s8[8388608]{0:T(1024)(128)(4,1)} %bitcast.20), calls=%async_computation | async-start | bytes 8388608
  126.5 36.1 %slice-start.1 = ((s8[8388608]{0:T(1024)(128)(4,1)}), s8[4194304]{0:T(1024)(128)(4,1)S(1)}, s32[]{:S(2)}) async-start(s8[8388608]{0:T(1024)(128)(4,1)} %bitcast.20), calls=%async_computation.1 | async-start | bytes 8388608
  133.0 41.6 %collective-permute-start.16 = (bf16[8,128,1024]{2,1,0:T(8,128)(2,1)}, bf16[8,128,1024]{2,1,0:T(8,128)(2,1)S(1)}, u32[]{:S(2)}, u32[]{:S(2)}) collective-permute-start(bf16[8,128,1024]{2,1,0:T(8,128)(2,1)} %collective-permute-done.3.refs_17_), channel_id=1, source_target_pairs={{0,4},{4,0},{8,12},{12,8},{16,20},{20,16},{24,28},{28,24},{1,5},{5... | collective-permute-start | bytes 6291464 | tf_op jit(solution)/shard_map/ppermute | solution.py:265
  133.1 41.6 %collective-permute-start.11 = (bf16[8,128,1024]{2,1,0:T(8,128)(2,1)}, bf16[8,128,1024]{2,1,0:T(8,128)(2,1)S(1)}, u32[]{:S(2)}, u32[]{:S(2)}) collective-permute-start(bf16[8,128,1024]{2,1,0:T(8,128)(2,1)} %collective-permute-done.7.refs_9_), channel_id=1, source_target_pairs={{0,4},{4,0},{8,12},{12,8},{16,20},{20,16},{24,28},{28,24},{1,5},{5... | collective-permute-start | bytes 6291464 | tf_op jit(solution)/shard_map/ppermute | solution.py:265
  161.6 13.0 %collective-permute-start.15 = (bf16[8,128,1024]{2,1,0:T(8,128)(2,1)}, bf16[8,128,1024]{2,1,0:T(8,128)(2,1)S(1)}, u32[]{:S(2)}, u32[]{:S(2)}) collective-permute-start(bf16[8,128,1024]{2,1,0:T(8,128)(2,1)} %collective-permute-done.6.refs_15_), channel_id=1, source_target_pairs={{0,4},{4,0},{8,12},{12,8},{16,20},{20,16},{24,28},{28,24},{1,5},{5... | collective-permute-start | bytes 6291464 | tf_op jit(solution)/shard_map/ppermute | solution.py:265
  161.6 13.0 %collective-permute-start.13 = (bf16[8,128,1024]{2,1,0:T(8,128)(2,1)}, bf16[8,128,1024]{2,1,0:T(8,128)(2,1)S(1)}, u32[]{:S(2)}, u32[]{:S(2)}) collective-permute-start(bf16[8,128,1024]{2,1,0:T(8,128)(2,1)} %collective-permute-done.12.refs_11_), channel_id=1, source_target_pairs={{0,4},{4,0},{8,12},{12,8},{16,20},{20,16},{24,28},{28,24},{1,5},{5... | collective-permute-start | bytes 6291464 | tf_op jit(solution)/shard_map/ppermute | solution.py:265
  162.5 12.1 %collective-permute-start.18 = (bf16[8,128,1024]{2,1,0:T(8,128)(2,1)}, bf16[8,128,1024]{2,1,0:T(8,128)(2,1)S(1)}, u32[]{:S(2)}, u32[]{:S(2)}) collective-permute-start(bf16[8,128,1024]{2,1,0:T(8,128)(2,1)} %collective-permute-done.17.refs_19_), channel_id=1, source_target_pairs={{0,4},{4,0},{8,12},{12,8},{16,20},{20,16},{24,28},{28,24},{1,5},{5... | collective-permute-start | bytes 6291464 | tf_op jit(solution)/shard_map/ppermute | solution.py:265
  170.6 6.7 %copy-start.1 = (s32[16]{0:T(128)S(1)}, s32[16]{0:T(128)}, u32[]{:S(2)}) copy-start(s32[16]{0:T(128)} %counts_ref.7) | copy-start | bytes 196
  174.6 1.3 copy-start.2
  176.0 1.3 copy-start.3
  200.2 51.5 %collective-permute-start.22 = (bf16[256,4096]{1,0:T(8,128)(2,1)S(1)}, bf16[256,4096]{1,0:T(8,128)(2,1)S(1)}, u32[]{:S(2)}, u32[]{:S(2)}) collective-permute-start(bf16[256,4096]{1,0:T(8,128)(2,1)S(1)} %convolution_convert_fusion), channel_id=1, source_target_pairs={{0,1},{3,2},{4,5},{7,6},{8,9},{11,10},{12,13},{15,14},{16,17},{19,... | collective-permute-start | bytes 6291464 | tf_op jit(solution)/shard_map/ppermute | solution.py:269
  219.6 77.0 %collective-permute-start.20 = (bf16[256,4096]{1,0:T(8,128)(2,1)S(1)}, bf16[256,4096]{1,0:T(8,128)(2,1)}, u32[]{:S(2)}, u32[]{:S(2)}) collective-permute-start(bf16[256,4096]{1,0:T(8,128)(2,1)S(1)} %convolution_convert_fusion.1), channel_id=1, source_target_pairs={{0,1},{3,2},{4,5},{7,6},{8,9},{11,10},{12,13},{15,14},{16,17},{19,... | collective-permute-start | bytes 6291464 | tf_op jit(solution)/shard_map/ppermute | solution.py:269
  253.8 47.2 %collective-permute-start.23 = (bf16[256,4096]{1,0:T(8,128)(2,1)}, bf16[256,4096]{1,0:T(8,128)(2,1)}, u32[]{:S(2)}, u32[]{:S(2)}) collective-permute-start(bf16[256,4096]{1,0:T(8,128)(2,1)} %add_convert_fusion.1), channel_id=1, source_target_pairs={{1,2},{2,1},{5,6},{6,5},{9,10},{10,9},{13,14},{14,13},{17,18},{18,... | collective-permute-start | bytes 6291464 | tf_op jit(solution)/shard_map/ppermute | solution.py:269
  275.4 62.5 %collective-permute-start.19 = (bf16[256,4096]{1,0:T(8,128)(2,1)S(1)}, bf16[256,4096]{1,0:T(8,128)(2,1)}, u32[]{:S(2)}, u32[]{:S(2)}) collective-permute-start(bf16[256,4096]{1,0:T(8,128)(2,1)S(1)} %convolution_convert_fusion.2), channel_id=1, source_target_pairs={{0,1},{3,2},{4,5},{7,6},{8,9},{11,10},{12,13},{15,14},{16,17},{19,... | collective-permute-start | bytes 6291464 | tf_op jit(solution)/shard_map/ppermute | solution.py:269
  299.0 39.0 %collective-permute-start.21 = (bf16[256,4096]{1,0:T(8,128)(2,1)S(1)}, bf16[256,4096]{1,0:T(8,128)(2,1)}, u32[]{:S(2)}, u32[]{:S(2)}) collective-permute-start(bf16[256,4096]{1,0:T(8,128)(2,1)S(1)} %add_convert_fusion.2), channel_id=1, source_target_pairs={{1,2},{2,1},{5,6},{6,5},{9,10},{10,9},{13,14},{14,13},{17,18},{18,... | collective-permute-start | bytes 6291464 | tf_op jit(solution)/shard_map/ppermute | solution.py:269
  303.4 42.8 %collective-permute-start.24 = (bf16[256,4096]{1,0:T(8,128)(2,1)S(1)}, bf16[256,4096]{1,0:T(8,128)(2,1)}, u32[]{:S(2)}, u32[]{:S(2)}) collective-permute-start(bf16[256,4096]{1,0:T(8,128)(2,1)S(1)} %add_convert_fusion), channel_id=1, source_target_pairs={{1,0},{2,3},{5,4},{6,7},{9,8},{10,11},{13,12},{14,15},{17,16},{18,... | collective-permute-start | bytes 6291464 | tf_op jit(solution)/shard_map/ppermute | solution.py:269

commit v2 on v1

--- a/solution.py
+++ b/solution.py
@@ -117,29 +117,23 @@
     )
 
 
-SHARD_ORDER = ((3, 2, 1, 0), (3, 2, 0, 1), (0, 1, 3, 2), (0, 1, 2, 3))
-QUERY_ARRAY = {0: 0, -1: 1, 1: 2, 2: 3, -2: 3, 3: 4, -3: 4}
+SHARD_ORDER = ((3, 2, 1, 0), (3, 2, 1, 0), (0, 1, 2, 3), (0, 1, 2, 3))
+HEADS_TOGETHER = 8
 OUTWARD = ((1, 0), (2, 3))
 INWARD = ((0, 1), (3, 2))
 MIDDLE = ((1, 2), (2, 1))
 
 
-def attention_kernel(step, blocks, steps_ref, relative_ref, slots_ref, counts_ref, *refs):
-    query_refs = refs[:5]
-    key_refs = refs[5:13]
-    value_refs = refs[13:21]
-    out_ref = refs[21]
-    query_buf, key_buf, value_buf, total_buf, query_sem, cache_sem = refs[22:]
-    shard = steps_ref[2 * step]
-    query_array = steps_ref[2 * step + 1]
+def attention_kernel(step, blocks, order_ref, relative_ref, slots_ref, counts_ref, *refs):
+    query_buf = refs[0]
+    pair_refs = refs[1:7]
+    key_refs = [ref.at[0] for ref in pair_refs] + [refs[7], refs[9]]
+    value_refs = [ref.at[1] for ref in pair_refs] + [refs[8], refs[10]]
+    out_ref = refs[11]
+    key_buf, value_buf, total_buf, cache_sem = refs[12:]
+    shard = order_ref[step]
     rows, width = query_buf.shape
     head_count = width // HD
-
-    for index, query_ref in enumerate(query_refs):
-
-        @pl.when(query_array == index)
-        def _():
-            pltpu.make_async_copy(query_ref, query_buf, query_sem).start()
 
     def entry_of(turn):
         span = shard * blocks - 1 + turn
@@ -172,13 +166,13 @@
         return carry
 
     lax.fori_loop(0, blocks + 1, fetch, 0)
-    pltpu.make_async_copy(query_refs[0], query_buf, query_sem).wait()
 
     def attend(turn, carry):
         _, count = entry_of(turn)
-        start = pl.multiple_of(jnp.minimum(turn, blocks - 1) * M, M)
-        before_start = pl.multiple_of(jnp.maximum(turn - 1, 0) * M, M)
-        earlier = pl.ds(pl.multiple_of(before_start + M - 8, 8), 8)
+        start = pl.multiple_of(turn * M, M)
+        block = pl.ds(pl.multiple_of(jnp.minimum(turn, blocks - 1) * M, M), M)
+        before = pl.ds(pl.multiple_of(jnp.maximum(turn - 1, 0) * M + M - 16, 16), 16)
+        earlier = pl.ds(pl.multiple_of(jnp.maximum(turn - 1, 0) * M + M - 8, 8), 8)
 
         @pl.when(count > 0)
         def _():
@@ -186,53 +180,53 @@
                 for copy in copies(turn, neighbour, 0, 0):
                     copy.wait()
             real = lax.broadcasted_iota(jnp.int32, (M, 2 * NL), 1) < count * NL
-            row = lax.broadcasted_iota(jnp.int32, (M, HD), 0)
-            for head in range(head_count):
-                columns = pl.ds(head * HD, HD)
-                queries = query_buf[pl.ds(start, M), columns].astype(jnp.float32)
-                before = query_buf[pl.ds(before_start, M), columns].astype(jnp.float32)
-                queries = jnp.where(row == M - 1, before, queries).astype(jnp.bfloat16)
-                scores = lax.dot_general(
-                    queries,
-                    key_buf[turn, :, columns],
-                    (((1,), (1,)), ((), ())),
-                    preferred_element_type=jnp.float32,
-                )
-                scores = jnp.where(real, scores, -1e30)
-                weights = jnp.exp(scores - jnp.max(scores, axis=-1, keepdims=True))
-                totals = jnp.sum(weights, axis=-1, keepdims=True)
-                mixture = jnp.dot(
-                    weights.astype(jnp.bfloat16),
-                    value_buf[turn, :, columns],
-                    preferred_element_type=jnp.float32,
-                )
-                mixture = mixture / totals
-
-                @pl.when(turn < blocks)
-                def _():
+            row = lax.broadcasted_iota(jnp.int32, (16, HD), 0)
+            for first_head in range(0, head_count, HEADS_TOGETHER):
+                heads = [
+                    pl.ds(head * HD, HD) for head in range(first_head, first_head + HEADS_TOGETHER)
+                ]
+                weights = []
+                for columns in heads:
+                    queries = query_buf[block, columns]
+                    tail = jnp.where(
+                        row == 15,
+                        query_buf[before, columns].astype(jnp.float32),
+                        queries[M - 16 :].astype(jnp.float32),
+                    ).astype(jnp.bfloat16)
+                    scores = lax.dot_general(
+                        jnp.concatenate([queries[: M - 16], tail], axis=0),
+                        key_buf[turn, :, columns],
+                        (((1,), (1,)), ((), ())),
+                        preferred_element_type=jnp.float32,
+                    )
+                    weights.append(jnp.where(real, scores, -1e30))
+                weights = [jnp.exp(w - jnp.max(w, axis=-1, keepdims=True)) for w in weights]
+                shares = [1.0 / jnp.sum(w, axis=-1, keepdims=True) for w in weights]
+                for columns, weight, share in zip(heads, weights, shares):
+                    mixture = share * jnp.dot(
+                        weight.astype(jnp.bfloat16),
+                        value_buf[turn, :, columns],
+                        preferred_element_type=jnp.float32,
+                    )
                     total_buf[pl.ds(start, M), columns] = mixture
-
-                total_buf[earlier, columns] = jnp.where(
-                    row[:8] == 7, mixture[M - 8 :], total_buf[earlier, columns]
-                )
+                    total_buf[earlier, columns] = jnp.where(
+                        row[8:] == 15, mixture[M - 8 :], total_buf[earlier, columns]
+                    )
 
         @pl.when(count <= 0)
         def _():
-            @pl.when(turn < blocks)
-            def _():
-                total_buf[pl.ds(start, M), :] = jnp.zeros((M, width), jnp.float32)
-
+            total_buf[pl.ds(start, M), :] = jnp.zeros((M, width), jnp.float32)
             row = lax.broadcasted_iota(jnp.int32, (8, width), 0)
             total_buf[earlier, :] = jnp.where(row == 7, 0.0, total_buf[earlier, :])
 
         return carry
 
     lax.fori_loop(0, blocks + 1, attend, 0)
-    out_ref[...] = total_buf[...].astype(jnp.bfloat16)
-
-
-def shard_attention(step, steps, relative, slots, counts, queries, keys, values):
-    rows, width = queries[0].shape
+    out_ref[...] = total_buf[:rows].astype(jnp.bfloat16)
+
+
+def shard_attention(step, order, relative, slots, counts, queries, caches):
+    rows, width = queries.shape
     blocks = rows // M
     anywhere = pl.BlockSpec(memory_space=pl.ANY)
     return pl.pallas_call(
@@ -241,24 +235,22 @@
         grid_spec=pltpu.PrefetchScalarGridSpec(
             num_scalar_prefetch=4,
             grid=(1,),
-            in_specs=[anywhere] * 21,
+            in_specs=[pl.BlockSpec((rows, width), lambda i, *_: (0, 0))] + [anywhere] * 10,
             out_specs=pl.BlockSpec((rows, width), lambda i, *_: (0, 0)),
             scratch_shapes=[
-                pltpu.VMEM((rows, width), jnp.bfloat16),
                 pltpu.VMEM((blocks + 1, 2 * NL, width), jnp.bfloat16),
                 pltpu.VMEM((blocks + 1, 2 * NL, width), jnp.bfloat16),
-                pltpu.VMEM((rows, width), jnp.float32),
-                pltpu.SemaphoreType.DMA,
+                pltpu.VMEM((rows + M, width), jnp.float32),
                 pltpu.SemaphoreType.DMA((blocks + 1, 4)),
             ],
         ),
-        compiler_params=pltpu.CompilerParams(vmem_limit_bytes=24 << 20),
+        compiler_params=pltpu.CompilerParams(vmem_limit_bytes=16 << 20),
         cost_estimate=pl.CostEstimate(
             flops=4 * rows * 2 * NL * width,
             bytes_accessed=2 * (rows * width * 2 + (blocks + 1) * 2 * NL * width * 2),
             transcendentals=rows * 2 * NL * (width // HD),
         ),
-    )(steps, relative, slots, counts, *queries, *keys, *values)
+    )(order, relative, slots, counts, queries, *caches)
 
 
 def swap(values, bits):
@@ -289,57 +281,91 @@
         )
 
     together = lax.optimization_barrier
+    core = lax.axis_index("dp") % 2
+    half = output_weight.shape[0] // 2
+    inside = (place == 1) | (place == 2)
+    low = place < 2
     normed = layer_norm(tokens, norm_gain)
     below = along(normed, ((0, 1), (1, 2), (2, 3)))
     above = along(normed, ((1, 0), (2, 1), (3, 2)))
-    keys = [key_cache, swap(key_cache, 1), swap(key_cache, 2)] + [None] * 5
-    values = [value_cache, swap(value_cache, 1), None, None, swap(value_cache, 4)] + [None] * 3
-    below, above, keys[2], values[4], key_cache, value_cache = together(
-        (below, above, keys[2], values[4], key_cache, value_cache)
-    )
+    cache = jnp.stack([key_cache, value_cache])
+    cache_x, cache_y, cache_core = swap(cache, 2), swap(cache, 4), swap(cache, 1)
+    handed = lax.dynamic_slice_in_dim(output_weight, core * half, half, 0)
+    below, above, handed = together((below, above, handed))
     below_two = along(below, ((1, 2), (2, 3)))
     above_two = along(above, ((1, 0), (2, 1)))
-    values[2], keys[4] = swap(value_cache, 2), swap(key_cache, 4)
-    keys[3], values[5] = swap(keys[2], 1), swap(values[4], 1)
-    below_two, above_two, values[2], keys[4], keys_x, values_y = together(
-        (below_two, above_two, values[2], keys[4], keys[2], values[4])
-    )
-    two = jnp.where(place >= 2, below_two, above_two)
+    inner = along(handed, INWARD)
+    third_queries = project(jnp.where(inside, normed, jnp.where(low, above, below)))
+    fourth_queries = project(jnp.where(inside, jnp.where(low, below, above), normed))
+    below_two, above_two, cache_x, cache_y, third_queries, fourth_queries = together(
+        (below_two, above_two, cache_x, cache_y, third_queries, fourth_queries)
+    )
+    two = jnp.where(low, above_two, below_two)
     three = along(two, OUTWARD)
-    keys[6], values[6] = swap(keys_x, 4), swap(values_y, 2)
-    values[3], keys[5] = swap(values[2], 1), swap(keys[4], 1)
-    keys[7], values[7] = swap(keys[6], 1), swap(values[6], 1)
-    queries = [project(rows) for rows in (normed, below, above, two, three)]
-
-    table = [
-        [number for shard in order for number in (shard, QUERY_ARRAY[shard - z])]
-        for z, order in enumerate(SHARD_ORDER)
-    ]
-    steps = lax.dynamic_index_in_dim(jnp.array(table, jnp.int32), place, 0, keepdims=False)
+    keys_xy, values_xy = swap(cache_x[0], 4), swap(cache_y[1], 2)
+    cache_x_core, cache_y_core = swap(cache_x, 1), swap(cache_y, 1)
+    three, keys_xy, values_xy, inner = together((three, keys_xy, values_xy, inner))
+    keys_xy_core, values_xy_core = swap(keys_xy, 1), swap(values_xy, 1)
+    other_inner = swap(inner, 1)
+    first_queries = project(jnp.where(inside, two, three))
+    caches = [cache, cache_core, cache_x, cache_x_core, cache_y, cache_y_core]
+    caches += [keys_xy, values_xy, keys_xy_core, values_xy_core]
+
+    order = lax.dynamic_index_in_dim(jnp.array(SHARD_ORDER, jnp.int32), place, 0, keepdims=False)
     relative = owners.reshape(-1) ^ lax.axis_index("dp")
     slots = slot_ids.reshape(-1)
 
-    def part(step):
-        attended = shard_attention(step, steps, relative, slots, valid_counts, queries, keys, values)
-        return jnp.dot(attended, output_weight, preferred_element_type=jnp.float32).astype(jnp.bfloat16)
-
-    def plus(*terms):
-        total = terms[0].astype(jnp.float32)
-        for term in terms[1:]:
-            total = total + term.astype(jnp.float32)
-        return total.astype(jnp.bfloat16)
-
-    first = part(0)
+    def attend(step, queries):
+        return shard_attention(step, order, relative, slots, valid_counts, queries, caches)
+
+    def product(attended, weight):
+        return jnp.dot(attended, weight, preferred_element_type=jnp.float32)
+
+    def handed_product(attended, columns):
+        total = None
+        for piece, from_core in ((inner, core), (other_inner, 1 - core)):
+            heads = lax.dynamic_slice_in_dim(attended, from_core * half, half, 1)
+            term = product(heads, piece[:, columns])
+            total = term if total is None else total + term
+        return total
+
+    def rounded_sum(one, other):
+        return (one.astype(jnp.float32) + other.astype(jnp.float32)).astype(jnp.bfloat16)
+
+    width = output_weight.shape[1] // 2
+    left, right = slice(0, width), slice(width, 2 * width)
+    first = attend(0, first_queries)
     first_in = along(first, INWARD)
-    second = part(1)
+    first, two, above, below = together((first, two, above, below))
+    first_part = product(first, output_weight)
+    second = attend(
+        1, project(jnp.where(inside, jnp.where(low, above, below), two))
+    )
     second_in = along(second, INWARD)
-    first_middle = along(plus(first, first_in), MIDDLE)
-    third = part(2)
+    first_in, first_part, second = together((first_in, first_part, second))
+    first_across = []
+    for columns in (left, right):
+        piece = rounded_sum(first_part[:, columns], handed_product(first_in, columns))
+        piece, fourth_queries, second, first_in = together((piece, fourth_queries, second, first_in))
+        first_across.append(along(piece, MIDDLE))
+    fourth = product(attend(3, fourth_queries), output_weight).astype(jnp.bfloat16)
+    second_part = product(second, output_weight)
+    first_left, fourth, second_part, second_in = together((first_across[0], fourth, second_part, second_in))
+    outward_left = along(rounded_sum(fourth[:, left], first_left), OUTWARD)
+    second = rounded_sum(second_part, handed_product(second_in, slice(0, 2 * width)))
+    second, third_queries = together((second, third_queries))
+    second_across = along(second, MIDDLE)
+    outward_right = along(rounded_sum(fourth[:, right], first_across[1]), OUTWARD)
+    third = attend(2, third_queries)
     third_in = along(third, INWARD)
-    second_middle = along(plus(second, second_in), MIDDLE)
-    third_out = along(plus(third, first_middle), OUTWARD)
-    own = part(3)
-    return plus(own, third_in, second_middle, third_out)
+    third = rounded_sum(product(third, output_weight), handed_product(third_in, slice(0, 2 * width)))
+    third, fourth, second_across, outward_left, outward_right = together(
+        (third, fourth, second_across, outward_left, outward_right)
+    )
+    return rounded_sum(
+        jnp.where(inside, third, fourth),
+        jnp.where(inside, second_across, jnp.concatenate([outward_left, outward_right], axis=1)),
+    )
 
 
 def on_device(*arguments):

time: 360 us -> 312 us (0.87)
  the two profiles are of different devices: /device:TPU:6 before, /device:TPU:8 now
where the time goes in v2:
time: 312 us; the launch traced here: 309 us
  waiting for transfers between devices  165 us (53%)
  matrix products  60 us (19%)
  starting transfers between devices  41.1 us (13%)
  Pallas kernels  16 us (5%)
  other arithmetic  13.4 us (4%)
  local copies, waits for them, and re-layouts  12.4 us (4%)
    ppermute x14, waiting for transfers between devices, along(): return lax.ppermute(values, 'mp', list(pairs))  154 us
    dot_general x12, matrix products, product(): return jnp.dot(attended, weight, preferred_element_type=jnp.float32)  34.1 us
    ppermute x14, starting transfers between devices, along(): return lax.ppermute(values, 'mp', list(pairs))  34.1 us
    dot_general x4, matrix products, project(): jnp.dot(rows, query_weight, preferred_element_type=jnp.float32)  25.9 us
    pallas_call x4, Pallas kernels, shard_attention(): pl.pallas_call(functools.partial(attention_kernel, step, blocks), out_sha...  16 us
    ppermute x10, waiting for transfers between devices, swap(): return lax.ppermute(values, 'dp', [(i, i ^ bits) for i in range(8)])  11.4 us
    ppermute x10, starting transfers between devices, swap(): return lax.ppermute(values, 'dp', [(i, i ^ bits) for i in range(8)])  7.08 us
  transfers between devices with their start and end apart: 24, of which 15 were waited for; matrix products, arithmetic and copies ran while one was open for 25% of the time, Pallas kernels for 5%

profile of v2, /device:TPU:8, one launch (start us, length us, event | category | flops | bytes accessed | tf_op | source)
XLA Modules:
  0.0 308.9 jit_solution(1744213442174008365)
XLA Ops:
  0.0 2.1 convert_reduce_fusion
  2.2 0.7 fusion.3
  3.0 0.9 fusion.5
  3.9 2.2 collective-permute-start.1
  6.1 3.9 %collective-permute-start = (bf16[256,4096]{1,0:T(8,128)(2,1)S(1)}, bf16[256,4096]{1,0:T(8,128)(2,1)}, u32[]{:S(2)}, u32[]{:S(2)}) collective-permute-start(bf16[256,4096]{1,0:T(8,128)(2,1)S(1)} %fusion.5), channel_id=1, source_target_pairs={{0,1},{1,2},{2,3},{4,5},{5,6},{6,7},{8,9},{9,10},{10,11},{12,13},{... | collective-permute-start | bytes 6291464 | tf_op jit(solution)/shard_map/ppermute | solution.py:261
  10.1 2.4 pad_maximum_fusion.refs_1_
  12.4 1.5 collective-permute-start.5
  14.0 1.5 collective-permute-start.4
  15.5 4.7 %constant_dynamic-slice_fusion = bf16[512,4096]{1,0:T(8,128)(2,1)} fusion(bf16[1024,4096]{1,0:T(8,128)(2,1)} %param.13, s32[]{:T(128)S(6)} %select_n.74), kind=kLoop, calls=%fused_computation.75 | loop fusion | bytes 8388612 | tf_op jit(solution)/shard_map/dynamic_slice | solution.py:293
  20.1 33.4 %collective-permute-done.1 = bf16[256,4096]{1,0:T(8,128)(2,1)} collective-permute-done((bf16[256,4096]{1,0:T(8,128)(2,1)S(1)}, bf16[256,4096]{1,0:T(8,128)(2,1)}, u32[]{:S(2)}, u32[]{:S(2)}) %collective-permute-start.1) | collective-permute-done | bytes 2097184 | tf_op jit(solution)/shard_map/ppermute | solution.py:261
  53.5 1.9 collective-permute-done
  55.5 4.1 %collective-permute-start.2 = (bf16[256,4096]{1,0:T(8,128)(2,1)}, bf16[256,4096]{1,0:T(8,128)(2,1)S(1)}, u32[]{:S(2)}, u32[]{:S(2)}) collective-permute-start(bf16[256,4096]{1,0:T(8,128)(2,1)} %collective-permute-done), channel_id=1, source_target_pairs={{1,2},{2,3},{5,6},{6,7},{9,10},{10,11},{13,14},{14,15},{17,18},{18... | collective-permute-start | bytes 6291464 | tf_op jit(solution)/shard_map/ppermute | solution.py:261
  59.5 1.9 collective-permute-start.3
  61.5 1.4 collective-permute-start.9
  62.9 6.4 %fusion.48.refs_0_ = bf16[256,1024]{1,0:T(8,128)(2,1)S(1)} fusion(bf16[4096,1024]{1,0:T(8,128)(2,1)} %param.12, bf16[256,4096]{1,0:T(8,128)(2,1)} %copy-done.8, bf16[256,4096]{1,0:T(8,128)(2,1)} %collective-permute-done, bf16[256,4096]{1,0:T(8,128)(2,1)} %collective-permute-done.1, pred[]{:T(512)S(6)} %lt.27, pred[]{:T(512)S(6)} %or.3), kind=kOutput, calls=%fused_computation.55 | convolution fusion | flops 2150105088 | bytes 15204354 | tf_op jit(solution)/shard_map/dot_general | solution.py:279
  69.3 6.4 %fusion.51.refs_0_ = bf16[256,1024]{1,0:T(8,128)(2,1)S(1)} fusion(bf16[4096,1024]{1,0:T(8,128)(2,1)} %param.12, bf16[256,4096]{1,0:T(8,128)(2,1)S(1)} %copy-done.9, bf16[256,4096]{1,0:T(8,128)(2,1)} %collective-permute-done.1, bf16[256,4096]{1,0:T(8,128)(2,1)} %collective-permute-done, pred[]{:T(512)S(6)} %lt.27, pred[]{:T(512)S(6)} %or.3), kind=kOutput, calls=%fused_computation.56 | convolution fusion | flops 2150105088 | bytes 15204354 | tf_op jit(solution)/shard_map/dot_general | solution.py:279
  75.8 27.6 %collective-permute-done.2 = bf16[256,4096]{1,0:T(8,128)(2,1)S(1)} collective-permute-done((bf16[256,4096]{1,0:T(8,128)(2,1)}, bf16[256,4096]{1,0:T(8,128)(2,1)S(1)}, u32[]{:S(2)}, u32[]{:S(2)}) %collective-permute-start.2) | collective-permute-done | bytes 2097184 | tf_op jit(solution)/shard_map/ppermute | solution.py:261
  103.4 4.3 %collective-permute-done.3 = bf16[256,4096]{1,0:T(8,128)(2,1)} collective-permute-done((bf16[256,4096]{1,0:T(8,128)(2,1)}, bf16[256,4096]{1,0:T(8,128)(2,1)}, u32[]{:S(2)}, u32[]{:S(2)}) %collective-permute-start.3) | collective-permute-done | bytes 2097184 | tf_op jit(solution)/shard_map/ppermute | solution.py:261
  107.8 1.9 slice_bitcast_fusion
  109.6 1.6 collective-permute-start.8
  111.2 1.9 slice_bitcast_fusion.1
  113.1 1.6 collective-permute-start.7
  114.7 1.8 broadcast_select_fusion
  116.5 2.2 collective-permute-start.6
  118.8 35.9 %collective-permute-done.9 = bf16[512,4096]{1,0:T(8,128)(2,1)} collective-permute-done((bf16[512,4096]{1,0:T(8,128)(2,1)}, bf16[512,4096]{1,0:T(8,128)(2,1)}, u32[]{:S(2)}, u32[]{:S(2)}) %collective-permute-start.9) | collective-permute-done | bytes 4194336 | tf_op jit(solution)/shard_map/ppermute | solution.py:261
  155.2 2.9 collective-permute-done.7.refs_7_
  158.1 2.8 collective-permute-done.6
  161.3 0.8 copy-done.15
  162.2 2.0 copy-done
  164.5 0.7 fusion.80.order_ref
  165.2 6.5 %fusion.42.refs_0_ = bf16[256,1024]{1,0:T(8,128)(2,1)S(1)} fusion(bf16[4096,1024]{1,0:T(8,128)(2,1)} %param.12, bf16[256,4096]{1,0:T(8,128)(2,1)} %copy-done.4, bf16[256,4096]{1,0:T(8,128)(2,1)} %copy-done.15, pred[]{:T(512)S(6)} %or.3), kind=kOutput, calls=%fused_computation.53 | convolution fusion | flops 2149056512 | bytes 13107201 | tf_op jit(solution)/shard_map/dot_general | solution.py:279
  171.7 8.4 %collective-permute-done.13.refs_9_ = bf16[8,128,1024]{2,1,0:T(8,128)(2,1)} collective-permute-done((bf16[8,128,1024]{2,1,0:T(8,128)(2,1)}, bf16[8,128,1024]{2,1,0:T(8,128)(2,1)}, u32[]{:S(2)}, u32[]{:S(2)}) %collective-permute-start.13) | collective-permute-done | bytes 2097184 | tf_op jit(solution)/shard_map/ppermute | solution.py:257
  180.2 3.2 %shard_map.100 = bf16[256,1024]{1,0:T(8,128)(2,1)S(1)} custom-call(s32[4]{0:T(128)S(1)} %fusion.80.order_ref, s32[32]{0:T(128)S(1)} %xor.10.relative_ref, s32[32]{0:T(128)S(1)} %reshape.19.slots_ref, s32[16]{0:T(128)S(1)} %copy-done.2, bf16[256,1024]{1,0:T(8,128)(2,1)S(1)} %fusion.42.refs_0_, bf16[2,8,128,1024]{3,2,1,0:T(8,128)(2,1)} %pad_maximum_fusion.refs_1_, ...), custom_call_target="tpu_custom_call" | custom-call | flops 268435456 | bytes 6291456 | tf_op jit(solution)/shard_map/pallas_call | solution.py:232
  183.4 1.5 collective-permute-start.15
  184.9 6.6 %fusion.45.refs_0_ = bf16[256,1024]{1,0:T(8,128)(2,1)S(1)} fusion(bf16[4096,1024]{1,0:T(8,128)(2,1)} %param.12, bf16[256,4096]{1,0:T(8,128)(2,1)S(1)} %copy-done.5, bf16[256,4096]{1,0:T(8,128)(2,1)} %collective-permute-done.1, bf16[256,4096]{1,0:T(8,128)(2,1)} %collective-permute-done, pred[]{:T(512)S(6)} %lt.27, pred[]{:T(512)S(6)} %or.3), kind=kOutput, calls=%fused_computation.54 | convolution fusion | flops 2150105088 | bytes 15204354 | tf_op jit(solution)/shard_map/dot_general | solution.py:279
  191.5 4.1 %shard_map.101 = bf16[256,1024]{1,0:T(8,128)(2,1)S(1)} custom-call(s32[4]{0:T(128)S(1)} %fusion.80.order_ref, s32[32]{0:T(128)S(1)} %xor.10.relative_ref, s32[32]{0:T(128)S(1)} %reshape.19.slots_ref, s32[16]{0:T(128)S(1)} %copy-done.2, bf16[256,1024]{1,0:T(8,128)(2,1)S(1)} %fusion.45.refs_0_, bf16[2,8,128,1024]{3,2,1,0:T(8,128)(2,1)} %pad_maximum_fusion.refs_1_, ...), custom_call_target="tpu_custom_call" | custom-call | flops 268435456 | bytes 6291456 | tf_op jit(solution)/shard_map/pallas_call | solution.py:232
  195.7 1.3 collective-permute-start.18
  197.0 2.4 fusion.81
  199.8 2.3 fusion.8
  202.1 2.4 add_convert_fusion.5
  204.6 6.3 %collective-permute-start.17 = (bf16[256,2048]{1,0:T(8,128)(2,1)S(1)}, bf16[256,2048]{1,0:T(8,128)(2,1)S(1)}, u32[]{:S(2)}, u32[]{:S(2)}) collective-permute-start(bf16[256,2048]{1,0:T(8,128)(2,1)S(1)} %add_convert_fusion.5), channel_id=1, source_target_pairs={{1,2},{2,1},{5,6},{6,5},{9,10},{10,9},{13,14},{14,13},{17,18},{18,... | collective-permute-start | bytes 3145736 | tf_op jit(solution)/shard_map/ppermute | solution.py:261
  210.8 2.3 fusion.6
  213.1 3.4 %add_convert_fusion.4 = bf16[256,2048]{1,0:T(8,128)(2,1)} fusion(f32[256,4096]{1,0:T(8,128)S(1)} %fusion.81, f32[256,2048]{1,0:T(8,128)S(1)} %fusion.6, bf16[512,4096]{1,0:T(8,128)(2,1)} %collective-permute-done.9, bf16[256,1024]{1,0:T(8,128)(2,1)S(1)} %collective-permute-done.15, s32[]{:T(128)S(6)} %select_n.74), kind=kOutput, calls=%fused_computation.24 | convolution fusion | flops 538443776 | bytes 7602180 | tf_op jit(solution)/shard_map/dot_general | solution.py:322
  216.5 2.1 collective-permute-start.22
  218.7 3.7 %shard_map.102 = bf16[256,1024]{1,0:T(8,128)(2,1)S(1)} custom-call(s32[4]{0:T(128)S(1)} %fusion.80.order_ref, s32[32]{0:T(128)S(1)} %xor.10.relative_ref, s32[32]{0:T(128)S(1)} %reshape.19.slots_ref, s32[16]{0:T(128)S(1)} %copy-done.2, bf16[256,1024]{1,0:T(8,128)(2,1)S(1)} %fusion.48.refs_0_, bf16[2,8,128,1024]{3,2,1,0:T(8,128)(2,1)} %pad_maximum_fusion.refs_1_, ...), custom_call_target="tpu_custom_call" | custom-call | flops 268435456 | bytes 6291456 | tf_op jit(solution)/shard_map/pallas_call | solution.py:232
  222.4 2.4 convolution_convert_fusion
  224.8 2.4 fusion.82
  227.2 7.6 %collective-permute-done.17 = bf16[256,2048]{1,0:T(8,128)(2,1)S(1)} collective-permute-done((bf16[256,2048]{1,0:T(8,128)(2,1)S(1)}, bf16[256,2048]{1,0:T(8,128)(2,1)S(1)}, u32[]{:S(2)}, u32[]{:S(2)}) %collective-permute-start.17) | collective-permute-done | bytes 1048608 | tf_op jit(solution)/shard_map/ppermute | solution.py:261
  234.7 3.5 %fusion.57 = f32[256,4096]{1,0:T(8,128)S(1)} fusion(bf16[512,4096]{1,0:T(8,128)(2,1)} %collective-permute-done.16, bf16[256,1024]{1,0:T(8,128)(2,1)S(1)} %collective-permute-done.18, s32[]{:T(128)S(6)} %select_n.83), kind=kOutput, calls=%fused_computation.60 | convolution fusion | flops 1073741824 | bytes 8650756 | tf_op jit(solution)/shard_map/dot_general | solution.py:322
  238.2 3.6 %convolution_add_fusion.1 = f32[256,4096]{1,0:T(8,128)S(1)} fusion(f32[256,4096]{1,0:T(8,128)S(1)} %fusion.57, bf16[512,4096]{1,0:T(8,128)(2,1)} %collective-permute-done.9, bf16[256,1024]{1,0:T(8,128)(2,1)S(1)} %collective-permute-done.18, s32[]{:T(128)S(6)} %select_n.74), kind=kOutput, calls=%fused_computation.1 | convolution fusion | flops 1074790400 | bytes 12845060 | tf_op jit(solution)/shard_map/dot_general | solution.py:322
  242.4 5.0 %shard_map.103 = bf16[256,1024]{1,0:T(8,128)(2,1)S(1)} custom-call(s32[4]{0:T(128)S(1)} %fusion.80.order_ref, s32[32]{0:T(128)S(1)} %xor.10.relative_ref, s32[32]{0:T(128)S(1)} %reshape.19.slots_ref, s32[16]{0:T(128)S(1)} %copy-done.2, bf16[256,1024]{1,0:T(8,128)(2,1)S(1)} %fusion.51.refs_0_, bf16[2,8,128,1024]{3,2,1,0:T(8,128)(2,1)} %pad_maximum_fusion.refs_1_, ...), custom_call_target="tpu_custom_call" | custom-call | flops 268435456 | bytes 6291456 | tf_op jit(solution)/shard_map/pallas_call | solution.py:232
  247.4 1.3 collective-permute-start.19
  248.7 2.9 collective-permute-start.20
  251.6 5.7 %collective-permute-done.22 = bf16[256,2048]{1,0:T(8,128)(2,1)} collective-permute-done((bf16[256,2048]{1,0:T(8,128)(2,1)}, bf16[256,2048]{1,0:T(8,128)(2,1)}, u32[]{:S(2)}, u32[]{:S(2)}) %collective-permute-start.22) | collective-permute-done | bytes 1048608 | tf_op jit(solution)/shard_map/ppermute | solution.py:261
  257.3 2.1 add_convert_fusion.2
  259.5 1.4 collective-permute-start.23
  260.8 1.6 collective-permute-start.21
  262.4 1.0 collective-permute-done.19
  263.5 3.5 %fusion.54 = f32[256,4096]{1,0:T(8,128)S(1)} fusion(bf16[512,4096]{1,0:T(8,128)(2,1)} %collective-permute-done.16, bf16[256,1024]{1,0:T(8,128)(2,1)S(1)} %collective-permute-done.19, s32[]{:T(128)S(6)} %select_n.83), kind=kOutput, calls=%fused_computation.57 | convolution fusion | flops 1073741824 | bytes 8650756 | tf_op jit(solution)/shard_map/dot_general | solution.py:322
  266.9 3.6 %convolution_add_fusion = f32[256,4096]{1,0:T(8,128)S(1)} fusion(f32[256,4096]{1,0:T(8,128)S(1)} %fusion.54, bf16[512,4096]{1,0:T(8,128)(2,1)} %collective-permute-done.9, bf16[256,1024]{1,0:T(8,128)(2,1)S(1)} %collective-permute-done.19, s32[]{:T(128)S(6)} %select_n.74), kind=kOutput, calls=%fused_computation | convolution fusion | flops 1074790400 | bytes 12845060 | tf_op jit(solution)/shard_map/dot_general | solution.py:322
  270.5 2.5 fusion
  273.0 11.2 %collective-permute-done.23 = bf16[256,2048]{1,0:T(8,128)(2,1)S(1)} collective-permute-done((bf16[256,2048]{1,0:T(8,128)(2,1)S(1)}, bf16[256,2048]{1,0:T(8,128)(2,1)S(1)}, u32[]{:S(2)}, u32[]{:S(2)}) %collective-permute-start.23) | collective-permute-done | bytes 1048608 | tf_op jit(solution)/shard_map/ppermute | solution.py:261
  284.2 22.0 %collective-permute-done.21 = bf16[256,2048]{1,0:T(8,128)(2,1)S(1)} collective-permute-done((bf16[256,2048]{1,0:T(8,128)(2,1)S(1)}, bf16[256,2048]{1,0:T(8,128)(2,1)S(1)}, u32[]{:S(2)}, u32[]{:S(2)}) %collective-permute-start.21) | collective-permute-done | bytes 1048608 | tf_op jit(solution)/shard_map/ppermute | solution.py:261
  306.2 2.7 add_convert_fusion
  (60 shorter events, 2.7 us)
Async XLA Ops:
  0.0 2.2 copy-start.3
  0.0 2.9 copy-start.12
  2.9 7.1 %copy-start.10 = (bf16[8,128,1024]{2,1,0:T(8,128)(2,1)S(1)}, bf16[8,128,1024]{2,1,0:T(8,128)(2,1)}, u32[]{:S(2)}) copy-start(bf16[8,128,1024]{2,1,0:T(8,128)(2,1)} %param.15) | copy-start | bytes 6291460
  2.9 7.1 %copy-start.11 = (bf16[8,128,1024]{2,1,0:T(8,128)(2,1)S(1)}, bf16[8,128,1024]{2,1,0:T(8,128)(2,1)}, u32[]{:S(2)}) copy-start(bf16[8,128,1024]{2,1,0:T(8,128)(2,1)} %param.14) | copy-start | bytes 6291460
  3.9 8.6 %copy-start.8 = (bf16[256,4096]{1,0:T(8,128)(2,1)}, bf16[256,4096]{1,0:T(8,128)(2,1)S(1)}, u32[]{:S(2)}) copy-start(bf16[256,4096]{1,0:T(8,128)(2,1)S(1)} %fusion.5) | copy-start | bytes 6291460
  3.9 49.6 %collective-permute-start.1 = (bf16[256,4096]{1,0:T(8,128)(2,1)S(1)}, bf16[256,4096]{1,0:T(8,128)(2,1)}, u32[]{:S(2)}, u32[]{:S(2)}) collective-permute-start(bf16[256,4096]{1,0:T(8,128)(2,1)S(1)} %fusion.5), channel_id=1, source_target_pairs={{1,0},{2,1},{3,2},{5,4},{6,5},{7,6},{9,8},{10,9},{11,10},{13,12},{... | collective-permute-start | bytes 6291464 | tf_op jit(solution)/shard_map/ppermute | solution.py:261
  6.1 49.4 %collective-permute-start = (bf16[256,4096]{1,0:T(8,128)(2,1)S(1)}, bf16[256,4096]{1,0:T(8,128)(2,1)}, u32[]{:S(2)}, u32[]{:S(2)}) collective-permute-start(bf16[256,4096]{1,0:T(8,128)(2,1)S(1)} %fusion.5), channel_id=1, source_target_pairs={{0,1},{1,2},{2,3},{4,5},{5,6},{6,7},{8,9},{9,10},{10,11},{12,13},{... | collective-permute-start | bytes 6291464 | tf_op jit(solution)/shard_map/ppermute | solution.py:261
  12.4 95.3 %collective-permute-start.5 = (bf16[2,8,128,1024]{3,2,1,0:T(8,128)(2,1)}, bf16[2,8,128,1024]{3,2,1,0:T(8,128)(2,1)}, u32[]{:S(2)}, u32[]{:S(2)}) collective-permute-start(bf16[2,8,128,1024]{3,2,1,0:T(8,128)(2,1)} %pad_maximum_fusion.refs_1_), channel_id=1, source_target_pairs={{0,16},{4,20},{8,24},{12,28},{16,0},{20,4},{24,8},{28,12},{1,17},{... | collective-permute-start | bytes 12582920 | tf_op jit(solution)/shard_map/ppermute | solution.py:257
  14.0 93.8 %collective-permute-start.4 = (bf16[2,8,128,1024]{3,2,1,0:T(8,128)(2,1)}, bf16[2,8,128,1024]{3,2,1,0:T(8,128)(2,1)}, u32[]{:S(2)}, u32[]{:S(2)}) collective-permute-start(bf16[2,8,128,1024]{3,2,1,0:T(8,128)(2,1)} %pad_maximum_fusion.refs_1_), channel_id=1, source_target_pairs={{0,8},{4,12},{8,0},{12,4},{16,24},{20,28},{24,16},{28,20},{1,9},{5... | collective-permute-start | bytes 12582920 | tf_op jit(solution)/shard_map/ppermute | solution.py:257
  55.5 47.9 %collective-permute-start.2 = (bf16[256,4096]{1,0:T(8,128)(2,1)}, bf16[256,4096]{1,0:T(8,128)(2,1)S(1)}, u32[]{:S(2)}, u32[]{:S(2)}) collective-permute-start(bf16[256,4096]{1,0:T(8,128)(2,1)} %collective-permute-done), channel_id=1, source_target_pairs={{1,2},{2,3},{5,6},{6,7},{9,10},{10,11},{13,14},{14,15},{17,18},{18... | collective-permute-start | bytes 6291464 | tf_op jit(solution)/shard_map/ppermute | solution.py:261
  59.5 48.2 %collective-permute-start.3 = (bf16[256,4096]{1,0:T(8,128)(2,1)}, bf16[256,4096]{1,0:T(8,128)(2,1)}, u32[]{:S(2)}, u32[]{:S(2)}) collective-permute-start(bf16[256,4096]{1,0:T(8,128)(2,1)} %collective-permute-done.1), channel_id=1, source_target_pairs={{1,0},{2,1},{5,4},{6,5},{9,8},{10,9},{13,12},{14,13},{17,16},{18,1... | collective-permute-start | bytes 6291464 | tf_op jit(solution)/shard_map/ppermute | solution.py:261
  61.5 7.8 %copy-start.9 = (bf16[256,4096]{1,0:T(8,128)(2,1)S(1)}, bf16[256,4096]{1,0:T(8,128)(2,1)}, u32[]{:S(2)}) copy-start(bf16[256,4096]{1,0:T(8,128)(2,1)} %copy-done.8) | copy-start | bytes 6291460
  61.5 93.2 %collective-permute-start.9 = (bf16[512,4096]{1,0:T(8,128)(2,1)}, bf16[512,4096]{1,0:T(8,128)(2,1)}, u32[]{:S(2)}, u32[]{:S(2)}) collective-permute-start(bf16[512,4096]{1,0:T(8,128)(2,1)} %constant_dynamic-slice_fusion), channel_id=1, source_target_pairs={{0,1},{3,2},{4,5},{7,6},{8,9},{11,10},{12,13},{15,14},{16,17},{19,... | collective-permute-start | bytes 12582920 | tf_op jit(solution)/shard_map/ppermute | solution.py:261
  103.4 4.4 %copy-start.6 = (bf16[256,4096]{1,0:T(8,128)(2,1)}, bf16[256,4096]{1,0:T(8,128)(2,1)S(1)}, u32[]{:S(2)}) copy-start(bf16[256,4096]{1,0:T(8,128)(2,1)S(1)} %collective-permute-done.2) | copy-start | bytes 6291460
  103.4 57.9 %collective-permute-start.10 = (bf16[2,8,128,1024]{3,2,1,0:T(8,128)(2,1)}, bf16[2,8,128,1024]{3,2,1,0:T(8,128)(2,1)S(1)}, u32[]{:S(2)}, u32[]{:S(2)}) collective-permute-start(bf16[2,8,128,1024]{3,2,1,0:T(8,128)(2,1)} %pad_maximum_fusion.refs_1_), channel_id=1, source_target_pairs={{0,4},{4,0},{8,12},{12,8},{16,20},{20,16},{24,28},{28,24},{1,5},{5... | collective-permute-start | bytes 12582920 | tf_op jit(solution)/shard_map/ppermute | solution.py:257
  109.6 5.1 %copy-start.7 = (bf16[256,4096]{1,0:T(8,128)(2,1)S(1)}, bf16[256,4096]{1,0:T(8,128)(2,1)}, u32[]{:S(2)}) copy-start(bf16[256,4096]{1,0:T(8,128)(2,1)} %copy-done.6) | copy-start | bytes 6291460
  109.6 45.1 %collective-permute-start.8 = (bf16[8,128,1024]{2,1,0:T(8,128)(2,1)S(1)}, bf16[8,128,1024]{2,1,0:T(8,128)(2,1)S(1)}, u32[]{:S(2)}, u32[]{:S(2)}) collective-permute-start(bf16[8,128,1024]{2,1,0:T(8,128)(2,1)S(1)} %slice_bitcast_fusion), channel_id=1, source_target_pairs={{0,8},{4,12},{8,0},{12,4},{16,24},{20,28},{24,16},{28,20},{1,9},{5... | collective-permute-start | bytes 6291464 | tf_op jit(solution)/shard_map/ppermute | solution.py:257
  113.1 51.1 %copy-start.14 = (s32[16,2]{0,1:T(2,128)S(1)}, s32[16,2]{0,1:T(2,128)}, u32[]{:S(2)}) copy-start(s32[16,2]{0,1:T(2,128)} %param.16) | copy-start | bytes 388
  113.1 51.2 %copy-start.13 = (s32[16,2]{0,1:T(2,128)S(1)}, s32[16,2]{0,1:T(2,128)}, u32[]{:S(2)}) copy-start(s32[16,2]{0,1:T(2,128)} %param.17) | copy-start | bytes 388
  113.1 45.0 %collective-permute-start.7 = (bf16[8,128,1024]{2,1,0:T(8,128)(2,1)S(1)}, bf16[8,128,1024]{2,1,0:T(8,128)(2,1)}, u32[]{:S(2)}, u32[]{:S(2)}) collective-permute-start(bf16[8,128,1024]{2,1,0:T(8,128)(2,1)S(1)} %slice_bitcast_fusion.1), channel_id=1, source_target_pairs={{0,16},{4,20},{8,24},{12,28},{16,0},{20,4},{24,8},{28,12},{1,17},{... | collective-permute-start | bytes 6291464 | tf_op jit(solution)/shard_map/ppermute | solution.py:257
  116.5 44.8 %copy-start.4 = (bf16[256,4096]{1,0:T(8,128)(2,1)}, bf16[256,4096]{1,0:T(8,128)(2,1)S(1)}, u32[]{:S(2)}) copy-start(bf16[256,4096]{1,0:T(8,128)(2,1)S(1)} %broadcast_select_fusion) | copy-start | bytes 6291460
  116.5 44.3 %collective-permute-start.6 = (bf16[256,4096]{1,0:T(8,128)(2,1)S(1)}, bf16[256,4096]{1,0:T(8,128)(2,1)S(1)}, u32[]{:S(2)}, u32[]{:S(2)}) collective-permute-start(bf16[256,4096]{1,0:T(8,128)(2,1)S(1)} %broadcast_select_fusion), channel_id=1, source_target_pairs={{1,0},{2,3},{5,4},{6,7},{9,8},{10,11},{13,12},{14,15},{17,16},{18,... | collective-permute-start | bytes 6291464 | tf_op jit(solution)/shard_map/ppermute | solution.py:261
  154.7 25.5 %collective-permute-start.11 = (bf16[2,8,128,1024]{3,2,1,0:T(8,128)(2,1)}, bf16[2,8,128,1024]{3,2,1,0:T(8,128)(2,1)}, u32[]{:S(2)}, u32[]{:S(2)}) collective-permute-start(bf16[2,8,128,1024]{3,2,1,0:T(8,128)(2,1)} %collective-permute-done.4.refs_3_), channel_id=1, source_target_pairs={{0,4},{4,0},{8,12},{12,8},{16,20},{20,16},{24,28},{28,24},{1,5},{5... | collective-permute-start | bytes 12582920 | tf_op jit(solution)/shard_map/ppermute | solution.py:257
  154.8 25.4 %collective-permute-start.12 = (bf16[2,8,128,1024]{3,2,1,0:T(8,128)(2,1)}, bf16[2,8,128,1024]{3,2,1,0:T(8,128)(2,1)}, u32[]{:S(2)}, u32[]{:S(2)}) collective-permute-start(bf16[2,8,128,1024]{3,2,1,0:T(8,128)(2,1)} %collective-permute-done.5.refs_5_), channel_id=1, source_target_pairs={{0,4},{4,0},{8,12},{12,8},{16,20},{20,16},{24,28},{28,24},{1,5},{5... | collective-permute-start | bytes 12582920 | tf_op jit(solution)/shard_map/ppermute | solution.py:257
  160.8 1.4 copy-start.15
  160.8 39.0 %collective-permute-start.16 = (bf16[512,4096]{1,0:T(8,128)(2,1)}, bf16[512,4096]{1,0:T(8,128)(2,1)}, u32[]{:S(2)}, u32[]{:S(2)}) collective-permute-start(bf16[512,4096]{1,0:T(8,128)(2,1)} %collective-permute-done.9), channel_id=1, source_target_pairs={{0,4},{4,0},{8,12},{12,8},{16,20},{20,16},{24,28},{28,24},{1,5},{5... | collective-permute-start | bytes 12582920 | tf_op jit(solution)/shard_map/ppermute | solution.py:257
  160.8 19.3 %collective-permute-start.13 = (bf16[8,128,1024]{2,1,0:T(8,128)(2,1)}, bf16[8,128,1024]{2,1,0:T(8,128)(2,1)}, u32[]{:S(2)}, u32[]{:S(2)}) collective-permute-start(bf16[8,128,1024]{2,1,0:T(8,128)(2,1)} %collective-permute-done.7.refs_7_), channel_id=1, source_target_pairs={{0,4},{4,0},{8,12},{12,8},{16,20},{20,16},{24,28},{28,24},{1,5},{5... | collective-permute-start | bytes 6291464 | tf_op jit(solution)/shard_map/ppermute | solution.py:257
  162.2 2.0 copy-start
  164.1 16.0 %collective-permute-start.14 = (bf16[8,128,1024]{2,1,0:T(8,128)(2,1)S(1)}, bf16[8,128,1024]{2,1,0:T(8,128)(2,1)}, u32[]{:S(2)}, u32[]{:S(2)}) collective-permute-start(bf16[8,128,1024]{2,1,0:T(8,128)(2,1)S(1)} %collective-permute-done.8.refs_8_), channel_id=1, source_target_pairs={{0,4},{4,0},{8,12},{12,8},{16,20},{20,16},{24,28},{28,24},{1,5},{5... | collective-permute-start | bytes 6291464 | tf_op jit(solution)/shard_map/ppermute | solution.py:257
  165.2 15.0 %copy-start.1 = (bf16[2,8,128,1024]{3,2,1,0:T(8,128)(2,1)S(1)}, bf16[2,8,128,1024]{3,2,1,0:T(8,128)(2,1)}, u32[]{:S(2)}) copy-start(bf16[2,8,128,1024]{3,2,1,0:T(8,128)(2,1)} %copy-done) | copy-start | bytes 12582916
  165.2 15.0 %copy-start.2 = (s32[16]{0:T(128)S(1)}, s32[16]{0:T(128)}, u32[]{:S(2)}) copy-start(s32[16]{0:T(128)} %counts_ref.7) | copy-start | bytes 196
  171.7 13.2 %copy-start.5 = (bf16[256,4096]{1,0:T(8,128)(2,1)S(1)}, bf16[256,4096]{1,0:T(8,128)(2,1)}, u32[]{:S(2)}) copy-start(bf16[256,4096]{1,0:T(8,128)(2,1)} %copy-done.4) | copy-start | bytes 6291460
  183.4 16.4 %collective-permute-start.15 = (bf16[256,1024]{1,0:T(8,128)(2,1)S(1)}, bf16[256,1024]{1,0:T(8,128)(2,1)S(1)}, u32[]{:S(2)}, u32[]{:S(2)}) collective-permute-start(bf16[256,1024]{1,0:T(8,128)(2,1)S(1)} %shard_map.100), channel_id=1, source_target_pairs={{0,1},{3,2},{4,5},{7,6},{8,9},{11,10},{12,13},{15,14},{16,17},{19,... | collective-permute-start | bytes 1572872 | tf_op jit(solution)/shard_map/ppermute | solution.py:261
  184.9 12.1 %slice-start = ((s8[8388608]{0:T(1024)(128)(4,1)}), s8[4194304]{0:T(1024)(128)(4,1)S(1)}, s32[]{:S(2)}) async-start(s8[8388608]{0:T(1024)(128)(4,1)} %bitcast.24), calls=%async_computation | async-start | bytes 8388608
  191.5 5.5 %slice-start.1 = ((s8[8388608]{0:T(1024)(128)(4,1)}), s8[4194304]{0:T(1024)(128)(4,1)S(1)}, s32[]{:S(2)}) async-start(s8[8388608]{0:T(1024)(128)(4,1)} %bitcast.24), calls=%async_computation.1 | async-start | bytes 8388608
  195.7 31.5 %collective-permute-start.18 = (bf16[256,1024]{1,0:T(8,128)(2,1)S(1)}, bf16[256,1024]{1,0:T(8,128)(2,1)S(1)}, u32[]{:S(2)}, u32[]{:S(2)}) collective-permute-start(bf16[256,1024]{1,0:T(8,128)(2,1)S(1)} %shard_map.101), channel_id=1, source_target_pairs={{0,1},{3,2},{4,5},{7,6},{8,9},{11,10},{12,13},{15,14},{16,17},{19,... | collective-permute-start | bytes 1572872 | tf_op jit(solution)/shard_map/ppermute | solution.py:261
  204.6 30.2 %collective-permute-start.17 = (bf16[256,2048]{1,0:T(8,128)(2,1)S(1)}, bf16[256,2048]{1,0:T(8,128)(2,1)S(1)}, u32[]{:S(2)}, u32[]{:S(2)}) collective-permute-start(bf16[256,2048]{1,0:T(8,128)(2,1)S(1)} %add_convert_fusion.5), channel_id=1, source_target_pairs={{1,2},{2,1},{5,6},{6,5},{9,10},{10,9},{13,14},{14,13},{17,18},{18,... | collective-permute-start | bytes 3145736 | tf_op jit(solution)/shard_map/ppermute | solution.py:261
  216.5 40.8 %collective-permute-start.22 = (bf16[256,2048]{1,0:T(8,128)(2,1)}, bf16[256,2048]{1,0:T(8,128)(2,1)}, u32[]{:S(2)}, u32[]{:S(2)}) collective-permute-start(bf16[256,2048]{1,0:T(8,128)(2,1)} %add_convert_fusion.4), channel_id=1, source_target_pairs={{1,2},{2,1},{5,6},{6,5},{9,10},{10,9},{13,14},{14,13},{17,18},{18,... | collective-permute-start | bytes 3145736 | tf_op jit(solution)/shard_map/ppermute | solution.py:261
  247.4 16.1 %collective-permute-start.19 = (bf16[256,1024]{1,0:T(8,128)(2,1)S(1)}, bf16[256,1024]{1,0:T(8,128)(2,1)S(1)}, u32[]{:S(2)}, u32[]{:S(2)}) collective-permute-start(bf16[256,1024]{1,0:T(8,128)(2,1)S(1)} %shard_map.103), channel_id=1, source_target_pairs={{0,1},{3,2},{4,5},{7,6},{8,9},{11,10},{12,13},{15,14},{16,17},{19,... | collective-permute-start | bytes 1572872 | tf_op jit(solution)/shard_map/ppermute | solution.py:261
  248.7 57.5 %collective-permute-start.20 = (bf16[256,4096]{1,0:T(8,128)(2,1)S(1)}, bf16[256,4096]{1,0:T(8,128)(2,1)S(1)}, u32[]{:S(2)}, u32[]{:S(2)}) collective-permute-start(bf16[256,4096]{1,0:T(8,128)(2,1)S(1)} %add_convert_fusion.1), channel_id=1, source_target_pairs={{1,2},{2,1},{5,6},{6,5},{9,10},{10,9},{13,14},{14,13},{17,18},{18,... | collective-permute-start | bytes 6291464 | tf_op jit(solution)/shard_map/ppermute | solution.py:261
  259.5 24.8 %collective-permute-start.23 = (bf16[256,2048]{1,0:T(8,128)(2,1)S(1)}, bf16[256,2048]{1,0:T(8,128)(2,1)S(1)}, u32[]{:S(2)}, u32[]{:S(2)}) collective-permute-start(bf16[256,2048]{1,0:T(8,128)(2,1)S(1)} %get-tuple-element.81), channel_id=1, source_target_pairs={{1,0},{2,3},{5,4},{6,7},{9,8},{10,11},{13,12},{14,15},{17,16},{18,... | collective-permute-start | bytes 3145736 | tf_op jit(solution)/shard_map/ppermute | solution.py:261
  260.8 45.4 %collective-permute-start.21 = (bf16[256,2048]{1,0:T(8,128)(2,1)S(1)}, bf16[256,2048]{1,0:T(8,128)(2,1)S(1)}, u32[]{:S(2)}, u32[]{:S(2)}) collective-permute-start(bf16[256,2048]{1,0:T(8,128)(2,1)S(1)} %get-tuple-element.82), channel_id=1, source_target_pairs={{1,0},{2,3},{5,4},{6,7},{9,8},{10,11},{13,12},{14,15},{17,16},{18,... | collective-permute-start | bytes 3145736 | tf_op jit(solution)/shard_map/ppermute | solution.py:261

commit v3 on v2

--- a/solution.py
+++ b/solution.py
@@ -119,18 +119,22 @@
 
 SHARD_ORDER = ((3, 2, 1, 0), (3, 2, 1, 0), (0, 1, 2, 3), (0, 1, 2, 3))
 HEADS_TOGETHER = 8
+SMALL = pl.CostEstimate(flops=1, bytes_accessed=1, transcendentals=0)
 OUTWARD = ((1, 0), (2, 3))
 INWARD = ((0, 1), (3, 2))
 MIDDLE = ((1, 2), (2, 1))
 
 
+def in_hbm(values):
+    return pltpu.with_memory_space_constraint(values, pltpu.HBM)
+
+
 def attention_kernel(step, blocks, order_ref, relative_ref, slots_ref, counts_ref, *refs):
     query_buf = refs[0]
-    pair_refs = refs[1:7]
-    key_refs = [ref.at[0] for ref in pair_refs] + [refs[7], refs[9]]
-    value_refs = [ref.at[1] for ref in pair_refs] + [refs[8], refs[10]]
-    out_ref = refs[11]
-    key_buf, value_buf, total_buf, cache_sem = refs[12:]
+    key_refs = refs[1:9]
+    value_refs = refs[9:17]
+    out_ref = refs[17]
+    key_buf, value_buf, total_buf, cache_sem = refs[18:]
     shard = order_ref[step]
     rows, width = query_buf.shape
     head_count = width // HD
@@ -225,17 +229,17 @@
     out_ref[...] = total_buf[:rows].astype(jnp.bfloat16)
 
 
-def shard_attention(step, order, relative, slots, counts, queries, caches):
+def shard_attention(step, order, relative, slots, counts, queries, keys, values):
     rows, width = queries.shape
     blocks = rows // M
-    anywhere = pl.BlockSpec(memory_space=pl.ANY)
+    anywhere = pl.BlockSpec(memory_space=pltpu.HBM)
     return pl.pallas_call(
         functools.partial(attention_kernel, step, blocks),
         out_shape=jax.ShapeDtypeStruct((rows, width), jnp.bfloat16),
         grid_spec=pltpu.PrefetchScalarGridSpec(
             num_scalar_prefetch=4,
             grid=(1,),
-            in_specs=[pl.BlockSpec((rows, width), lambda i, *_: (0, 0))] + [anywhere] * 10,
+            in_specs=[pl.BlockSpec((rows, width), lambda i, *_: (0, 0))] + [anywhere] * 16,
             out_specs=pl.BlockSpec((rows, width), lambda i, *_: (0, 0)),
             scratch_shapes=[
                 pltpu.VMEM((blocks + 1, 2 * NL, width), jnp.bfloat16),
@@ -245,12 +249,162 @@
             ],
         ),
         compiler_params=pltpu.CompilerParams(vmem_limit_bytes=16 << 20),
-        cost_estimate=pl.CostEstimate(
-            flops=4 * rows * 2 * NL * width,
-            bytes_accessed=2 * (rows * width * 2 + (blocks + 1) * 2 * NL * width * 2),
-            transcendentals=rows * 2 * NL * (width // HD),
+        cost_estimate=SMALL,
+    )(order, relative, slots, counts, queries, *keys, *values)
+
+
+def project_kernel(scale, which_ref, *refs):
+    sources = refs[: len(refs) - 4]
+    weight_ref, out_ref, rows_buf, sem = refs[len(refs) - 4 :]
+
+    @pl.when(pl.program_id(0) == 0)
+    def _():
+        for index, source in enumerate(sources):
+
+            @pl.when(which_ref[0] == index)
+            def _():
+                copy = pltpu.make_async_copy(source, rows_buf, sem)
+                copy.start()
+                copy.wait()
+
+    total = jnp.dot(rows_buf[...], weight_ref[...], preferred_element_type=jnp.float32)
+    out_ref[...] = (total * scale).astype(jnp.bfloat16)
+
+
+def project(which, sources, weight, streamed=True):
+    rows, depth = sources[0].shape
+    width = weight.shape[1]
+    return pl.pallas_call(
+        functools.partial(project_kernel, 1.0 / math.sqrt(HD)),
+        out_shape=jax.ShapeDtypeStruct((rows, width), jnp.bfloat16),
+        grid_spec=pltpu.PrefetchScalarGridSpec(
+            num_scalar_prefetch=1,
+            grid=(width // 256,),
+            in_specs=[pl.BlockSpec(memory_space=pltpu.HBM)] * len(sources)
+            + [pl.BlockSpec((depth, 256), lambda i, _: (0, i))],
+            out_specs=pl.BlockSpec((rows, 256), lambda i, _: (0, i)),
+            scratch_shapes=[pltpu.VMEM((rows, depth), jnp.bfloat16), pltpu.SemaphoreType.DMA],
         ),
-    )(order, relative, slots, counts, queries, *caches)
+        compiler_params=pltpu.CompilerParams(vmem_limit_bytes=16 << 20),
+        cost_estimate=SMALL,
+    )(which.reshape(1), *sources, in_hbm(weight) if streamed else weight)
+
+
+def output_kernel(core_ref, attended_ref, handed_ref, weight_ref, *refs):
+    out_ref = refs[4]
+    height = refs[0].shape[0]
+    if weight_ref is None:
+        total = attended_ref[...]
+    else:
+        total = jnp.dot(attended_ref[...], weight_ref[...], preferred_element_type=jnp.float32)
+    for index, piece in enumerate(refs[:4]):
+        from_core = core_ref[0] if index < 2 else 1 - core_ref[0]
+        start = from_core * 2 * height + index % 2 * height
+        heads = handed_ref[:, pl.ds(pl.multiple_of(start, height), height)]
+        total += jnp.dot(heads, piece[...], preferred_element_type=jnp.float32)
+    out_ref[...] = total.astype(jnp.bfloat16)
+
+
+def output_rest_kernel(core_ref, part_ref, handed_ref, *refs):
+    output_kernel(core_ref, part_ref, handed_ref, None, *refs)
+
+
+def output_plus_kernel(attended_ref, weight_ref, plus_ref, out_ref):
+    total = jnp.dot(attended_ref[...], weight_ref[...], preferred_element_type=jnp.float32)
+    out_ref[...] = (total + plus_ref[...].astype(jnp.float32)).astype(jnp.bfloat16)
+
+
+def output_only_kernel(attended_ref, weight_ref, out_ref):
+    out_ref[...] = jnp.dot(attended_ref[...], weight_ref[...], preferred_element_type=jnp.float32)
+
+
+def fixed_block(rows, depth):
+    return pl.BlockSpec((rows, depth), lambda i, *_: (0, 0))
+
+
+def column_block(height, start):
+    return pl.BlockSpec((height, 512), lambda i, *_: (0, start + i))
+
+
+def output_call(kernel, prefetched, in_specs, rows, count, kind, *operands):
+    return pl.pallas_call(
+        kernel,
+        out_shape=jax.ShapeDtypeStruct((rows, count * 512), kind),
+        grid_spec=pltpu.PrefetchScalarGridSpec(
+            num_scalar_prefetch=prefetched,
+            grid=(count,),
+            in_specs=in_specs,
+            out_specs=column_block(rows, 0),
+        ),
+        compiler_params=pltpu.CompilerParams(vmem_limit_bytes=16 << 20),
+        cost_estimate=SMALL,
+    )(*operands)
+
+
+def output_part(core, attended, handed, weight, inner, first, count):
+    rows, depth = handed.shape
+    inner = [in_hbm(piece) for piece in inner]
+    pieces = [column_block(piece.shape[0], first) for piece in inner]
+    return output_call(
+        output_kernel,
+        1,
+        [fixed_block(rows, depth), fixed_block(rows, depth), column_block(depth, first)] + pieces,
+        rows,
+        count,
+        jnp.bfloat16,
+        core.reshape(1),
+        attended,
+        handed,
+        in_hbm(weight),
+        *inner,
+    )
+
+
+def output_rest(core, part, handed, inner, first, count):
+    rows, depth = handed.shape
+    inner = [in_hbm(piece) for piece in inner]
+    pieces = [column_block(piece.shape[0], first) for piece in inner]
+    return output_call(
+        output_rest_kernel,
+        1,
+        [column_block(rows, 0), fixed_block(rows, depth)] + pieces,
+        rows,
+        count,
+        jnp.bfloat16,
+        core.reshape(1),
+        part,
+        handed,
+        *inner,
+    )
+
+
+def output_only(attended, weight, first, count):
+    rows, depth = attended.shape
+    return output_call(
+        output_only_kernel,
+        0,
+        [fixed_block(rows, depth), column_block(depth, first)],
+        rows,
+        count,
+        jnp.float32,
+        attended,
+        in_hbm(weight),
+    )
+
+
+def output_plus(attended, weight, plus, first, count):
+    rows, depth = attended.shape
+    return output_call(
+        output_plus_kernel,
+        0,
+        [fixed_block(rows, depth), column_block(depth, first), column_block(rows, 0)],
+        rows,
+        count,
+        jnp.bfloat16,
+        attended,
+        in_hbm(weight),
+        plus,
+    )
 
 
 def swap(values, bits):
@@ -272,100 +426,125 @@
     slot_ids,
     valid_counts,
 ):
-    score_scale = 1.0 / math.sqrt(HD)
     place = lax.axis_index("mp")
-
-    def project(rows):
-        return (jnp.dot(rows, query_weight, preferred_element_type=jnp.float32) * score_scale).astype(
-            jnp.bfloat16
-        )
 
     together = lax.optimization_barrier
     core = lax.axis_index("dp") % 2
     half = output_weight.shape[0] // 2
     inside = (place == 1) | (place == 2)
-    low = place < 2
+    keys, values = [key_cache] + [None] * 7, [value_cache] + [None] * 7
     normed = layer_norm(tokens, norm_gain)
-    below = along(normed, ((0, 1), (1, 2), (2, 3)))
-    above = along(normed, ((1, 0), (2, 1), (3, 2)))
-    cache = jnp.stack([key_cache, value_cache])
-    cache_x, cache_y, cache_core = swap(cache, 2), swap(cache, 4), swap(cache, 1)
-    handed = lax.dynamic_slice_in_dim(output_weight, core * half, half, 0)
-    below, above, handed = together((below, above, handed))
-    below_two = along(below, ((1, 2), (2, 3)))
-    above_two = along(above, ((1, 0), (2, 1)))
-    inner = along(handed, INWARD)
-    third_queries = project(jnp.where(inside, normed, jnp.where(low, above, below)))
-    fourth_queries = project(jnp.where(inside, jnp.where(low, below, above), normed))
-    below_two, above_two, cache_x, cache_y, third_queries, fourth_queries = together(
-        (below_two, above_two, cache_x, cache_y, third_queries, fourth_queries)
-    )
-    two = jnp.where(low, above_two, below_two)
-    three = along(two, OUTWARD)
-    keys_xy, values_xy = swap(cache_x[0], 4), swap(cache_y[1], 2)
-    cache_x_core, cache_y_core = swap(cache_x, 1), swap(cache_y, 1)
-    three, keys_xy, values_xy, inner = together((three, keys_xy, values_xy, inner))
-    keys_xy_core, values_xy_core = swap(keys_xy, 1), swap(values_xy, 1)
-    other_inner = swap(inner, 1)
-    first_queries = project(jnp.where(inside, two, three))
-    caches = [cache, cache_core, cache_x, cache_x_core, cache_y, cache_y_core]
-    caches += [keys_xy, values_xy, keys_xy_core, values_xy_core]
-
-    order = lax.dynamic_index_in_dim(jnp.array(SHARD_ORDER, jnp.int32), place, 0, keepdims=False)
+    beside = along(normed, INWARD + OUTWARD)
+    middle = along(normed, MIDDLE)
+    keys_x, values_y = swap(key_cache, 2), swap(value_cache, 4)
+    keys[1] = swap(key_cache, 1)
+    keys[1], value_source = together((keys[1], value_cache))
+    values[1] = swap(value_source, 1)
+    handed = [
+        lax.dynamic_slice_in_dim(output_weight, core * half + start, half // 2, 0) for start in (0, half // 2)
+    ]
+    order, third_from, fourth_from, second_from, first_from = (
+        lax.dynamic_index_in_dim(jnp.array(table, jnp.int32), place, 0, keepdims=False)
+        for table in (SHARD_ORDER, (1, 0, 0, 1), (0, 1, 1, 0), (0, 1, 1, 0), (1, 0, 0, 1))
+    )
     relative = owners.reshape(-1) ^ lax.axis_index("dp")
     slots = slot_ids.reshape(-1)
+    beside, middle, handed, keys[1], values[1], order, relative, slots, keys_x, values_y, keys_far, values_far = (
+        together(
+            (
+                beside,
+                middle,
+                handed,
+                keys[1],
+                values[1],
+                order,
+                relative,
+                slots,
+                keys_x,
+                values_y,
+                key_cache,
+                value_cache,
+            )
+        )
+    )
+    beside_two = along(beside, MIDDLE)
+    middle_two = along(middle, OUTWARD)
+    keys_y, values_x = swap(keys_far, 4), swap(values_far, 2)
+    inner = [along(handed[0], INWARD)]
+    third_queries = project(third_from, (normed, beside), query_weight)
+    fourth_queries = project(fourth_from, (normed, beside), query_weight)
+    beside_two, middle_two, keys_y, values_x, keys_x, values_y, third_queries, fourth_queries, handed, inner = (
+        together(
+            (
+                beside_two,
+                middle_two,
+                keys_y,
+                values_x,
+                keys_x,
+                values_y,
+                third_queries,
+                fourth_queries,
+                handed,
+                inner,
+            )
+        )
+    )
+    keys[2], values[4], keys[4], values[2] = keys_x, values_y, keys_y, values_x
+    three = along(beside_two, OUTWARD)
+    keys[6], values[6] = swap(keys_x, 4), swap(values_y, 2)
+    inner += [along(handed[1], INWARD)]
+    second_queries = project(second_from, (middle_two, middle), query_weight)
+    keys[3], values[5] = swap(keys_x, 1), swap(values_y, 1)
+    keys[3], keys_y, values_x, second_queries = together((keys[3], keys_y, values_x, second_queries))
+    keys[5], values[3] = swap(keys_y, 1), swap(values_x, 1)
+    three, keys[6], values[6], inner = together((three, keys[6], values[6], inner))
+    keys[7], values[7] = swap(keys[6], 1), swap(values[6], 1)
+    first_queries = project(first_from, (beside_two, three), query_weight, streamed=False)
 
     def attend(step, queries):
-        return shard_attention(step, order, relative, slots, valid_counts, queries, caches)
-
-    def product(attended, weight):
-        return jnp.dot(attended, weight, preferred_element_type=jnp.float32)
-
-    def handed_product(attended, columns):
-        total = None
-        for piece, from_core in ((inner, core), (other_inner, 1 - core)):
-            heads = lax.dynamic_slice_in_dim(attended, from_core * half, half, 1)
-            term = product(heads, piece[:, columns])
-            total = term if total is None else total + term
-        return total
-
-    def rounded_sum(one, other):
-        return (one.astype(jnp.float32) + other.astype(jnp.float32)).astype(jnp.bfloat16)
-
-    width = output_weight.shape[1] // 2
-    left, right = slice(0, width), slice(width, 2 * width)
+        return shard_attention(step, order, relative, slots, valid_counts, queries, keys, values)
+
+    def output(attended, handed, first, count):
+        return output_part(core, attended, handed, output_weight, inner, first, count)
+
+    tiles = output_weight.shape[1] // 512
     first = attend(0, first_queries)
     first_in = along(first, INWARD)
-    first, two, above, below = together((first, two, above, below))
-    first_part = product(first, output_weight)
-    second = attend(
-        1, project(jnp.where(inside, jnp.where(low, above, below), two))
-    )
+    first, second_queries, inner = together((first, second_queries, inner))
+    inner += [swap(piece, 1) for piece in inner]
+    left = output_only(first, output_weight, 0, tiles // 2)
+    left, second_queries = together((left, second_queries))
+    second = attend(1, second_queries)
     second_in = along(second, INWARD)
-    first_in, first_part, second = together((first_in, first_part, second))
-    first_across = []
-    for columns in (left, right):
-        piece = rounded_sum(first_part[:, columns], handed_product(first_in, columns))
-        piece, fourth_queries, second, first_in = together((piece, fourth_queries, second, first_in))
-        first_across.append(along(piece, MIDDLE))
-    fourth = product(attend(3, fourth_queries), output_weight).astype(jnp.bfloat16)
-    second_part = product(second, output_weight)
-    first_left, fourth, second_part, second_in = together((first_across[0], fourth, second_part, second_in))
-    outward_left = along(rounded_sum(fourth[:, left], first_left), OUTWARD)
-    second = rounded_sum(second_part, handed_product(second_in, slice(0, 2 * width)))
-    second, third_queries = together((second, third_queries))
-    second_across = along(second, MIDDLE)
-    outward_right = along(rounded_sum(fourth[:, right], first_across[1]), OUTWARD)
+    first_in, second = together((first_in, second))
+    left = output_rest(core, left, first_in, inner, 0, tiles // 2)
+    across_left = along(left, MIDDLE)
+    _, first, first_in = together((left, first, first_in))
+    right = output(first, first_in, tiles // 2, tiles // 2)
+    across_right = along(right, MIDDLE)
+    _, fourth_queries = together((right, fourth_queries))
+    fourth = attend(3, fourth_queries)
+    fourth, third_queries = together((fourth, third_queries))
     third = attend(2, third_queries)
     third_in = along(third, INWARD)
-    third = rounded_sum(product(third, output_weight), handed_product(third_in, slice(0, 2 * width)))
-    third, fourth, second_across, outward_left, outward_right = together(
-        (third, fourth, second_across, outward_left, outward_right)
-    )
-    return rounded_sum(
-        jnp.where(inside, third, fourth),
-        jnp.where(inside, second_across, jnp.concatenate([outward_left, outward_right], axis=1)),
-    )
+    _, second, second_in = together((third, second, second_in))
+    second = output(second, second_in, 0, tiles)
+    second_across = along(second, MIDDLE)
+    _, fourth, across_left = together((second, fourth, across_left))
+    left = output_plus(fourth, output_weight, across_left, 0, tiles // 2)
+    outward_left = along(left, OUTWARD)
+    fourth, across_right, outward_left, third_in = together((fourth, across_right, outward_left, third_in))
+    right = output_plus(fourth, output_weight, across_right, tiles // 2, tiles // 2)
+    outward_right = along(right, OUTWARD)
+    _, third, third_in = together((right, third, third_in))
+    third = output(third, third_in, 0, tiles)
+    third, second_across, outward_left, outward_right = together(
+        (third, second_across, outward_left, outward_right)
+    )
+    fourth = jnp.concatenate([left, right], axis=1)
+    outward = jnp.concatenate([outward_left, outward_right], axis=1)
+    mine = jnp.where(inside, third, fourth).astype(jnp.float32)
+    return (mine + jnp.where(inside, second_across, outward).astype(jnp.float32)).astype(jnp.bfloat16)
 
 
 def on_device(*arguments):

time: 312 us -> 299 us (0.958)
  Pallas kernels: 16 us -> 88.9 us
  matrix products: 60 us -> 0 us
  waiting for transfers between devices: 165 us -> 145 us
  other arithmetic: 13.4 us -> 8.69 us
    pallas_call x0 -> x11, Pallas kernels: none -> 72.5 us  [the longest x7 43.1 us: output_call(): pl.pallas_call(kernel, out_shape=jax.ShapeDtypeStruct((rows, count * 512)...]
    dot_general x16 -> x0, matrix products: 60 us -> none  [the longest x12 34.1 us: product(): return jnp.dot(attended, weight, preferred_element_type=jnp.float32)]
    ppermute x14 -> x15, waiting for transfers between devices: 154 us -> 134 us  [along(): return lax.ppermute(values, 'mp', list(pairs))]
    squeeze x3 -> x1, local copies, waits for them, and re-layouts: 4.43 us -> 0.69 us  [cube_on_device(): lax.dynamic_index_in_dim(jnp.array(table, jnp.int32), place, 0, keepdims=...]
    ppermute x14 -> x15, starting transfers between devices: 34.1 us -> 35.4 us  [along(): return lax.ppermute(values, 'mp', list(pairs))]
    ppermute x10 -> x16, starting transfers between devices: 7.08 us -> 7.8 us  [swap(): return lax.ppermute(values, 'dp', [(i, i ^ bits) for i in range(8)])]
    ppermute x10 -> x16, waiting for transfers between devices: 11.4 us -> 11.9 us  [swap(): return lax.ppermute(values, 'dp', [(i, i ^ bits) for i in range(8)])]
  transfers between devices with their start and end apart: 24 -> 31, of which waited for: 15 -> 18; matrix products, arithmetic and copies ran while one was open for 25% -> 4% of each run, Pallas kernels for 5% -> 27%
where the time goes in v3:
time: 299 us; the launch traced here: 298 us
  waiting for transfers between devices  145 us (48%)
  Pallas kernels  88.9 us (30%)
  starting transfers between devices  43.2 us (14%)
  local copies, waits for them, and re-layouts  11 us (4%)
  other arithmetic  8.69 us (3%)
    ppermute x15, waiting for transfers between devices, along(): return lax.ppermute(values, 'mp', list(pairs))  134 us
    pallas_call x7, Pallas kernels, output_call(): pl.pallas_call(kernel, out_shape=jax.ShapeDtypeStruct((rows, count * 512)...  43.1 us
    ppermute x15, starting transfers between devices, along(): return lax.ppermute(values, 'mp', list(pairs))  35.4 us
    pallas_call x4, Pallas kernels, project(): pl.pallas_call(functools.partial(project_kernel, 1.0 / math.sqrt(HD)), ou...  29.4 us
    pallas_call x4, Pallas kernels, shard_attention(): pl.pallas_call(functools.partial(attention_kernel, step, blocks), out_sha...  16.4 us
    ppermute x16, waiting for transfers between devices, swap(): return lax.ppermute(values, 'dp', [(i, i ^ bits) for i in range(8)])  11.9 us
    ppermute x16, starting transfers between devices, swap(): return lax.ppermute(values, 'dp', [(i, i ^ bits) for i in range(8)])  7.8 us
  transfers between devices with their start and end apart: 31, of which 18 were waited for; matrix products, arithmetic and copies ran while one was open for 4% of the time, Pallas kernels for 27%

profile of v3, /device:TPU:8, one launch (start us, length us, event | category | flops | bytes accessed | tf_op | source)
XLA Modules:
  0.0 297.7 jit_solution(10556784587993496125)
XLA Ops:
  0.0 2.1 convert_reduce_fusion
  2.2 0.7 fusion.2
  3.0 2.2 fusion.4.refs_0_
  5.2 5.0 %collective-permute-start.1 = (bf16[256,4096]{1,0:T(8,128)(2,1)}, bf16[256,4096]{1,0:T(8,128)(2,1)}, u32[]{:S(2)}, u32[]{:S(2)}) collective-permute-start(bf16[256,4096]{1,0:T(8,128)(2,1)} %fusion.4.refs_0_), channel_id=1, source_target_pairs={{1,2},{2,1},{5,6},{6,5},{9,10},{10,9},{13,14},{14,13},{17,18},{18,... | collective-permute-start | bytes 6291464 | tf_op jit(solution)/shard_map/ppermute | solution.py:415
  10.2 1.6 collective-permute-start.4
  11.8 1.5 collective-permute-start.5
  13.3 1.4 copy-done.1
  15.1 0.7 fusion.5.order_ref
  15.8 4.0 %constant_dynamic-slice_fusion.1 = (bf16[256,4096]{1,0:T(8,128)(2,1)}, bf16[256,4096]{1,0:T(8,128)(2,1)S(1)}) fusion(bf16[1024,4096]{1,0:T(8,128)(2,1)} %weight_ref.11, s32[]{:T(128)S(6)} %select_n.37, s32[]{:T(128)S(6)} %select_n.36), kind=kLoop, calls=%fused_computation.12 | loop fusion | bytes 8388616 | tf_op jit(solution)/shard_map/dynamic_slice | solution.py:444
  19.8 33.5 %collective-permute-done.refs_1_ = bf16[256,4096]{1,0:T(8,128)(2,1)} collective-permute-done((bf16[256,4096]{1,0:T(8,128)(2,1)}, bf16[256,4096]{1,0:T(8,128)(2,1)}, u32[]{:S(2)}, u32[]{:S(2)}) %collective-permute-start) | collective-permute-done | bytes 2097184 | tf_op jit(solution)/shard_map/ppermute | solution.py:415
  53.3 3.0 %collective-permute-done.1.refs_1_ = bf16[256,4096]{1,0:T(8,128)(2,1)} collective-permute-done((bf16[256,4096]{1,0:T(8,128)(2,1)}, bf16[256,4096]{1,0:T(8,128)(2,1)}, u32[]{:S(2)}, u32[]{:S(2)}) %collective-permute-start.1) | collective-permute-done | bytes 2097184 | tf_op jit(solution)/shard_map/ppermute | solution.py:415
  56.3 1.3 collective-permute-done.4.refs_3_
  57.7 1.4 collective-permute-done.5.refs_13_
  59.1 1.3 collective-permute-start.10
  60.4 2.2 collective-permute-start.6
  62.6 3.4 %collective-permute-start.7 = (bf16[256,4096]{1,0:T(8,128)(2,1)}, bf16[256,4096]{1,0:T(8,128)(2,1)S(1)}, u32[]{:S(2)}, u32[]{:S(2)}) collective-permute-start(bf16[256,4096]{1,0:T(8,128)(2,1)} %collective-permute-done.1.refs_1_), channel_id=1, source_target_pairs={{1,0},{2,3},{5,4},{6,7},{9,8},{10,11},{13,12},{14,15},{17,16},{18,... | collective-permute-start | bytes 6291464 | tf_op jit(solution)/shard_map/ppermute | solution.py:415
  66.0 1.6 collective-permute-start.8
  67.6 0.5 collective-permute-start.9
  68.1 0.6 dynamic_slice.26.which_ref
  68.7 0.7 dynamic_slice.28.which_ref
  69.4 8.3 %shard_map.136.refs_0_ = bf16[256,1024]{1,0:T(8,128)(2,1)S(1)} custom-call(s32[1]{0:T(128)} %dynamic_slice.26.which_ref, bf16[256,4096]{1,0:T(8,128)(2,1)} %fusion.4.refs_0_, bf16[256,4096]{1,0:T(8,128)(2,1)} %collective-permute-done.refs_1_, bf16[4096,1024]{1,0:T(8,128)(2,1)} %refs_2_.7), custom_call_target="tpu_custom_call" | custom-call | flops 1 | bytes 1 | tf_op jit(solution)/shard_map/pallas_call | solution.py:277
  77.7 8.3 %shard_map.137.refs_0_ = bf16[256,1024]{1,0:T(8,128)(2,1)S(1)} custom-call(s32[1]{0:T(128)} %dynamic_slice.28.which_ref, bf16[256,4096]{1,0:T(8,128)(2,1)} %fusion.4.refs_0_, bf16[256,4096]{1,0:T(8,128)(2,1)} %collective-permute-done.refs_1_, bf16[4096,1024]{1,0:T(8,128)(2,1)} %refs_2_.7), custom_call_target="tpu_custom_call" | custom-call | flops 1 | bytes 1 | tf_op jit(solution)/shard_map/pallas_call | solution.py:277
  86.0 21.0 %collective-permute-done.10.refs_0_ = bf16[256,4096]{1,0:T(8,128)(2,1)S(1)} collective-permute-done((bf16[256,4096]{1,0:T(8,128)(2,1)S(1)}, bf16[256,4096]{1,0:T(8,128)(2,1)S(1)}, u32[]{:S(2)}, u32[]{:S(2)}) %collective-permute-start.10) | collective-permute-done | bytes 2097184 | tf_op jit(solution)/shard_map/ppermute | solution.py:415
  107.0 1.5 collective-permute-done.6.refs_0_
  108.5 0.9 collective-permute-done.7.refs_0_
  109.4 2.1 collective-permute-done.8.refs_5_
  111.5 1.4 collective-permute-done.9.refs_11_
  113.0 1.6 collective-permute-start.11
  114.6 0.9 collective-permute-start.12
  115.5 0.5 collective-permute-start.13
  116.0 1.3 collective-permute-start.14
  117.3 8.0 %shard_map.139.refs_0_ = bf16[256,1024]{1,0:T(8,128)(2,1)S(1)} custom-call(s32[1]{0:T(128)} %dynamic_slice.28.which_ref, bf16[256,4096]{1,0:T(8,128)(2,1)S(1)} %collective-permute-done.7.refs_0_, bf16[256,4096]{1,0:T(8,128)(2,1)} %collective-permute-done.1.refs_1_, bf16[4096,1024]{1,0:T(8,128)(2,1)} %refs_2_.7), custom_call_target="tpu_custom_call" | custom-call | flops 1 | bytes 1 | tf_op jit(solution)/shard_map/pallas_call | solution.py:277
  125.4 34.7 %collective-permute-done.11.refs_1_ = bf16[256,4096]{1,0:T(8,128)(2,1)S(1)} collective-permute-done((bf16[256,4096]{1,0:T(8,128)(2,1)S(1)}, bf16[256,4096]{1,0:T(8,128)(2,1)S(1)}, u32[]{:S(2)}, u32[]{:S(2)}) %collective-permute-start.11) | collective-permute-done | bytes 2097184 | tf_op jit(solution)/shard_map/ppermute | solution.py:415
  160.1 2.6 collective-permute-done.12.refs_7_
  163.1 2.1 collective-permute-done.14.refs_1_
  165.3 0.5 collective-permute-start.20
  165.8 4.8 %shard_map.138.refs_0_ = bf16[256,1024]{1,0:T(8,128)(2,1)S(1)} custom-call(s32[1]{0:T(128)} %dynamic_slice.26.which_ref, bf16[256,4096]{1,0:T(8,128)(2,1)S(1)} %collective-permute-done.6.refs_0_, bf16[256,4096]{1,0:T(8,128)(2,1)S(1)} %collective-permute-done.11.refs_1_, bf16[4096,1024]{1,0:T(8,128)(2,1)S(1)} %bitcast.4), custom_call_target="tpu_custom_call" | custom-call | flops 1 | bytes 1 | tf_op jit(solution)/shard_map/pallas_call | solution.py:277
  170.7 2.5 collective-permute-done.20.refs_16_
  173.3 1.6 copy-done.4
  174.9 4.4 %shard_map.140.attended_ref = bf16[256,1024]{1,0:T(8,128)(2,1)S(1)} custom-call(s32[4]{0:T(128)S(1)} %fusion.5.order_ref, s32[32]{0:T(128)S(1)} %xor.11.relative_ref, s32[32]{0:T(128)S(1)} %reshape.30.slots_ref, s32[16]{0:T(128)S(1)} %copy-done.12, bf16[256,1024]{1,0:T(8,128)(2,1)S(1)} %shard_map.138.refs_0_, bf16[8,128,1024]{2,1,0:T(8,128)(2,1)S(1)} %copy-done, ...), custom_call_target="tpu_custom_call" | custom-call | flops 1 | bytes 1 | tf_op jit(solution)/shard_map/pallas_call | solution.py:236
  179.8 1.5 collective-permute-start.21
  181.4 4.0 %shard_map.141.part_ref = f32[256,2048]{1,0:T(8,128)S(1)} custom-call(bf16[256,1024]{1,0:T(8,128)(2,1)S(1)} %shard_map.140.attended_ref, bf16[1024,4096]{1,0:T(8,128)(2,1)} %weight_ref.11), custom_call_target="tpu_custom_call" | custom-call | flops 1 | bytes 1 | tf_op jit(solution)/shard_map/pallas_call | solution.py:330
  185.4 3.6 %shard_map.142.attended_ref = bf16[256,1024]{1,0:T(8,128)(2,1)S(1)} custom-call(s32[4]{0:T(128)S(1)} %fusion.5.order_ref, s32[32]{0:T(128)S(1)} %xor.11.relative_ref, s32[32]{0:T(128)S(1)} %reshape.30.slots_ref, s32[16]{0:T(128)S(1)} %copy-done.12, bf16[256,1024]{1,0:T(8,128)(2,1)S(1)} %shard_map.139.refs_0_, bf16[8,128,1024]{2,1,0:T(8,128)(2,1)S(1)} %copy-done, ...), custom_call_target="tpu_custom_call" | custom-call | flops 1 | bytes 1 | tf_op jit(solution)/shard_map/pallas_call | solution.py:236
  189.1 7.0 %collective-permute-done.21.handed_ref = bf16[256,1024]{1,0:T(8,128)(2,1)S(1)} collective-permute-done((bf16[256,1024]{1,0:T(8,128)(2,1)S(1)}, bf16[256,1024]{1,0:T(8,128)(2,1)S(1)}, u32[]{:S(2)}, u32[]{:S(2)}) %collective-permute-start.21) | collective-permute-done | bytes 524320 | tf_op jit(solution)/shard_map/ppermute | solution.py:415
  196.1 4.0 %shard_map.143 = bf16[256,2048]{1,0:T(8,128)(2,1)S(1)} custom-call(s32[1]{0:T(128)} %bitcast.core_ref, f32[256,2048]{1,0:T(8,128)S(1)} %shard_map.141.part_ref, bf16[256,1024]{1,0:T(8,128)(2,1)S(1)} %collective-permute-done.21.handed_ref, bf16[256,4096]{1,0:T(8,128)(2,1)} %copy-done.13, bf16[256,4096]{1,0:T(8,128)(2,1)} %copy-done.14, ...), custom_call_target="tpu_custom_call" | custom-call | flops 1 | bytes 1 | tf_op jit(solution)/shard_map/pallas_call | solution.py:330
  200.1 2.4 collective-permute-start.25
  202.5 1.3 collective-permute-start.24
  203.8 5.4 %shard_map.144 = bf16[256,2048]{1,0:T(8,128)(2,1)S(1)} custom-call(s32[1]{0:T(128)} %bitcast.core_ref, bf16[256,1024]{1,0:T(8,128)(2,1)S(1)} %shard_map.140.attended_ref, bf16[256,1024]{1,0:T(8,128)(2,1)S(1)} %collective-permute-done.21.handed_ref, bf16[1024,4096]{1,0:T(8,128)(2,1)} %weight_ref.11, bf16[256,4096]{1,0:T(8,128)(2,1)} %copy-done.13, ...), custom_call_target="tpu_custom_call" | custom-call | flops 1 | bytes 1 | tf_op jit(solution)/shard_map/pallas_call | solution.py:330
  209.2 3.8 %collective-permute-start.26 = (bf16[256,2048]{1,0:T(8,128)(2,1)S(1)}, bf16[256,2048]{1,0:T(8,128)(2,1)S(1)}, u32[]{:S(2)}, u32[]{:S(2)}) collective-permute-start(bf16[256,2048]{1,0:T(8,128)(2,1)S(1)} %shard_map.144), channel_id=1, source_target_pairs={{1,2},{2,1},{5,6},{6,5},{9,10},{10,9},{13,14},{14,13},{17,18},{18,... | collective-permute-start | bytes 3145736 | tf_op jit(solution)/shard_map/ppermute | solution.py:415
  213.0 4.2 %shard_map.145.attended_ref = bf16[256,1024]{1,0:T(8,128)(2,1)S(1)} custom-call(s32[4]{0:T(128)S(1)} %fusion.5.order_ref, s32[32]{0:T(128)S(1)} %xor.11.relative_ref, s32[32]{0:T(128)S(1)} %reshape.30.slots_ref, s32[16]{0:T(128)S(1)} %copy-done.12, bf16[256,1024]{1,0:T(8,128)(2,1)S(1)} %shard_map.137.refs_0_, bf16[8,128,1024]{2,1,0:T(8,128)(2,1)S(1)} %copy-done, ...), custom_call_target="tpu_custom_call" | custom-call | flops 1 | bytes 1 | tf_op jit(solution)/shard_map/pallas_call | solution.py:236
  217.2 1.6 copy-done.7
  218.8 4.2 %shard_map.146.attended_ref = bf16[256,1024]{1,0:T(8,128)(2,1)S(1)} custom-call(s32[4]{0:T(128)S(1)} %fusion.5.order_ref, s32[32]{0:T(128)S(1)} %xor.11.relative_ref, s32[32]{0:T(128)S(1)} %reshape.30.slots_ref, s32[16]{0:T(128)S(1)} %copy-done.12, bf16[256,1024]{1,0:T(8,128)(2,1)S(1)} %shard_map.136.refs_0_, bf16[8,128,1024]{2,1,0:T(8,128)(2,1)S(1)} %copy-done, ...), custom_call_target="tpu_custom_call" | custom-call | flops 1 | bytes 1 | tf_op jit(solution)/shard_map/pallas_call | solution.py:236
  223.0 11.2 %shard_map.147 = bf16[256,4096]{1,0:T(8,128)(2,1)} custom-call(s32[1]{0:T(128)} %bitcast.core_ref, bf16[256,1024]{1,0:T(8,128)(2,1)S(1)} %shard_map.142.attended_ref, bf16[256,1024]{1,0:T(8,128)(2,1)S(1)} %collective-permute-done.24.handed_ref, bf16[1024,4096]{1,0:T(8,128)(2,1)} %weight_ref.11, bf16[256,4096]{1,0:T(8,128)(2,1)} %copy-done.13, ...), custom_call_target="tpu_custom_call" | custom-call | flops 1 | bytes 1 | tf_op jit(solution)/shard_map/pallas_call | solution.py:330
  234.2 3.9 %shard_map.148 = bf16[256,2048]{1,0:T(8,128)(2,1)S(1)} custom-call(bf16[256,1024]{1,0:T(8,128)(2,1)S(1)} %shard_map.145.attended_ref, bf16[1024,4096]{1,0:T(8,128)(2,1)} %weight_ref.11, bf16[256,2048]{1,0:T(8,128)(2,1)S(1)} %collective-permute-done.25.plus_ref), custom_call_target="tpu_custom_call" | custom-call | flops 1 | bytes 1 | tf_op jit(solution)/shard_map/pallas_call | solution.py:330
  238.1 1.9 collective-permute-start.27
  240.0 3.1 %collective-permute-start.29 = (bf16[256,4096]{1,0:T(8,128)(2,1)}, bf16[256,4096]{1,0:T(8,128)(2,1)}, u32[]{:S(2)}, u32[]{:S(2)}) collective-permute-start(bf16[256,4096]{1,0:T(8,128)(2,1)} %shard_map.147), channel_id=1, source_target_pairs={{1,2},{2,1},{5,6},{6,5},{9,10},{10,9},{13,14},{14,13},{17,18},{18,... | collective-permute-start | bytes 6291464 | tf_op jit(solution)/shard_map/ppermute | solution.py:415
  243.1 1.3 collective-permute-start.28
  244.4 12.1 %collective-permute-done.28.handed_ref = bf16[256,1024]{1,0:T(8,128)(2,1)S(1)} collective-permute-done((bf16[256,1024]{1,0:T(8,128)(2,1)S(1)}, bf16[256,1024]{1,0:T(8,128)(2,1)S(1)}, u32[]{:S(2)}, u32[]{:S(2)}) %collective-permute-start.28) | collective-permute-done | bytes 524320 | tf_op jit(solution)/shard_map/ppermute | solution.py:415
  256.5 0.7 collective-permute-done.27
  257.3 4.3 %shard_map.149 = bf16[256,2048]{1,0:T(8,128)(2,1)S(1)} custom-call(bf16[256,1024]{1,0:T(8,128)(2,1)S(1)} %shard_map.145.attended_ref, bf16[1024,4096]{1,0:T(8,128)(2,1)} %weight_ref.11, bf16[256,2048]{1,0:T(8,128)(2,1)S(1)} %collective-permute-done.26.plus_ref), custom_call_target="tpu_custom_call" | custom-call | flops 1 | bytes 1 | tf_op jit(solution)/shard_map/pallas_call | solution.py:330
  261.6 5.4 %collective-permute-start.30 = (bf16[256,2048]{1,0:T(8,128)(2,1)S(1)}, bf16[256,2048]{1,0:T(8,128)(2,1)}, u32[]{:S(2)}, u32[]{:S(2)}) collective-permute-start(bf16[256,2048]{1,0:T(8,128)(2,1)S(1)} %shard_map.149), channel_id=1, source_target_pairs={{1,0},{2,3},{5,4},{6,7},{9,8},{10,11},{13,12},{14,15},{17,16},{18,... | collective-permute-start | bytes 3145736 | tf_op jit(solution)/shard_map/ppermute | solution.py:415
  267.0 10.3 %shard_map.150 = bf16[256,4096]{1,0:T(8,128)(2,1)S(1)} custom-call(s32[1]{0:T(128)} %bitcast.core_ref, bf16[256,1024]{1,0:T(8,128)(2,1)S(1)} %shard_map.146.attended_ref, bf16[256,1024]{1,0:T(8,128)(2,1)S(1)} %collective-permute-done.28.handed_ref, bf16[1024,4096]{1,0:T(8,128)(2,1)} %weight_ref.11, bf16[256,4096]{1,0:T(8,128)(2,1)} %copy-done.13, ...), custom_call_target="tpu_custom_call" | custom-call | flops 1 | bytes 1 | tf_op jit(solution)/shard_map/pallas_call | solution.py:330
  277.2 16.8 %collective-permute-done.29 = bf16[256,4096]{1,0:T(8,128)(2,1)} collective-permute-done((bf16[256,4096]{1,0:T(8,128)(2,1)}, bf16[256,4096]{1,0:T(8,128)(2,1)}, u32[]{:S(2)}, u32[]{:S(2)}) %collective-permute-start.29) | collective-permute-done | bytes 2097184 | tf_op jit(solution)/shard_map/ppermute | solution.py:415
  294.1 3.7 %add_convert_fusion = bf16[256,4096]{1,0:T(8,128)(2,1)} fusion(bf16[256,4096]{1,0:T(8,128)(2,1)S(1)} %shard_map.150, bf16[256,2048]{1,0:T(8,128)(2,1)S(1)} %shard_map.149, bf16[256,2048]{1,0:T(8,128)(2,1)S(1)} %shard_map.148, bf16[256,4096]{1,0:T(8,128)(2,1)} %collective-permute-done.29, bf16[256,2048]{1,0:T(8,128)(2,1)} %collective-permute-done.30, ...), kind=kLoop, calls=%fused_computation.7 | loop fusion | flops 14680064 | bytes 10485761 | tf_op jit(solution)/shard_map/convert_element_type | solution.py:547
  (79 shorter events, 1.7 us)
Async XLA Ops:
  0.0 2.2 copy-start.15
  0.0 2.9 copy-start.18
  0.0 13.3 %collective-permute-start.2 = (bf16[8,128,1024]{2,1,0:T(8,128)(2,1)}, bf16[8,128,1024]{2,1,0:T(8,128)(2,1)S(1)}, u32[]{:S(2)}, u32[]{:S(2)}) collective-permute-start(bf16[8,128,1024]{2,1,0:T(8,128)(2,1)} %refs_1_.7), channel_id=1, source_target_pairs={{0,4},{4,0},{8,12},{12,8},{16,20},{20,16},{24,28},{28,24},{1,5},{5... | collective-permute-start | bytes 6291464 | tf_op jit(solution)/shard_map/ppermute | solution.py:411
  2.9 7.3 %copy-start = (bf16[8,128,1024]{2,1,0:T(8,128)(2,1)S(1)}, bf16[8,128,1024]{2,1,0:T(8,128)(2,1)}, u32[]{:S(2)}) copy-start(bf16[8,128,1024]{2,1,0:T(8,128)(2,1)} %refs_1_.7) | copy-start | bytes 6291460
  2.9 11.8 %copy-start.20 = (s32[16,2]{0,1:T(2,128)S(1)}, s32[16,2]{0,1:T(2,128)}, u32[]{:S(2)}) copy-start(s32[16,2]{0,1:T(2,128)} %param.20) | copy-start | bytes 388
  3.0 12.0 %copy-start.19 = (s32[16,2]{0,1:T(2,128)S(1)}, s32[16,2]{0,1:T(2,128)}, u32[]{:S(2)}) copy-start(s32[16,2]{0,1:T(2,128)} %param.21) | copy-start | bytes 388
  5.2 48.1 %collective-permute-start = (bf16[256,4096]{1,0:T(8,128)(2,1)}, bf16[256,4096]{1,0:T(8,128)(2,1)}, u32[]{:S(2)}, u32[]{:S(2)}) collective-permute-start(bf16[256,4096]{1,0:T(8,128)(2,1)} %fusion.4.refs_0_), channel_id=1, source_target_pairs={{0,1},{3,2},{1,0},{2,3},{4,5},{7,6},{5,4},{6,7},{8,9},{11,10},{9,8... | collective-permute-start | bytes 6291464 | tf_op jit(solution)/shard_map/ppermute | solution.py:415
  5.2 51.1 %collective-permute-start.1 = (bf16[256,4096]{1,0:T(8,128)(2,1)}, bf16[256,4096]{1,0:T(8,128)(2,1)}, u32[]{:S(2)}, u32[]{:S(2)}) collective-permute-start(bf16[256,4096]{1,0:T(8,128)(2,1)} %fusion.4.refs_0_), channel_id=1, source_target_pairs={{1,2},{2,1},{5,6},{6,5},{9,10},{10,9},{13,14},{14,13},{17,18},{18,... | collective-permute-start | bytes 6291464 | tf_op jit(solution)/shard_map/ppermute | solution.py:415
  10.2 47.4 %collective-permute-start.4 = (bf16[8,128,1024]{2,1,0:T(8,128)(2,1)S(1)}, bf16[8,128,1024]{2,1,0:T(8,128)(2,1)}, u32[]{:S(2)}, u32[]{:S(2)}) collective-permute-start(bf16[8,128,1024]{2,1,0:T(8,128)(2,1)S(1)} %copy-done), channel_id=1, source_target_pairs={{0,8},{4,12},{8,0},{12,4},{16,24},{20,28},{24,16},{28,20},{1,9},{5... | collective-permute-start | bytes 6291464 | tf_op jit(solution)/shard_map/ppermute | solution.py:411
  11.8 47.3 %collective-permute-start.5 = (bf16[8,128,1024]{2,1,0:T(8,128)(2,1)}, bf16[8,128,1024]{2,1,0:T(8,128)(2,1)}, u32[]{:S(2)}, u32[]{:S(2)}) collective-permute-start(bf16[8,128,1024]{2,1,0:T(8,128)(2,1)} %refs_9_.7), channel_id=1, source_target_pairs={{0,16},{4,20},{8,24},{12,28},{16,0},{20,4},{24,8},{28,12},{1,17},{... | collective-permute-start | bytes 6291464 | tf_op jit(solution)/shard_map/ppermute | solution.py:411
  13.3 1.4 copy-start.1
  14.7 44.3 %collective-permute-start.3 = (bf16[8,128,1024]{2,1,0:T(8,128)(2,1)}, bf16[8,128,1024]{2,1,0:T(8,128)(2,1)}, u32[]{:S(2)}, u32[]{:S(2)}) collective-permute-start(bf16[8,128,1024]{2,1,0:T(8,128)(2,1)} %refs_9_.7), channel_id=1, source_target_pairs={{0,4},{4,0},{8,12},{12,8},{16,20},{20,16},{24,28},{28,24},{1,5},{5... | collective-permute-start | bytes 6291464 | tf_op jit(solution)/shard_map/ppermute | solution.py:411
  15.8 52.3 %copy-start.22 = (s32[4]{0:T(128)S(1)}, s32[4]{0:T(128)}, u32[]{:S(2)}) copy-start(s32[4]{0:T(128)} %constant.62.clone) | copy-start | bytes 52
  15.8 52.9 %copy-start.21 = (s32[4]{0:T(128)S(1)}, s32[4]{0:T(128)}, u32[]{:S(2)}) copy-start(s32[4]{0:T(128)} %constant.63.clone) | copy-start | bytes 52
  59.1 47.9 %collective-permute-start.10 = (bf16[256,4096]{1,0:T(8,128)(2,1)S(1)}, bf16[256,4096]{1,0:T(8,128)(2,1)S(1)}, u32[]{:S(2)}, u32[]{:S(2)}) collective-permute-start(bf16[256,4096]{1,0:T(8,128)(2,1)S(1)} %get-tuple-element.77), channel_id=1, source_target_pairs={{0,1},{3,2},{4,5},{7,6},{8,9},{11,10},{12,13},{15,14},{16,17},{19,... | collective-permute-start | bytes 6291464 | tf_op jit(solution)/shard_map/ppermute | solution.py:415
  60.4 48.1 %collective-permute-start.6 = (bf16[256,4096]{1,0:T(8,128)(2,1)}, bf16[256,4096]{1,0:T(8,128)(2,1)S(1)}, u32[]{:S(2)}, u32[]{:S(2)}) collective-permute-start(bf16[256,4096]{1,0:T(8,128)(2,1)} %collective-permute-done.refs_1_), channel_id=1, source_target_pairs={{1,2},{2,1},{5,6},{6,5},{9,10},{10,9},{13,14},{14,13},{17,18},{18,... | collective-permute-start | bytes 6291464 | tf_op jit(solution)/shard_map/ppermute | solution.py:415
  62.6 46.8 %collective-permute-start.7 = (bf16[256,4096]{1,0:T(8,128)(2,1)}, bf16[256,4096]{1,0:T(8,128)(2,1)S(1)}, u32[]{:S(2)}, u32[]{:S(2)}) collective-permute-start(bf16[256,4096]{1,0:T(8,128)(2,1)} %collective-permute-done.1.refs_1_), channel_id=1, source_target_pairs={{1,0},{2,3},{5,4},{6,7},{9,8},{10,11},{13,12},{14,15},{17,16},{18,... | collective-permute-start | bytes 6291464 | tf_op jit(solution)/shard_map/ppermute | solution.py:415
  66.0 45.5 %collective-permute-start.8 = (bf16[8,128,1024]{2,1,0:T(8,128)(2,1)S(1)}, bf16[8,128,1024]{2,1,0:T(8,128)(2,1)S(1)}, u32[]{:S(2)}, u32[]{:S(2)}) collective-permute-start(bf16[8,128,1024]{2,1,0:T(8,128)(2,1)S(1)} %copy-done), channel_id=1, source_target_pairs={{0,16},{4,20},{8,24},{12,28},{16,0},{20,4},{24,8},{28,12},{1,17},{... | collective-permute-start | bytes 6291464 | tf_op jit(solution)/shard_map/ppermute | solution.py:411
  67.6 45.4 %collective-permute-start.9 = (bf16[8,128,1024]{2,1,0:T(8,128)(2,1)}, bf16[8,128,1024]{2,1,0:T(8,128)(2,1)S(1)}, u32[]{:S(2)}, u32[]{:S(2)}) collective-permute-start(bf16[8,128,1024]{2,1,0:T(8,128)(2,1)} %refs_9_.7), channel_id=1, source_target_pairs={{0,8},{4,12},{8,0},{12,4},{16,24},{20,28},{24,16},{28,20},{1,9},{5... | collective-permute-start | bytes 6291464 | tf_op jit(solution)/shard_map/ppermute | solution.py:411
  69.4 96.4 %slice-start = ((s8[8388608]{0:T(1024)(128)(4,1)}), s8[4194304]{0:T(1024)(128)(4,1)S(1)}, s32[]{:S(2)}) async-start(s8[8388608]{0:T(1024)(128)(4,1)} %bitcast.3), calls=%async_computation | async-start | bytes 8388608
  77.6 88.1 %slice-start.1 = ((s8[8388608]{0:T(1024)(128)(4,1)}), s8[4194304]{0:T(1024)(128)(4,1)S(1)}, s32[]{:S(2)}) async-start(s8[8388608]{0:T(1024)(128)(4,1)} %bitcast.3), calls=%async_computation.1 | async-start | bytes 8388608
  107.0 72.2 %copy-start.13 = (bf16[256,4096]{1,0:T(8,128)(2,1)}, bf16[256,4096]{1,0:T(8,128)(2,1)S(1)}, u32[]{:S(2)}) copy-start(bf16[256,4096]{1,0:T(8,128)(2,1)S(1)} %collective-permute-done.10.refs_0_) | copy-start | bytes 6291460
  113.0 12.3 %collective-permute-start.15 = (bf16[8,128,1024]{2,1,0:T(8,128)(2,1)}, bf16[8,128,1024]{2,1,0:T(8,128)(2,1)S(1)}, u32[]{:S(2)}, u32[]{:S(2)}) collective-permute-start(bf16[8,128,1024]{2,1,0:T(8,128)(2,1)} %collective-permute-done.4.refs_3_), channel_id=1, source_target_pairs={{0,4},{4,0},{8,12},{12,8},{16,20},{20,16},{24,28},{28,24},{1,5},{5... | collective-permute-start | bytes 6291464 | tf_op jit(solution)/shard_map/ppermute | solution.py:411
  113.0 47.1 %collective-permute-start.11 = (bf16[256,4096]{1,0:T(8,128)(2,1)S(1)}, bf16[256,4096]{1,0:T(8,128)(2,1)S(1)}, u32[]{:S(2)}, u32[]{:S(2)}) collective-permute-start(bf16[256,4096]{1,0:T(8,128)(2,1)S(1)} %collective-permute-done.6.refs_0_), channel_id=1, source_target_pairs={{1,0},{2,3},{5,4},{6,7},{9,8},{10,11},{13,12},{14,15},{17,16},{18,... | collective-permute-start | bytes 6291464 | tf_op jit(solution)/shard_map/ppermute | solution.py:415
  114.6 48.2 %collective-permute-start.12 = (bf16[8,128,1024]{2,1,0:T(8,128)(2,1)}, bf16[8,128,1024]{2,1,0:T(8,128)(2,1)S(1)}, u32[]{:S(2)}, u32[]{:S(2)}) collective-permute-start(bf16[8,128,1024]{2,1,0:T(8,128)(2,1)} %collective-permute-done.4.refs_3_), channel_id=1, source_target_pairs={{0,16},{4,20},{8,24},{12,28},{16,0},{20,4},{24,8},{28,12},{1,17},{... | collective-permute-start | bytes 6291464 | tf_op jit(solution)/shard_map/ppermute | solution.py:411
  115.5 47.7 %collective-permute-start.13 = (bf16[8,128,1024]{2,1,0:T(8,128)(2,1)}, bf16[8,128,1024]{2,1,0:T(8,128)(2,1)S(1)}, u32[]{:S(2)}, u32[]{:S(2)}) collective-permute-start(bf16[8,128,1024]{2,1,0:T(8,128)(2,1)} %collective-permute-done.5.refs_13_), channel_id=1, source_target_pairs={{0,8},{4,12},{8,0},{12,4},{16,24},{20,28},{24,16},{28,20},{1,9},{5... | collective-permute-start | bytes 6291464 | tf_op jit(solution)/shard_map/ppermute | solution.py:411
  116.0 49.3 %collective-permute-start.14 = (bf16[256,4096]{1,0:T(8,128)(2,1)}, bf16[256,4096]{1,0:T(8,128)(2,1)S(1)}, u32[]{:S(2)}, u32[]{:S(2)}) collective-permute-start(bf16[256,4096]{1,0:T(8,128)(2,1)} %get-tuple-element.83), channel_id=1, source_target_pairs={{0,1},{3,2},{4,5},{7,6},{8,9},{11,10},{12,13},{15,14},{16,17},{19,... | collective-permute-start | bytes 6291464 | tf_op jit(solution)/shard_map/ppermute | solution.py:415
  125.3 48.0 %copy-start.2 = (bf16[8,128,1024]{2,1,0:T(8,128)(2,1)S(1)}, bf16[8,128,1024]{2,1,0:T(8,128)(2,1)}, u32[]{:S(2)}) copy-start(bf16[8,128,1024]{2,1,0:T(8,128)(2,1)} %copy-done.1) | copy-start | bytes 6291460
  125.3 48.0 %copy-start.12 = (s32[16]{0:T(128)S(1)}, s32[16]{0:T(128)}, u32[]{:S(2)}) copy-start(s32[16]{0:T(128)} %counts_ref.7) | copy-start | bytes 196
  125.3 45.3 %collective-permute-start.19 = (bf16[8,128,1024]{2,1,0:T(8,128)(2,1)}, bf16[8,128,1024]{2,1,0:T(8,128)(2,1)S(1)}, u32[]{:S(2)}, u32[]{:S(2)}) collective-permute-start(bf16[8,128,1024]{2,1,0:T(8,128)(2,1)} %collective-permute-done.5.refs_13_), channel_id=1, source_target_pairs={{0,4},{4,0},{8,12},{12,8},{16,20},{20,16},{24,28},{28,24},{1,5},{5... | collective-permute-start | bytes 6291464 | tf_op jit(solution)/shard_map/ppermute | solution.py:411
  160.1 10.6 %collective-permute-start.16 = (bf16[8,128,1024]{2,1,0:T(8,128)(2,1)S(1)}, bf16[8,128,1024]{2,1,0:T(8,128)(2,1)S(1)}, u32[]{:S(2)}, u32[]{:S(2)}) collective-permute-start(bf16[8,128,1024]{2,1,0:T(8,128)(2,1)S(1)} %collective-permute-done.8.refs_5_), channel_id=1, source_target_pairs={{0,4},{4,0},{8,12},{12,8},{16,20},{20,16},{24,28},{28,24},{1,5},{5... | collective-permute-start | bytes 6291464 | tf_op jit(solution)/shard_map/ppermute | solution.py:411
  162.7 8.0 %collective-permute-start.18 = (bf16[8,128,1024]{2,1,0:T(8,128)(2,1)S(1)}, bf16[8,128,1024]{2,1,0:T(8,128)(2,1)S(1)}, u32[]{:S(2)}, u32[]{:S(2)}) collective-permute-start(bf16[8,128,1024]{2,1,0:T(8,128)(2,1)S(1)} %collective-permute-done.9.refs_11_), channel_id=1, source_target_pairs={{0,4},{4,0},{8,12},{12,8},{16,20},{20,16},{24,28},{28,24},{1,5},{5... | collective-permute-start | bytes 6291464 | tf_op jit(solution)/shard_map/ppermute | solution.py:411
  163.1 7.5 %copy-start.3 = (bf16[8,128,1024]{2,1,0:T(8,128)(2,1)}, bf16[8,128,1024]{2,1,0:T(8,128)(2,1)S(1)}, u32[]{:S(2)}) copy-start(bf16[8,128,1024]{2,1,0:T(8,128)(2,1)S(1)} %collective-permute-done.13.refs_15_) | copy-start | bytes 6291460
  165.3 14.2 %copy-start.14 = (bf16[256,4096]{1,0:T(8,128)(2,1)}, bf16[256,4096]{1,0:T(8,128)(2,1)S(1)}, u32[]{:S(2)}) copy-start(bf16[256,4096]{1,0:T(8,128)(2,1)S(1)} %collective-permute-done.14.refs_1_) | copy-start | bytes 6291460
  165.3 5.4 %collective-permute-start.17 = (bf16[8,128,1024]{2,1,0:T(8,128)(2,1)S(1)}, bf16[8,128,1024]{2,1,0:T(8,128)(2,1)S(1)}, u32[]{:S(2)}, u32[]{:S(2)}) collective-permute-start(bf16[8,128,1024]{2,1,0:T(8,128)(2,1)S(1)} %collective-permute-done.12.refs_7_), channel_id=1, source_target_pairs={{0,4},{4,0},{8,12},{12,8},{16,20},{20,16},{24,28},{28,24},{1,5},{5... | collective-permute-start | bytes 6291464 | tf_op jit(solution)/shard_map/ppermute | solution.py:411
  165.3 8.0 %collective-permute-start.20 = (bf16[8,128,1024]{2,1,0:T(8,128)(2,1)S(1)}, bf16[8,128,1024]{2,1,0:T(8,128)(2,1)S(1)}, u32[]{:S(2)}, u32[]{:S(2)}) collective-permute-start(bf16[8,128,1024]{2,1,0:T(8,128)(2,1)S(1)} %collective-permute-done.13.refs_15_), channel_id=1, source_target_pairs={{0,4},{4,0},{8,12},{12,8},{16,20},{20,16},{24,28},{28,24},{1,5},{5... | collective-permute-start | bytes 6291464 | tf_op jit(solution)/shard_map/ppermute | solution.py:411
  170.7 42.4 %copy-start.6 = (bf16[8,128,1024]{2,1,0:T(8,128)(2,1)}, bf16[8,128,1024]{2,1,0:T(8,128)(2,1)S(1)}, u32[]{:S(2)}) copy-start(bf16[8,128,1024]{2,1,0:T(8,128)(2,1)S(1)} %collective-permute-done.16.refs_6_) | copy-start | bytes 6291460
  170.7 8.6 %copy-start.8 = (bf16[8,128,1024]{2,1,0:T(8,128)(2,1)}, bf16[8,128,1024]{2,1,0:T(8,128)(2,1)S(1)}, u32[]{:S(2)}) copy-start(bf16[8,128,1024]{2,1,0:T(8,128)(2,1)S(1)} %collective-permute-done.18.refs_12_) | copy-start | bytes 6291460
  173.3 1.6 copy-start.4
  174.9 4.4 %copy-start.10 = (bf16[8,128,1024]{2,1,0:T(8,128)(2,1)}, bf16[8,128,1024]{2,1,0:T(8,128)(2,1)S(1)}, u32[]{:S(2)}) copy-start(bf16[8,128,1024]{2,1,0:T(8,128)(2,1)S(1)} %collective-permute-done.20.refs_16_) | copy-start | bytes 6291460
  179.3 16.8 %collective-permute-start.22 = (bf16[256,4096]{1,0:T(8,128)(2,1)S(1)}, bf16[256,4096]{1,0:T(8,128)(2,1)}, u32[]{:S(2)}, u32[]{:S(2)}) collective-permute-start(bf16[256,4096]{1,0:T(8,128)(2,1)S(1)} %collective-permute-done.10.refs_0_), channel_id=1, source_target_pairs={{0,4},{4,0},{8,12},{12,8},{16,20},{20,16},{24,28},{28,24},{1,5},{5... | collective-permute-start | bytes 6291464 | tf_op jit(solution)/shard_map/ppermute | solution.py:411
  179.5 5.9 %copy-start.9 = (bf16[8,128,1024]{2,1,0:T(8,128)(2,1)S(1)}, bf16[8,128,1024]{2,1,0:T(8,128)(2,1)}, u32[]{:S(2)}) copy-start(bf16[8,128,1024]{2,1,0:T(8,128)(2,1)} %copy-done.8) | copy-start | bytes 6291460
  179.5 5.9 %copy-start.11 = (bf16[8,128,1024]{2,1,0:T(8,128)(2,1)S(1)}, bf16[8,128,1024]{2,1,0:T(8,128)(2,1)}, u32[]{:S(2)}) copy-start(bf16[8,128,1024]{2,1,0:T(8,128)(2,1)} %copy-done.10) | copy-start | bytes 6291460
  179.5 16.6 %collective-permute-start.23 = (bf16[256,4096]{1,0:T(8,128)(2,1)S(1)}, bf16[256,4096]{1,0:T(8,128)(2,1)}, u32[]{:S(2)}, u32[]{:S(2)}) collective-permute-start(bf16[256,4096]{1,0:T(8,128)(2,1)S(1)} %collective-permute-done.14.refs_1_), channel_id=1, source_target_pairs={{0,4},{4,0},{8,12},{12,8},{16,20},{20,16},{24,28},{28,24},{1,5},{5... | collective-permute-start | bytes 6291464 | tf_op jit(solution)/shard_map/ppermute | solution.py:411
  179.8 16.3 %collective-permute-start.21 = (bf16[256,1024]{1,0:T(8,128)(2,1)S(1)}, bf16[256,1024]{1,0:T(8,128)(2,1)S(1)}, u32[]{:S(2)}, u32[]{:S(2)}) collective-permute-start(bf16[256,1024]{1,0:T(8,128)(2,1)S(1)} %shard_map.140.attended_ref), channel_id=1, source_target_pairs={{0,1},{3,2},{4,5},{7,6},{8,9},{11,10},{12,13},{15,14},{16,17},{19,... | collective-permute-start | bytes 1572872 | tf_op jit(solution)/shard_map/ppermute | solution.py:415
  200.1 34.1 %collective-permute-start.25 = (bf16[256,2048]{1,0:T(8,128)(2,1)S(1)}, bf16[256,2048]{1,0:T(8,128)(2,1)S(1)}, u32[]{:S(2)}, u32[]{:S(2)}) collective-permute-start(bf16[256,2048]{1,0:T(8,128)(2,1)S(1)} %shard_map.143), channel_id=1, source_target_pairs={{1,2},{2,1},{5,6},{6,5},{9,10},{10,9},{13,14},{14,13},{17,18},{18,... | collective-permute-start | bytes 3145736 | tf_op jit(solution)/shard_map/ppermute | solution.py:415
  202.5 20.5 %collective-permute-start.24 = (bf16[256,1024]{1,0:T(8,128)(2,1)S(1)}, bf16[256,1024]{1,0:T(8,128)(2,1)S(1)}, u32[]{:S(2)}, u32[]{:S(2)}) collective-permute-start(bf16[256,1024]{1,0:T(8,128)(2,1)S(1)} %shard_map.142.attended_ref), channel_id=1, source_target_pairs={{0,1},{3,2},{4,5},{7,6},{8,9},{11,10},{12,13},{15,14},{16,17},{19,... | collective-permute-start | bytes 1572872 | tf_op jit(solution)/shard_map/ppermute | solution.py:415
  209.2 8.0 %copy-start.5 = (bf16[8,128,1024]{2,1,0:T(8,128)(2,1)S(1)}, bf16[8,128,1024]{2,1,0:T(8,128)(2,1)}, u32[]{:S(2)}) copy-start(bf16[8,128,1024]{2,1,0:T(8,128)(2,1)} %copy-done.3) | copy-start | bytes 6291460
  209.2 47.3 %collective-permute-start.26 = (bf16[256,2048]{1,0:T(8,128)(2,1)S(1)}, bf16[256,2048]{1,0:T(8,128)(2,1)S(1)}, u32[]{:S(2)}, u32[]{:S(2)}) collective-permute-start(bf16[256,2048]{1,0:T(8,128)(2,1)S(1)} %shard_map.144), channel_id=1, source_target_pairs={{1,2},{2,1},{5,6},{6,5},{9,10},{10,9},{13,14},{14,13},{17,18},{18,... | collective-permute-start | bytes 3145736 | tf_op jit(solution)/shard_map/ppermute | solution.py:415
  217.2 1.6 copy-start.7
  238.1 19.1 %collective-permute-start.27 = (bf16[256,2048]{1,0:T(8,128)(2,1)S(1)}, bf16[256,2048]{1,0:T(8,128)(2,1)S(1)}, u32[]{:S(2)}, u32[]{:S(2)}) collective-permute-start(bf16[256,2048]{1,0:T(8,128)(2,1)S(1)} %shard_map.148), channel_id=1, source_target_pairs={{1,0},{2,3},{5,4},{6,7},{9,8},{10,11},{13,12},{14,15},{17,16},{18,... | collective-permute-start | bytes 3145736 | tf_op jit(solution)/shard_map/ppermute | solution.py:415
  240.0 54.0 %collective-permute-start.29 = (bf16[256,4096]{1,0:T(8,128)(2,1)}, bf16[256,4096]{1,0:T(8,128)(2,1)}, u32[]{:S(2)}, u32[]{:S(2)}) collective-permute-start(bf16[256,4096]{1,0:T(8,128)(2,1)} %shard_map.147), channel_id=1, source_target_pairs={{1,2},{2,1},{5,6},{6,5},{9,10},{10,9},{13,14},{14,13},{17,18},{18,... | collective-permute-start | bytes 6291464 | tf_op jit(solution)/shard_map/ppermute | solution.py:415
  243.1 13.4 %collective-permute-start.28 = (bf16[256,1024]{1,0:T(8,128)(2,1)S(1)}, bf16[256,1024]{1,0:T(8,128)(2,1)S(1)}, u32[]{:S(2)}, u32[]{:S(2)}) collective-permute-start(bf16[256,1024]{1,0:T(8,128)(2,1)S(1)} %shard_map.146.attended_ref), channel_id=1, source_target_pairs={{0,1},{3,2},{4,5},{7,6},{8,9},{11,10},{12,13},{15,14},{16,17},{19,... | collective-permute-start | bytes 1572872 | tf_op jit(solution)/shard_map/ppermute | solution.py:415
  257.3 4.3 %copy-start.16 = (bf16[256,2048]{1,0:T(8,128)(2,1)}, bf16[256,2048]{1,0:T(8,128)(2,1)S(1)}, u32[]{:S(2)}) copy-start(bf16[256,2048]{1,0:T(8,128)(2,1)S(1)} %collective-permute-done.27) | copy-start | bytes 3145732
  261.6 32.5 %collective-permute-start.30 = (bf16[256,2048]{1,0:T(8,128)(2,1)S(1)}, bf16[256,2048]{1,0:T(8,128)(2,1)}, u32[]{:S(2)}, u32[]{:S(2)}) collective-permute-start(bf16[256,2048]{1,0:T(8,128)(2,1)S(1)} %shard_map.149), channel_id=1, source_target_pairs={{1,0},{2,3},{5,4},{6,7},{9,8},{10,11},{13,12},{14,15},{17,16},{18,... | collective-permute-start | bytes 3145736 | tf_op jit(solution)/shard_map/ppermute | solution.py:415
  267.0 27.1 %copy-start.17 = (bf16[256,2048]{1,0:T(8,128)(2,1)S(1)}, bf16[256,2048]{1,0:T(8,128)(2,1)}, u32[]{:S(2)}) copy-start(bf16[256,2048]{1,0:T(8,128)(2,1)} %copy-done.16) | copy-start | bytes 3145732

commit v4 on v3

--- a/solution.py
+++ b/solution.py
@@ -527,13 +527,15 @@
     fourth, third_queries = together((fourth, third_queries))
     third = attend(2, third_queries)
     third_in = along(third, INWARD)
-    _, second, second_in = together((third, second, second_in))
+    _, fourth, across_left = together((third, fourth, across_left))
+    left = output_plus(fourth, output_weight, across_left, 0, tiles // 2)
+    outward_left = along(left, OUTWARD)
+    _, second, second_in = together((left, second, second_in))
     second = output(second, second_in, 0, tiles)
     second_across = along(second, MIDDLE)
-    _, fourth, across_left = together((second, fourth, across_left))
-    left = output_plus(fourth, output_weight, across_left, 0, tiles // 2)
-    outward_left = along(left, OUTWARD)
-    fourth, across_right, outward_left, third_in = together((fourth, across_right, outward_left, third_in))
+    _, fourth, across_right, outward_left, third_in = together(
+        (second, fourth, across_right, outward_left, third_in)
+    )
     right = output_plus(fourth, output_weight, across_right, tiles // 2, tiles // 2)
     outward_right = along(right, OUTWARD)
     _, third, third_in = together((right, third, third_in))

time: 299 us -> 299 us (level)
  waiting for transfers between devices: 145 us -> 153 us
  starting transfers between devices: 43.2 us -> 38.5 us
  Pallas kernels: 88.9 us -> 85.9 us
    ppermute x15, waiting for transfers between devices: 134 us -> 142 us  [along(): return lax.ppermute(values, 'mp', list(pairs))]
    ppermute x15, starting transfers between devices: 35.4 us -> 30.7 us  [along(): return lax.ppermute(values, 'mp', list(pairs))]
    pallas_call x4, Pallas kernels: 16.4 us -> 13.3 us  [shard_attention(): pl.pallas_call(functools.partial(attention_kernel, step, blocks), out_sha...]
  transfers between devices with their start and end apart: 31 -> 31, of which waited for: 18 -> 18; matrix products, arithmetic and copies ran while one was open for 4% -> 4% of each run, Pallas kernels for 27% -> 26%
where the time goes in v4:
time: 299 us; the launch traced here: 298 us
  waiting for transfers between devices  153 us (51%)
  Pallas kernels  85.9 us (29%)
  starting transfers between devices  38.5 us (13%)
  local copies, waits for them, and re-layouts  11 us (4%)
  other arithmetic  8.69 us (3%)
    ppermute x15, waiting for transfers between devices, along(): return lax.ppermute(values, 'mp', list(pairs))  142 us
    pallas_call x7, Pallas kernels, output_call(): pl.pallas_call(kernel, out_shape=jax.ShapeDtypeStruct((rows, count * 512)...  43.1 us
    ppermute x15, starting transfers between devices, along(): return lax.ppermute(values, 'mp', list(pairs))  30.7 us
    pallas_call x4, Pallas kernels, project(): pl.pallas_call(functools.partial(project_kernel, 1.0 / math.sqrt(HD)), ou...  29.4 us
    pallas_call x4, Pallas kernels, shard_attention(): pl.pallas_call(functools.partial(attention_kernel, step, blocks), out_sha...  13.3 us
    ppermute x16, waiting for transfers between devices, swap(): return lax.ppermute(values, 'dp', [(i, i ^ bits) for i in range(8)])  11.9 us
    ppermute x16, starting transfers between devices, swap(): return lax.ppermute(values, 'dp', [(i, i ^ bits) for i in range(8)])  7.76 us
  transfers between devices with their start and end apart: 31, of which 18 were waited for; matrix products, arithmetic and copies ran while one was open for 4% of the time, Pallas kernels for 26%

profile of v4, /device:TPU:8, one launch (start us, length us, event | category | flops | bytes accessed | tf_op | source)
XLA Modules:
  0.0 298.1 jit_solution(7138047958424321831)
XLA Ops:
  0.0 2.1 convert_reduce_fusion
  2.2 0.7 fusion.2
  3.0 2.2 fusion.4.refs_0_
  5.2 5.0 %collective-permute-start.1 = (bf16[256,4096]{1,0:T(8,128)(2,1)}, bf16[256,4096]{1,0:T(8,128)(2,1)}, u32[]{:S(2)}, u32[]{:S(2)}) collective-permute-start(bf16[256,4096]{1,0:T(8,128)(2,1)} %fusion.4.refs_0_), channel_id=1, source_target_pairs={{1,2},{2,1},{5,6},{6,5},{9,10},{10,9},{13,14},{14,13},{17,18},{18,... | collective-permute-start | bytes 6291464 | tf_op jit(solution)/shard_map/ppermute | solution.py:415
  10.2 1.6 collective-permute-start.4
  11.8 1.5 collective-permute-start.5
  13.3 1.4 copy-done.1
  15.1 0.7 fusion.5.order_ref
  15.8 4.0 %constant_dynamic-slice_fusion.1 = (bf16[256,4096]{1,0:T(8,128)(2,1)}, bf16[256,4096]{1,0:T(8,128)(2,1)S(1)}) fusion(bf16[1024,4096]{1,0:T(8,128)(2,1)} %weight_ref.11, s32[]{:T(128)S(6)} %select_n.37, s32[]{:T(128)S(6)} %select_n.36), kind=kLoop, calls=%fused_computation.12 | loop fusion | bytes 8388616 | tf_op jit(solution)/shard_map/dynamic_slice | solution.py:444
  19.8 33.5 %collective-permute-done.refs_1_ = bf16[256,4096]{1,0:T(8,128)(2,1)} collective-permute-done((bf16[256,4096]{1,0:T(8,128)(2,1)}, bf16[256,4096]{1,0:T(8,128)(2,1)}, u32[]{:S(2)}, u32[]{:S(2)}) %collective-permute-start) | collective-permute-done | bytes 2097184 | tf_op jit(solution)/shard_map/ppermute | solution.py:415
  53.3 3.0 %collective-permute-done.1.refs_1_ = bf16[256,4096]{1,0:T(8,128)(2,1)} collective-permute-done((bf16[256,4096]{1,0:T(8,128)(2,1)}, bf16[256,4096]{1,0:T(8,128)(2,1)}, u32[]{:S(2)}, u32[]{:S(2)}) %collective-permute-start.1) | collective-permute-done | bytes 2097184 | tf_op jit(solution)/shard_map/ppermute | solution.py:415
  56.3 1.3 collective-permute-done.4.refs_3_
  57.7 1.4 collective-permute-done.5.refs_13_
  59.1 1.3 collective-permute-start.10
  60.4 2.2 collective-permute-start.6
  62.6 3.4 %collective-permute-start.7 = (bf16[256,4096]{1,0:T(8,128)(2,1)}, bf16[256,4096]{1,0:T(8,128)(2,1)S(1)}, u32[]{:S(2)}, u32[]{:S(2)}) collective-permute-start(bf16[256,4096]{1,0:T(8,128)(2,1)} %collective-permute-done.1.refs_1_), channel_id=1, source_target_pairs={{1,0},{2,3},{5,4},{6,7},{9,8},{10,11},{13,12},{14,15},{17,16},{18,... | collective-permute-start | bytes 6291464 | tf_op jit(solution)/shard_map/ppermute | solution.py:415
  66.0 1.6 collective-permute-start.8
  67.6 0.5 collective-permute-start.9
  68.1 0.6 dynamic_slice.26.which_ref
  68.7 0.7 dynamic_slice.28.which_ref
  69.4 8.3 %shard_map.136.refs_0_ = bf16[256,1024]{1,0:T(8,128)(2,1)S(1)} custom-call(s32[1]{0:T(128)} %dynamic_slice.26.which_ref, bf16[256,4096]{1,0:T(8,128)(2,1)} %fusion.4.refs_0_, bf16[256,4096]{1,0:T(8,128)(2,1)} %collective-permute-done.refs_1_, bf16[4096,1024]{1,0:T(8,128)(2,1)} %refs_2_.7), custom_call_target="tpu_custom_call" | custom-call | flops 1 | bytes 1 | tf_op jit(solution)/shard_map/pallas_call | solution.py:277
  77.7 8.3 %shard_map.137.refs_0_ = bf16[256,1024]{1,0:T(8,128)(2,1)S(1)} custom-call(s32[1]{0:T(128)} %dynamic_slice.28.which_ref, bf16[256,4096]{1,0:T(8,128)(2,1)} %fusion.4.refs_0_, bf16[256,4096]{1,0:T(8,128)(2,1)} %collective-permute-done.refs_1_, bf16[4096,1024]{1,0:T(8,128)(2,1)} %refs_2_.7), custom_call_target="tpu_custom_call" | custom-call | flops 1 | bytes 1 | tf_op jit(solution)/shard_map/pallas_call | solution.py:277
  86.0 21.0 %collective-permute-done.10.refs_0_ = bf16[256,4096]{1,0:T(8,128)(2,1)S(1)} collective-permute-done((bf16[256,4096]{1,0:T(8,128)(2,1)S(1)}, bf16[256,4096]{1,0:T(8,128)(2,1)S(1)}, u32[]{:S(2)}, u32[]{:S(2)}) %collective-permute-start.10) | collective-permute-done | bytes 2097184 | tf_op jit(solution)/shard_map/ppermute | solution.py:415
  107.0 1.5 collective-permute-done.6.refs_0_
  108.5 0.9 collective-permute-done.7.refs_0_
  109.4 2.1 collective-permute-done.8.refs_5_
  111.5 1.4 collective-permute-done.9.refs_11_
  113.0 1.6 collective-permute-start.11
  114.6 0.9 collective-permute-start.12
  115.5 0.5 collective-permute-start.13
  116.0 1.3 collective-permute-start.14
  117.3 8.0 %shard_map.139.refs_0_ = bf16[256,1024]{1,0:T(8,128)(2,1)S(1)} custom-call(s32[1]{0:T(128)} %dynamic_slice.28.which_ref, bf16[256,4096]{1,0:T(8,128)(2,1)S(1)} %collective-permute-done.7.refs_0_, bf16[256,4096]{1,0:T(8,128)(2,1)} %collective-permute-done.1.refs_1_, bf16[4096,1024]{1,0:T(8,128)(2,1)} %refs_2_.7), custom_call_target="tpu_custom_call" | custom-call | flops 1 | bytes 1 | tf_op jit(solution)/shard_map/pallas_call | solution.py:277
  125.4 34.7 %collective-permute-done.11.refs_1_ = bf16[256,4096]{1,0:T(8,128)(2,1)S(1)} collective-permute-done((bf16[256,4096]{1,0:T(8,128)(2,1)S(1)}, bf16[256,4096]{1,0:T(8,128)(2,1)S(1)}, u32[]{:S(2)}, u32[]{:S(2)}) %collective-permute-start.11) | collective-permute-done | bytes 2097184 | tf_op jit(solution)/shard_map/ppermute | solution.py:415
  160.1 2.6 collective-permute-done.12.refs_7_
  163.1 2.1 collective-permute-done.14.refs_1_
  165.3 0.5 collective-permute-start.20
  165.8 4.8 %shard_map.138.refs_0_ = bf16[256,1024]{1,0:T(8,128)(2,1)S(1)} custom-call(s32[1]{0:T(128)} %dynamic_slice.26.which_ref, bf16[256,4096]{1,0:T(8,128)(2,1)S(1)} %collective-permute-done.6.refs_0_, bf16[256,4096]{1,0:T(8,128)(2,1)S(1)} %collective-permute-done.11.refs_1_, bf16[4096,1024]{1,0:T(8,128)(2,1)S(1)} %bitcast.4), custom_call_target="tpu_custom_call" | custom-call | flops 1 | bytes 1 | tf_op jit(solution)/shard_map/pallas_call | solution.py:277
  170.7 2.5 collective-permute-done.20.refs_16_
  173.3 1.6 copy-done.4
  174.9 4.8 %shard_map.140.attended_ref = bf16[256,1024]{1,0:T(8,128)(2,1)S(1)} custom-call(s32[4]{0:T(128)S(1)} %fusion.5.order_ref, s32[32]{0:T(128)S(1)} %xor.11.relative_ref, s32[32]{0:T(128)S(1)} %reshape.30.slots_ref, s32[16]{0:T(128)S(1)} %copy-done.12, bf16[256,1024]{1,0:T(8,128)(2,1)S(1)} %shard_map.138.refs_0_, bf16[8,128,1024]{2,1,0:T(8,128)(2,1)S(1)} %copy-done, ...), custom_call_target="tpu_custom_call" | custom-call | flops 1 | bytes 1 | tf_op jit(solution)/shard_map/pallas_call | solution.py:236
  180.3 1.5 collective-permute-start.21
  181.9 4.0 %shard_map.141.part_ref = f32[256,2048]{1,0:T(8,128)S(1)} custom-call(bf16[256,1024]{1,0:T(8,128)(2,1)S(1)} %shard_map.140.attended_ref, bf16[1024,4096]{1,0:T(8,128)(2,1)} %weight_ref.11), custom_call_target="tpu_custom_call" | custom-call | flops 1 | bytes 1 | tf_op jit(solution)/shard_map/pallas_call | solution.py:330
  185.9 4.2 %shard_map.142.attended_ref = bf16[256,1024]{1,0:T(8,128)(2,1)S(1)} custom-call(s32[4]{0:T(128)S(1)} %fusion.5.order_ref, s32[32]{0:T(128)S(1)} %xor.11.relative_ref, s32[32]{0:T(128)S(1)} %reshape.30.slots_ref, s32[16]{0:T(128)S(1)} %copy-done.12, bf16[256,1024]{1,0:T(8,128)(2,1)S(1)} %shard_map.139.refs_0_, bf16[8,128,1024]{2,1,0:T(8,128)(2,1)S(1)} %copy-done, ...), custom_call_target="tpu_custom_call" | custom-call | flops 1 | bytes 1 | tf_op jit(solution)/shard_map/pallas_call | solution.py:236
  190.1 6.5 %collective-permute-done.21.handed_ref = bf16[256,1024]{1,0:T(8,128)(2,1)S(1)} collective-permute-done((bf16[256,1024]{1,0:T(8,128)(2,1)S(1)}, bf16[256,1024]{1,0:T(8,128)(2,1)S(1)}, u32[]{:S(2)}, u32[]{:S(2)}) %collective-permute-start.21) | collective-permute-done | bytes 524320 | tf_op jit(solution)/shard_map/ppermute | solution.py:415
  196.5 4.0 %shard_map.143 = bf16[256,2048]{1,0:T(8,128)(2,1)S(1)} custom-call(s32[1]{0:T(128)} %bitcast.core_ref, f32[256,2048]{1,0:T(8,128)S(1)} %shard_map.141.part_ref, bf16[256,1024]{1,0:T(8,128)(2,1)S(1)} %collective-permute-done.21.handed_ref, bf16[256,4096]{1,0:T(8,128)(2,1)} %copy-done.13, bf16[256,4096]{1,0:T(8,128)(2,1)} %copy-done.14, ...), custom_call_target="tpu_custom_call" | custom-call | flops 1 | bytes 1 | tf_op jit(solution)/shard_map/pallas_call | solution.py:330
  200.5 1.9 collective-permute-start.24
  202.5 1.3 collective-permute-start.25
  203.8 5.4 %shard_map.144 = bf16[256,2048]{1,0:T(8,128)(2,1)S(1)} custom-call(s32[1]{0:T(128)} %bitcast.core_ref, bf16[256,1024]{1,0:T(8,128)(2,1)S(1)} %shard_map.140.attended_ref, bf16[256,1024]{1,0:T(8,128)(2,1)S(1)} %collective-permute-done.21.handed_ref, bf16[1024,4096]{1,0:T(8,128)(2,1)} %weight_ref.11, bf16[256,4096]{1,0:T(8,128)(2,1)} %copy-done.13, ...), custom_call_target="tpu_custom_call" | custom-call | flops 1 | bytes 1 | tf_op jit(solution)/shard_map/pallas_call | solution.py:330
  209.2 4.2 %collective-permute-start.26 = (bf16[256,2048]{1,0:T(8,128)(2,1)S(1)}, bf16[256,2048]{1,0:T(8,128)(2,1)S(1)}, u32[]{:S(2)}, u32[]{:S(2)}) collective-permute-start(bf16[256,2048]{1,0:T(8,128)(2,1)S(1)} %shard_map.144), channel_id=1, source_target_pairs={{1,2},{2,1},{5,6},{6,5},{9,10},{10,9},{13,14},{14,13},{17,18},{18,... | collective-permute-start | bytes 3145736 | tf_op jit(solution)/shard_map/ppermute | solution.py:415
  213.5 1.8 shard_map.145.attended_ref
  215.3 1.6 copy-done.7
  216.9 2.5 shard_map.146.attended_ref
  219.4 9.1 %collective-permute-done.24.plus_ref = bf16[256,2048]{1,0:T(8,128)(2,1)S(1)} collective-permute-done((bf16[256,2048]{1,0:T(8,128)(2,1)S(1)}, bf16[256,2048]{1,0:T(8,128)(2,1)S(1)}, u32[]{:S(2)}, u32[]{:S(2)}) %collective-permute-start.24) | collective-permute-done | bytes 1048608 | tf_op jit(solution)/shard_map/ppermute | solution.py:415
  228.5 3.9 %shard_map.147 = bf16[256,2048]{1,0:T(8,128)(2,1)S(1)} custom-call(bf16[256,1024]{1,0:T(8,128)(2,1)S(1)} %shard_map.145.attended_ref, bf16[1024,4096]{1,0:T(8,128)(2,1)} %weight_ref.11, bf16[256,2048]{1,0:T(8,128)(2,1)S(1)} %collective-permute-done.24.plus_ref), custom_call_target="tpu_custom_call" | custom-call | flops 1 | bytes 1 | tf_op jit(solution)/shard_map/pallas_call | solution.py:330
  232.5 1.4 collective-permute-start.27
  233.9 11.2 %shard_map.148 = bf16[256,4096]{1,0:T(8,128)(2,1)} custom-call(s32[1]{0:T(128)} %bitcast.core_ref, bf16[256,1024]{1,0:T(8,128)(2,1)S(1)} %shard_map.142.attended_ref, bf16[256,1024]{1,0:T(8,128)(2,1)S(1)} %collective-permute-done.25.handed_ref, bf16[1024,4096]{1,0:T(8,128)(2,1)} %weight_ref.11, bf16[256,4096]{1,0:T(8,128)(2,1)} %copy-done.13, ...), custom_call_target="tpu_custom_call" | custom-call | flops 1 | bytes 1 | tf_op jit(solution)/shard_map/pallas_call | solution.py:330
  245.0 1.9 collective-permute-start.29
  246.9 1.3 collective-permute-start.28
  248.2 11.6 %collective-permute-done.28.handed_ref = bf16[256,1024]{1,0:T(8,128)(2,1)S(1)} collective-permute-done((bf16[256,1024]{1,0:T(8,128)(2,1)S(1)}, bf16[256,1024]{1,0:T(8,128)(2,1)S(1)}, u32[]{:S(2)}, u32[]{:S(2)}) %collective-permute-start.28) | collective-permute-done | bytes 524320 | tf_op jit(solution)/shard_map/ppermute | solution.py:415
  259.8 4.3 %shard_map.149 = bf16[256,2048]{1,0:T(8,128)(2,1)S(1)} custom-call(bf16[256,1024]{1,0:T(8,128)(2,1)S(1)} %shard_map.145.attended_ref, bf16[1024,4096]{1,0:T(8,128)(2,1)} %weight_ref.11, bf16[256,2048]{1,0:T(8,128)(2,1)S(1)} %collective-permute-done.26.plus_ref), custom_call_target="tpu_custom_call" | custom-call | flops 1 | bytes 1 | tf_op jit(solution)/shard_map/pallas_call | solution.py:330
  264.2 2.4 collective-permute-start.30
  266.6 10.3 %shard_map.150 = bf16[256,4096]{1,0:T(8,128)(2,1)S(1)} custom-call(s32[1]{0:T(128)} %bitcast.core_ref, bf16[256,1024]{1,0:T(8,128)(2,1)S(1)} %shard_map.146.attended_ref, bf16[256,1024]{1,0:T(8,128)(2,1)S(1)} %collective-permute-done.28.handed_ref, bf16[1024,4096]{1,0:T(8,128)(2,1)} %weight_ref.11, bf16[256,4096]{1,0:T(8,128)(2,1)} %copy-done.13, ...), custom_call_target="tpu_custom_call" | custom-call | flops 1 | bytes 1 | tf_op jit(solution)/shard_map/pallas_call | solution.py:330
  276.9 17.6 %collective-permute-done.29 = bf16[256,4096]{1,0:T(8,128)(2,1)} collective-permute-done((bf16[256,4096]{1,0:T(8,128)(2,1)}, bf16[256,4096]{1,0:T(8,128)(2,1)}, u32[]{:S(2)}, u32[]{:S(2)}) %collective-permute-start.29) | collective-permute-done | bytes 2097184 | tf_op jit(solution)/shard_map/ppermute | solution.py:415
  294.4 3.7 %add_convert_fusion = bf16[256,4096]{1,0:T(8,128)(2,1)} fusion(bf16[256,4096]{1,0:T(8,128)(2,1)S(1)} %shard_map.150, bf16[256,2048]{1,0:T(8,128)(2,1)S(1)} %shard_map.149, bf16[256,2048]{1,0:T(8,128)(2,1)S(1)} %shard_map.147, bf16[256,4096]{1,0:T(8,128)(2,1)} %collective-permute-done.29, bf16[256,2048]{1,0:T(8,128)(2,1)} %collective-permute-done.30, ...), kind=kLoop, calls=%fused_computation.7 | loop fusion | flops 14680064 | bytes 10485761 | tf_op jit(solution)/shard_map/convert_element_type | solution.py:549
  (79 shorter events, 1.6 us)
Async XLA Ops:
  0.0 2.2 copy-start.15
  0.0 2.9 copy-start.18
  0.0 13.3 %collective-permute-start.2 = (bf16[8,128,1024]{2,1,0:T(8,128)(2,1)}, bf16[8,128,1024]{2,1,0:T(8,128)(2,1)S(1)}, u32[]{:S(2)}, u32[]{:S(2)}) collective-permute-start(bf16[8,128,1024]{2,1,0:T(8,128)(2,1)} %refs_1_.7), channel_id=1, source_target_pairs={{0,4},{4,0},{8,12},{12,8},{16,20},{20,16},{24,28},{28,24},{1,5},{5... | collective-permute-start | bytes 6291464 | tf_op jit(solution)/shard_map/ppermute | solution.py:411
  2.9 7.3 %copy-start = (bf16[8,128,1024]{2,1,0:T(8,128)(2,1)S(1)}, bf16[8,128,1024]{2,1,0:T(8,128)(2,1)}, u32[]{:S(2)}) copy-start(bf16[8,128,1024]{2,1,0:T(8,128)(2,1)} %refs_1_.7) | copy-start | bytes 6291460
  2.9 11.8 %copy-start.20 = (s32[16,2]{0,1:T(2,128)S(1)}, s32[16,2]{0,1:T(2,128)}, u32[]{:S(2)}) copy-start(s32[16,2]{0,1:T(2,128)} %param.20) | copy-start | bytes 388
  3.0 12.0 %copy-start.19 = (s32[16,2]{0,1:T(2,128)S(1)}, s32[16,2]{0,1:T(2,128)}, u32[]{:S(2)}) copy-start(s32[16,2]{0,1:T(2,128)} %param.21) | copy-start | bytes 388
  5.2 48.1 %collective-permute-start = (bf16[256,4096]{1,0:T(8,128)(2,1)}, bf16[256,4096]{1,0:T(8,128)(2,1)}, u32[]{:S(2)}, u32[]{:S(2)}) collective-permute-start(bf16[256,4096]{1,0:T(8,128)(2,1)} %fusion.4.refs_0_), channel_id=1, source_target_pairs={{0,1},{3,2},{1,0},{2,3},{4,5},{7,6},{5,4},{6,7},{8,9},{11,10},{9,8... | collective-permute-start | bytes 6291464 | tf_op jit(solution)/shard_map/ppermute | solution.py:415
  5.2 51.1 %collective-permute-start.1 = (bf16[256,4096]{1,0:T(8,128)(2,1)}, bf16[256,4096]{1,0:T(8,128)(2,1)}, u32[]{:S(2)}, u32[]{:S(2)}) collective-permute-start(bf16[256,4096]{1,0:T(8,128)(2,1)} %fusion.4.refs_0_), channel_id=1, source_target_pairs={{1,2},{2,1},{5,6},{6,5},{9,10},{10,9},{13,14},{14,13},{17,18},{18,... | collective-permute-start | bytes 6291464 | tf_op jit(solution)/shard_map/ppermute | solution.py:415
  10.2 47.4 %collective-permute-start.4 = (bf16[8,128,1024]{2,1,0:T(8,128)(2,1)S(1)}, bf16[8,128,1024]{2,1,0:T(8,128)(2,1)}, u32[]{:S(2)}, u32[]{:S(2)}) collective-permute-start(bf16[8,128,1024]{2,1,0:T(8,128)(2,1)S(1)} %copy-done), channel_id=1, source_target_pairs={{0,8},{4,12},{8,0},{12,4},{16,24},{20,28},{24,16},{28,20},{1,9},{5... | collective-permute-start | bytes 6291464 | tf_op jit(solution)/shard_map/ppermute | solution.py:411
  11.8 47.3 %collective-permute-start.5 = (bf16[8,128,1024]{2,1,0:T(8,128)(2,1)}, bf16[8,128,1024]{2,1,0:T(8,128)(2,1)}, u32[]{:S(2)}, u32[]{:S(2)}) collective-permute-start(bf16[8,128,1024]{2,1,0:T(8,128)(2,1)} %refs_9_.7), channel_id=1, source_target_pairs={{0,16},{4,20},{8,24},{12,28},{16,0},{20,4},{24,8},{28,12},{1,17},{... | collective-permute-start | bytes 6291464 | tf_op jit(solution)/shard_map/ppermute | solution.py:411
  13.3 1.4 copy-start.1
  14.7 44.3 %collective-permute-start.3 = (bf16[8,128,1024]{2,1,0:T(8,128)(2,1)}, bf16[8,128,1024]{2,1,0:T(8,128)(2,1)}, u32[]{:S(2)}, u32[]{:S(2)}) collective-permute-start(bf16[8,128,1024]{2,1,0:T(8,128)(2,1)} %refs_9_.7), channel_id=1, source_target_pairs={{0,4},{4,0},{8,12},{12,8},{16,20},{20,16},{24,28},{28,24},{1,5},{5... | collective-permute-start | bytes 6291464 | tf_op jit(solution)/shard_map/ppermute | solution.py:411
  15.8 52.3 %copy-start.22 = (s32[4]{0:T(128)S(1)}, s32[4]{0:T(128)}, u32[]{:S(2)}) copy-start(s32[4]{0:T(128)} %constant.62.clone) | copy-start | bytes 52
  15.8 52.9 %copy-start.21 = (s32[4]{0:T(128)S(1)}, s32[4]{0:T(128)}, u32[]{:S(2)}) copy-start(s32[4]{0:T(128)} %constant.63.clone) | copy-start | bytes 52
  59.1 47.9 %collective-permute-start.10 = (bf16[256,4096]{1,0:T(8,128)(2,1)S(1)}, bf16[256,4096]{1,0:T(8,128)(2,1)S(1)}, u32[]{:S(2)}, u32[]{:S(2)}) collective-permute-start(bf16[256,4096]{1,0:T(8,128)(2,1)S(1)} %get-tuple-element.77), channel_id=1, source_target_pairs={{0,1},{3,2},{4,5},{7,6},{8,9},{11,10},{12,13},{15,14},{16,17},{19,... | collective-permute-start | bytes 6291464 | tf_op jit(solution)/shard_map/ppermute | solution.py:415
  60.4 48.1 %collective-permute-start.6 = (bf16[256,4096]{1,0:T(8,128)(2,1)}, bf16[256,4096]{1,0:T(8,128)(2,1)S(1)}, u32[]{:S(2)}, u32[]{:S(2)}) collective-permute-start(bf16[256,4096]{1,0:T(8,128)(2,1)} %collective-permute-done.refs_1_), channel_id=1, source_target_pairs={{1,2},{2,1},{5,6},{6,5},{9,10},{10,9},{13,14},{14,13},{17,18},{18,... | collective-permute-start | bytes 6291464 | tf_op jit(solution)/shard_map/ppermute | solution.py:415
  62.6 46.8 %collective-permute-start.7 = (bf16[256,4096]{1,0:T(8,128)(2,1)}, bf16[256,4096]{1,0:T(8,128)(2,1)S(1)}, u32[]{:S(2)}, u32[]{:S(2)}) collective-permute-start(bf16[256,4096]{1,0:T(8,128)(2,1)} %collective-permute-done.1.refs_1_), channel_id=1, source_target_pairs={{1,0},{2,3},{5,4},{6,7},{9,8},{10,11},{13,12},{14,15},{17,16},{18,... | collective-permute-start | bytes 6291464 | tf_op jit(solution)/shard_map/ppermute | solution.py:415
  66.0 45.5 %collective-permute-start.8 = (bf16[8,128,1024]{2,1,0:T(8,128)(2,1)S(1)}, bf16[8,128,1024]{2,1,0:T(8,128)(2,1)S(1)}, u32[]{:S(2)}, u32[]{:S(2)}) collective-permute-start(bf16[8,128,1024]{2,1,0:T(8,128)(2,1)S(1)} %copy-done), channel_id=1, source_target_pairs={{0,16},{4,20},{8,24},{12,28},{16,0},{20,4},{24,8},{28,12},{1,17},{... | collective-permute-start | bytes 6291464 | tf_op jit(solution)/shard_map/ppermute | solution.py:411
  67.6 45.4 %collective-permute-start.9 = (bf16[8,128,1024]{2,1,0:T(8,128)(2,1)}, bf16[8,128,1024]{2,1,0:T(8,128)(2,1)S(1)}, u32[]{:S(2)}, u32[]{:S(2)}) collective-permute-start(bf16[8,128,1024]{2,1,0:T(8,128)(2,1)} %refs_9_.7), channel_id=1, source_target_pairs={{0,8},{4,12},{8,0},{12,4},{16,24},{20,28},{24,16},{28,20},{1,9},{5... | collective-permute-start | bytes 6291464 | tf_op jit(solution)/shard_map/ppermute | solution.py:411
  69.4 96.4 %slice-start = ((s8[8388608]{0:T(1024)(128)(4,1)}), s8[4194304]{0:T(1024)(128)(4,1)S(1)}, s32[]{:S(2)}) async-start(s8[8388608]{0:T(1024)(128)(4,1)} %bitcast.3), calls=%async_computation | async-start | bytes 8388608
  77.6 88.1 %slice-start.1 = ((s8[8388608]{0:T(1024)(128)(4,1)}), s8[4194304]{0:T(1024)(128)(4,1)S(1)}, s32[]{:S(2)}) async-start(s8[8388608]{0:T(1024)(128)(4,1)} %bitcast.3), calls=%async_computation.1 | async-start | bytes 8388608
  107.0 72.7 %copy-start.13 = (bf16[256,4096]{1,0:T(8,128)(2,1)}, bf16[256,4096]{1,0:T(8,128)(2,1)S(1)}, u32[]{:S(2)}) copy-start(bf16[256,4096]{1,0:T(8,128)(2,1)S(1)} %collective-permute-done.10.refs_0_) | copy-start | bytes 6291460
  113.0 12.3 %collective-permute-start.15 = (bf16[8,128,1024]{2,1,0:T(8,128)(2,1)}, bf16[8,128,1024]{2,1,0:T(8,128)(2,1)S(1)}, u32[]{:S(2)}, u32[]{:S(2)}) collective-permute-start(bf16[8,128,1024]{2,1,0:T(8,128)(2,1)} %collective-permute-done.4.refs_3_), channel_id=1, source_target_pairs={{0,4},{4,0},{8,12},{12,8},{16,20},{20,16},{24,28},{28,24},{1,5},{5... | collective-permute-start | bytes 6291464 | tf_op jit(solution)/shard_map/ppermute | solution.py:411
  113.0 47.1 %collective-permute-start.11 = (bf16[256,4096]{1,0:T(8,128)(2,1)S(1)}, bf16[256,4096]{1,0:T(8,128)(2,1)S(1)}, u32[]{:S(2)}, u32[]{:S(2)}) collective-permute-start(bf16[256,4096]{1,0:T(8,128)(2,1)S(1)} %collective-permute-done.6.refs_0_), channel_id=1, source_target_pairs={{1,0},{2,3},{5,4},{6,7},{9,8},{10,11},{13,12},{14,15},{17,16},{18,... | collective-permute-start | bytes 6291464 | tf_op jit(solution)/shard_map/ppermute | solution.py:415
  114.6 48.2 %collective-permute-start.12 = (bf16[8,128,1024]{2,1,0:T(8,128)(2,1)}, bf16[8,128,1024]{2,1,0:T(8,128)(2,1)S(1)}, u32[]{:S(2)}, u32[]{:S(2)}) collective-permute-start(bf16[8,128,1024]{2,1,0:T(8,128)(2,1)} %collective-permute-done.4.refs_3_), channel_id=1, source_target_pairs={{0,16},{4,20},{8,24},{12,28},{16,0},{20,4},{24,8},{28,12},{1,17},{... | collective-permute-start | bytes 6291464 | tf_op jit(solution)/shard_map/ppermute | solution.py:411
  115.5 47.7 %collective-permute-start.13 = (bf16[8,128,1024]{2,1,0:T(8,128)(2,1)}, bf16[8,128,1024]{2,1,0:T(8,128)(2,1)S(1)}, u32[]{:S(2)}, u32[]{:S(2)}) collective-permute-start(bf16[8,128,1024]{2,1,0:T(8,128)(2,1)} %collective-permute-done.5.refs_13_), channel_id=1, source_target_pairs={{0,8},{4,12},{8,0},{12,4},{16,24},{20,28},{24,16},{28,20},{1,9},{5... | collective-permute-start | bytes 6291464 | tf_op jit(solution)/shard_map/ppermute | solution.py:411
  116.0 49.3 %collective-permute-start.14 = (bf16[256,4096]{1,0:T(8,128)(2,1)}, bf16[256,4096]{1,0:T(8,128)(2,1)S(1)}, u32[]{:S(2)}, u32[]{:S(2)}) collective-permute-start(bf16[256,4096]{1,0:T(8,128)(2,1)} %get-tuple-element.83), channel_id=1, source_target_pairs={{0,1},{3,2},{4,5},{7,6},{8,9},{11,10},{12,13},{15,14},{16,17},{19,... | collective-permute-start | bytes 6291464 | tf_op jit(solution)/shard_map/ppermute | solution.py:415
  125.3 48.0 %copy-start.2 = (bf16[8,128,1024]{2,1,0:T(8,128)(2,1)S(1)}, bf16[8,128,1024]{2,1,0:T(8,128)(2,1)}, u32[]{:S(2)}) copy-start(bf16[8,128,1024]{2,1,0:T(8,128)(2,1)} %copy-done.1) | copy-start | bytes 6291460
  125.3 48.0 %copy-start.12 = (s32[16]{0:T(128)S(1)}, s32[16]{0:T(128)}, u32[]{:S(2)}) copy-start(s32[16]{0:T(128)} %counts_ref.7) | copy-start | bytes 196
  125.3 45.3 %collective-permute-start.19 = (bf16[8,128,1024]{2,1,0:T(8,128)(2,1)}, bf16[8,128,1024]{2,1,0:T(8,128)(2,1)S(1)}, u32[]{:S(2)}, u32[]{:S(2)}) collective-permute-start(bf16[8,128,1024]{2,1,0:T(8,128)(2,1)} %collective-permute-done.5.refs_13_), channel_id=1, source_target_pairs={{0,4},{4,0},{8,12},{12,8},{16,20},{20,16},{24,28},{28,24},{1,5},{5... | collective-permute-start | bytes 6291464 | tf_op jit(solution)/shard_map/ppermute | solution.py:411
  160.1 10.6 %collective-permute-start.16 = (bf16[8,128,1024]{2,1,0:T(8,128)(2,1)S(1)}, bf16[8,128,1024]{2,1,0:T(8,128)(2,1)S(1)}, u32[]{:S(2)}, u32[]{:S(2)}) collective-permute-start(bf16[8,128,1024]{2,1,0:T(8,128)(2,1)S(1)} %collective-permute-done.8.refs_5_), channel_id=1, source_target_pairs={{0,4},{4,0},{8,12},{12,8},{16,20},{20,16},{24,28},{28,24},{1,5},{5... | collective-permute-start | bytes 6291464 | tf_op jit(solution)/shard_map/ppermute | solution.py:411
  162.7 8.0 %collective-permute-start.18 = (bf16[8,128,1024]{2,1,0:T(8,128)(2,1)S(1)}, bf16[8,128,1024]{2,1,0:T(8,128)(2,1)S(1)}, u32[]{:S(2)}, u32[]{:S(2)}) collective-permute-start(bf16[8,128,1024]{2,1,0:T(8,128)(2,1)S(1)} %collective-permute-done.9.refs_11_), channel_id=1, source_target_pairs={{0,4},{4,0},{8,12},{12,8},{16,20},{20,16},{24,28},{28,24},{1,5},{5... | collective-permute-start | bytes 6291464 | tf_op jit(solution)/shard_map/ppermute | solution.py:411
  163.1 7.5 %copy-start.3 = (bf16[8,128,1024]{2,1,0:T(8,128)(2,1)}, bf16[8,128,1024]{2,1,0:T(8,128)(2,1)S(1)}, u32[]{:S(2)}) copy-start(bf16[8,128,1024]{2,1,0:T(8,128)(2,1)S(1)} %collective-permute-done.13.refs_15_) | copy-start | bytes 6291460
  165.3 14.6 %copy-start.14 = (bf16[256,4096]{1,0:T(8,128)(2,1)}, bf16[256,4096]{1,0:T(8,128)(2,1)S(1)}, u32[]{:S(2)}) copy-start(bf16[256,4096]{1,0:T(8,128)(2,1)S(1)} %collective-permute-done.14.refs_1_) | copy-start | bytes 6291460
  165.3 5.4 %collective-permute-start.17 = (bf16[8,128,1024]{2,1,0:T(8,128)(2,1)S(1)}, bf16[8,128,1024]{2,1,0:T(8,128)(2,1)S(1)}, u32[]{:S(2)}, u32[]{:S(2)}) collective-permute-start(bf16[8,128,1024]{2,1,0:T(8,128)(2,1)S(1)} %collective-permute-done.12.refs_7_), channel_id=1, source_target_pairs={{0,4},{4,0},{8,12},{12,8},{16,20},{20,16},{24,28},{28,24},{1,5},{5... | collective-permute-start | bytes 6291464 | tf_op jit(solution)/shard_map/ppermute | solution.py:411
  165.3 8.0 %collective-permute-start.20 = (bf16[8,128,1024]{2,1,0:T(8,128)(2,1)S(1)}, bf16[8,128,1024]{2,1,0:T(8,128)(2,1)S(1)}, u32[]{:S(2)}, u32[]{:S(2)}) collective-permute-start(bf16[8,128,1024]{2,1,0:T(8,128)(2,1)S(1)} %collective-permute-done.13.refs_15_), channel_id=1, source_target_pairs={{0,4},{4,0},{8,12},{12,8},{16,20},{20,16},{24,28},{28,24},{1,5},{5... | collective-permute-start | bytes 6291464 | tf_op jit(solution)/shard_map/ppermute | solution.py:411
  170.7 42.8 %copy-start.6 = (bf16[8,128,1024]{2,1,0:T(8,128)(2,1)}, bf16[8,128,1024]{2,1,0:T(8,128)(2,1)S(1)}, u32[]{:S(2)}) copy-start(bf16[8,128,1024]{2,1,0:T(8,128)(2,1)S(1)} %collective-permute-done.16.refs_6_) | copy-start | bytes 6291460
  170.7 9.0 %copy-start.8 = (bf16[8,128,1024]{2,1,0:T(8,128)(2,1)}, bf16[8,128,1024]{2,1,0:T(8,128)(2,1)S(1)}, u32[]{:S(2)}) copy-start(bf16[8,128,1024]{2,1,0:T(8,128)(2,1)S(1)} %collective-permute-done.18.refs_12_) | copy-start | bytes 6291460
  173.3 1.6 copy-start.4
  174.9 4.9 %copy-start.10 = (bf16[8,128,1024]{2,1,0:T(8,128)(2,1)}, bf16[8,128,1024]{2,1,0:T(8,128)(2,1)S(1)}, u32[]{:S(2)}) copy-start(bf16[8,128,1024]{2,1,0:T(8,128)(2,1)S(1)} %collective-permute-done.20.refs_16_) | copy-start | bytes 6291460
  179.7 16.8 %collective-permute-start.22 = (bf16[256,4096]{1,0:T(8,128)(2,1)S(1)}, bf16[256,4096]{1,0:T(8,128)(2,1)}, u32[]{:S(2)}, u32[]{:S(2)}) collective-permute-start(bf16[256,4096]{1,0:T(8,128)(2,1)S(1)} %collective-permute-done.10.refs_0_), channel_id=1, source_target_pairs={{0,4},{4,0},{8,12},{12,8},{16,20},{20,16},{24,28},{28,24},{1,5},{5... | collective-permute-start | bytes 6291464 | tf_op jit(solution)/shard_map/ppermute | solution.py:411
  179.8 6.0 %copy-start.9 = (bf16[8,128,1024]{2,1,0:T(8,128)(2,1)S(1)}, bf16[8,128,1024]{2,1,0:T(8,128)(2,1)}, u32[]{:S(2)}) copy-start(bf16[8,128,1024]{2,1,0:T(8,128)(2,1)} %copy-done.8) | copy-start | bytes 6291460
  179.8 6.0 %copy-start.11 = (bf16[8,128,1024]{2,1,0:T(8,128)(2,1)S(1)}, bf16[8,128,1024]{2,1,0:T(8,128)(2,1)}, u32[]{:S(2)}) copy-start(bf16[8,128,1024]{2,1,0:T(8,128)(2,1)} %copy-done.10) | copy-start | bytes 6291460
  179.8 16.7 %collective-permute-start.23 = (bf16[256,4096]{1,0:T(8,128)(2,1)S(1)}, bf16[256,4096]{1,0:T(8,128)(2,1)}, u32[]{:S(2)}, u32[]{:S(2)}) collective-permute-start(bf16[256,4096]{1,0:T(8,128)(2,1)S(1)} %collective-permute-done.14.refs_1_), channel_id=1, source_target_pairs={{0,4},{4,0},{8,12},{12,8},{16,20},{20,16},{24,28},{28,24},{1,5},{5... | collective-permute-start | bytes 6291464 | tf_op jit(solution)/shard_map/ppermute | solution.py:411
  180.3 16.2 %collective-permute-start.21 = (bf16[256,1024]{1,0:T(8,128)(2,1)S(1)}, bf16[256,1024]{1,0:T(8,128)(2,1)S(1)}, u32[]{:S(2)}, u32[]{:S(2)}) collective-permute-start(bf16[256,1024]{1,0:T(8,128)(2,1)S(1)} %shard_map.140.attended_ref), channel_id=1, source_target_pairs={{0,1},{3,2},{4,5},{7,6},{8,9},{11,10},{12,13},{15,14},{16,17},{19,... | collective-permute-start | bytes 1572872 | tf_op jit(solution)/shard_map/ppermute | solution.py:415
  200.5 28.0 %collective-permute-start.24 = (bf16[256,2048]{1,0:T(8,128)(2,1)S(1)}, bf16[256,2048]{1,0:T(8,128)(2,1)S(1)}, u32[]{:S(2)}, u32[]{:S(2)}) collective-permute-start(bf16[256,2048]{1,0:T(8,128)(2,1)S(1)} %shard_map.143), channel_id=1, source_target_pairs={{1,2},{2,1},{5,6},{6,5},{9,10},{10,9},{13,14},{14,13},{17,18},{18,... | collective-permute-start | bytes 3145736 | tf_op jit(solution)/shard_map/ppermute | solution.py:415
  202.5 31.4 %collective-permute-start.25 = (bf16[256,1024]{1,0:T(8,128)(2,1)S(1)}, bf16[256,1024]{1,0:T(8,128)(2,1)S(1)}, u32[]{:S(2)}, u32[]{:S(2)}) collective-permute-start(bf16[256,1024]{1,0:T(8,128)(2,1)S(1)} %shard_map.142.attended_ref), channel_id=1, source_target_pairs={{0,1},{3,2},{4,5},{7,6},{8,9},{11,10},{12,13},{15,14},{16,17},{19,... | collective-permute-start | bytes 1572872 | tf_op jit(solution)/shard_map/ppermute | solution.py:415
  209.2 6.1 %copy-start.5 = (bf16[8,128,1024]{2,1,0:T(8,128)(2,1)S(1)}, bf16[8,128,1024]{2,1,0:T(8,128)(2,1)}, u32[]{:S(2)}) copy-start(bf16[8,128,1024]{2,1,0:T(8,128)(2,1)} %copy-done.3) | copy-start | bytes 6291460
  209.2 50.6 %collective-permute-start.26 = (bf16[256,2048]{1,0:T(8,128)(2,1)S(1)}, bf16[256,2048]{1,0:T(8,128)(2,1)S(1)}, u32[]{:S(2)}, u32[]{:S(2)}) collective-permute-start(bf16[256,2048]{1,0:T(8,128)(2,1)S(1)} %shard_map.144), channel_id=1, source_target_pairs={{1,2},{2,1},{5,6},{6,5},{9,10},{10,9},{13,14},{14,13},{17,18},{18,... | collective-permute-start | bytes 3145736 | tf_op jit(solution)/shard_map/ppermute | solution.py:415
  215.3 1.6 copy-start.7
  232.5 27.4 %collective-permute-start.27 = (bf16[256,2048]{1,0:T(8,128)(2,1)S(1)}, bf16[256,2048]{1,0:T(8,128)(2,1)S(1)}, u32[]{:S(2)}, u32[]{:S(2)}) collective-permute-start(bf16[256,2048]{1,0:T(8,128)(2,1)S(1)} %shard_map.147), channel_id=1, source_target_pairs={{1,0},{2,3},{5,4},{6,7},{9,8},{10,11},{13,12},{14,15},{17,16},{18,... | collective-permute-start | bytes 3145736 | tf_op jit(solution)/shard_map/ppermute | solution.py:415
  245.0 49.4 %collective-permute-start.29 = (bf16[256,4096]{1,0:T(8,128)(2,1)}, bf16[256,4096]{1,0:T(8,128)(2,1)}, u32[]{:S(2)}, u32[]{:S(2)}) collective-permute-start(bf16[256,4096]{1,0:T(8,128)(2,1)} %shard_map.148), channel_id=1, source_target_pairs={{1,2},{2,1},{5,6},{6,5},{9,10},{10,9},{13,14},{14,13},{17,18},{18,... | collective-permute-start | bytes 6291464 | tf_op jit(solution)/shard_map/ppermute | solution.py:415
  246.9 12.9 %collective-permute-start.28 = (bf16[256,1024]{1,0:T(8,128)(2,1)S(1)}, bf16[256,1024]{1,0:T(8,128)(2,1)S(1)}, u32[]{:S(2)}, u32[]{:S(2)}) collective-permute-start(bf16[256,1024]{1,0:T(8,128)(2,1)S(1)} %shard_map.146.attended_ref), channel_id=1, source_target_pairs={{0,1},{3,2},{4,5},{7,6},{8,9},{11,10},{12,13},{15,14},{16,17},{19,... | collective-permute-start | bytes 1572872 | tf_op jit(solution)/shard_map/ppermute | solution.py:415
  259.8 4.3 %copy-start.16 = (bf16[256,2048]{1,0:T(8,128)(2,1)}, bf16[256,2048]{1,0:T(8,128)(2,1)S(1)}, u32[]{:S(2)}) copy-start(bf16[256,2048]{1,0:T(8,128)(2,1)S(1)} %collective-permute-done.27) | copy-start | bytes 3145732
  264.2 30.2 %collective-permute-start.30 = (bf16[256,2048]{1,0:T(8,128)(2,1)S(1)}, bf16[256,2048]{1,0:T(8,128)(2,1)}, u32[]{:S(2)}, u32[]{:S(2)}) collective-permute-start(bf16[256,2048]{1,0:T(8,128)(2,1)S(1)} %shard_map.149), channel_id=1, source_target_pairs={{1,0},{2,3},{5,4},{6,7},{9,8},{10,11},{13,12},{14,15},{17,16},{18,... | collective-permute-start | bytes 3145736 | tf_op jit(solution)/shard_map/ppermute | solution.py:415
  266.6 27.8 %copy-start.17 = (bf16[256,2048]{1,0:T(8,128)(2,1)S(1)}, bf16[256,2048]{1,0:T(8,128)(2,1)}, u32[]{:S(2)}) copy-start(bf16[256,2048]{1,0:T(8,128)(2,1)} %copy-done.16) | copy-start | bytes 3145732

commit v5 on v3

--- a/solution.py
+++ b/solution.py
@@ -248,7 +248,7 @@
                 pltpu.SemaphoreType.DMA((blocks + 1, 4)),
             ],
         ),
-        compiler_params=pltpu.CompilerParams(vmem_limit_bytes=16 << 20),
+        compiler_params=pltpu.CompilerParams(vmem_limit_bytes=13 << 20),
         cost_estimate=SMALL,
     )(order, relative, slots, counts, queries, *keys, *values)
 
@@ -285,7 +285,7 @@
             out_specs=pl.BlockSpec((rows, 256), lambda i, _: (0, i)),
             scratch_shapes=[pltpu.VMEM((rows, depth), jnp.bfloat16), pltpu.SemaphoreType.DMA],
         ),
-        compiler_params=pltpu.CompilerParams(vmem_limit_bytes=16 << 20),
+        compiler_params=pltpu.CompilerParams(vmem_limit_bytes=13 << 20),
         cost_estimate=SMALL,
     )(which.reshape(1), *sources, in_hbm(weight) if streamed else weight)
 
@@ -336,7 +336,7 @@
             in_specs=in_specs,
             out_specs=column_block(rows, 0),
         ),
-        compiler_params=pltpu.CompilerParams(vmem_limit_bytes=16 << 20),
+        compiler_params=pltpu.CompilerParams(vmem_limit_bytes=13 << 20),
         cost_estimate=SMALL,
     )(*operands)
 

time: 299 us -> 299 us (level)
  transfers between devices with their start and end apart: 31 -> 31, of which waited for: 18 -> 18; matrix products, arithmetic and copies ran while one was open for 4% -> 3% of each run, Pallas kernels for 27% -> 27%
where the time goes in v5:
time: 299 us; the launch traced here: 298 us
  waiting for transfers between devices  147 us (49%)
  Pallas kernels  87.5 us (29%)
  starting transfers between devices  45.9 us (15%)
  other arithmetic  8.69 us (3%)
  local copies, waits for them, and re-layouts  8.6 us (3%)
    ppermute x15, waiting for transfers between devices, along(): return lax.ppermute(values, 'mp', list(pairs))  135 us
    pallas_call x7, Pallas kernels, output_call(): pl.pallas_call(kernel, out_shape=jax.ShapeDtypeStruct((rows, count * 512)...  43.2 us
    ppermute x15, starting transfers between devices, along(): return lax.ppermute(values, 'mp', list(pairs))  38.1 us
    pallas_call x4, Pallas kernels, project(): pl.pallas_call(functools.partial(project_kernel, 1.0 / math.sqrt(HD)), ou...  29.3 us
    pallas_call x4, Pallas kernels, shard_attention(): pl.pallas_call(functools.partial(attention_kernel, step, blocks), out_sha...  15 us
    ppermute x16, waiting for transfers between devices, swap(): return lax.ppermute(values, 'dp', [(i, i ^ bits) for i in range(8)])  12 us
    ppermute x16, starting transfers between devices, swap(): return lax.ppermute(values, 'dp', [(i, i ^ bits) for i in range(8)])  7.77 us
  transfers between devices with their start and end apart: 31, of which 18 were waited for; matrix products, arithmetic and copies ran while one was open for 3% of the time, Pallas kernels for 27%

profile of v5, /device:TPU:8, one launch (start us, length us, event | category | flops | bytes accessed | tf_op | source)
XLA Modules:
  0.0 297.9 jit_solution(13500774483963276160)
XLA Ops:
  0.0 2.1 convert_reduce_fusion
  2.2 0.7 fusion.2
  3.0 2.2 fusion.4.refs_0_
  5.2 5.0 %collective-permute-start.1 = (bf16[256,4096]{1,0:T(8,128)(2,1)}, bf16[256,4096]{1,0:T(8,128)(2,1)}, u32[]{:S(2)}, u32[]{:S(2)}) collective-permute-start(bf16[256,4096]{1,0:T(8,128)(2,1)} %fusion.4.refs_0_), channel_id=1, source_target_pairs={{1,2},{2,1},{5,6},{6,5},{9,10},{10,9},{13,14},{14,13},{17,18},{18,... | collective-permute-start | bytes 6291464 | tf_op jit(solution)/shard_map/ppermute | solution.py:415
  10.2 1.6 collective-permute-start.4
  11.8 1.5 collective-permute-start.5
  13.3 1.4 copy-done.1
  15.1 0.7 fusion.5.order_ref
  15.8 2.6 constant_dynamic-slice_fusion.1
  18.5 34.8 %collective-permute-done.refs_1_ = bf16[256,4096]{1,0:T(8,128)(2,1)} collective-permute-done((bf16[256,4096]{1,0:T(8,128)(2,1)}, bf16[256,4096]{1,0:T(8,128)(2,1)}, u32[]{:S(2)}, u32[]{:S(2)}) %collective-permute-start) | collective-permute-done | bytes 2097184 | tf_op jit(solution)/shard_map/ppermute | solution.py:415
  53.3 3.0 %collective-permute-done.1.refs_1_ = bf16[256,4096]{1,0:T(8,128)(2,1)} collective-permute-done((bf16[256,4096]{1,0:T(8,128)(2,1)}, bf16[256,4096]{1,0:T(8,128)(2,1)}, u32[]{:S(2)}, u32[]{:S(2)}) %collective-permute-start.1) | collective-permute-done | bytes 2097184 | tf_op jit(solution)/shard_map/ppermute | solution.py:415
  56.3 1.3 collective-permute-done.4.refs_3_
  57.7 1.4 collective-permute-done.5.refs_13_
  59.1 1.3 collective-permute-start.10
  60.4 2.2 collective-permute-start.6
  62.6 3.4 %collective-permute-start.7 = (bf16[256,4096]{1,0:T(8,128)(2,1)}, bf16[256,4096]{1,0:T(8,128)(2,1)S(1)}, u32[]{:S(2)}, u32[]{:S(2)}) collective-permute-start(bf16[256,4096]{1,0:T(8,128)(2,1)} %collective-permute-done.1.refs_1_), channel_id=1, source_target_pairs={{1,0},{2,3},{5,4},{6,7},{9,8},{10,11},{13,12},{14,15},{17,16},{18,... | collective-permute-start | bytes 6291464 | tf_op jit(solution)/shard_map/ppermute | solution.py:415
  66.0 1.6 collective-permute-start.8
  67.6 0.5 collective-permute-start.9
  68.1 0.6 dynamic_slice.26.which_ref
  68.8 0.6 dynamic_slice.28.which_ref
  69.4 8.3 %shard_map.136.refs_0_ = bf16[256,1024]{1,0:T(8,128)(2,1)S(1)} custom-call(s32[1]{0:T(128)} %dynamic_slice.26.which_ref, bf16[256,4096]{1,0:T(8,128)(2,1)} %fusion.4.refs_0_, bf16[256,4096]{1,0:T(8,128)(2,1)} %collective-permute-done.refs_1_, bf16[4096,1024]{1,0:T(8,128)(2,1)} %refs_2_.7), custom_call_target="tpu_custom_call" | custom-call | flops 1 | bytes 1 | tf_op jit(solution)/shard_map/pallas_call | solution.py:277
  77.7 8.3 %shard_map.137.refs_0_ = bf16[256,1024]{1,0:T(8,128)(2,1)S(1)} custom-call(s32[1]{0:T(128)} %dynamic_slice.28.which_ref, bf16[256,4096]{1,0:T(8,128)(2,1)} %fusion.4.refs_0_, bf16[256,4096]{1,0:T(8,128)(2,1)} %collective-permute-done.refs_1_, bf16[4096,1024]{1,0:T(8,128)(2,1)} %refs_2_.7), custom_call_target="tpu_custom_call" | custom-call | flops 1 | bytes 1 | tf_op jit(solution)/shard_map/pallas_call | solution.py:277
  85.9 21.1 %collective-permute-done.10.refs_0_ = bf16[256,4096]{1,0:T(8,128)(2,1)S(1)} collective-permute-done((bf16[256,4096]{1,0:T(8,128)(2,1)S(1)}, bf16[256,4096]{1,0:T(8,128)(2,1)S(1)}, u32[]{:S(2)}, u32[]{:S(2)}) %collective-permute-start.10) | collective-permute-done | bytes 2097184 | tf_op jit(solution)/shard_map/ppermute | solution.py:415
  107.0 1.5 collective-permute-done.6.refs_0_
  108.5 0.9 collective-permute-done.7.refs_0_
  109.4 2.1 collective-permute-done.8.refs_5_
  111.5 1.4 collective-permute-done.9.refs_11_
  113.0 1.6 collective-permute-start.11
  114.6 0.9 collective-permute-start.12
  115.5 0.5 collective-permute-start.13
  116.0 1.3 collective-permute-start.14
  117.3 7.9 %shard_map.139.refs_0_ = bf16[256,1024]{1,0:T(8,128)(2,1)S(1)} custom-call(s32[1]{0:T(128)} %dynamic_slice.28.which_ref, bf16[256,4096]{1,0:T(8,128)(2,1)S(1)} %collective-permute-done.7.refs_0_, bf16[256,4096]{1,0:T(8,128)(2,1)} %collective-permute-done.1.refs_1_, bf16[4096,1024]{1,0:T(8,128)(2,1)} %refs_2_.7), custom_call_target="tpu_custom_call" | custom-call | flops 1 | bytes 1 | tf_op jit(solution)/shard_map/pallas_call | solution.py:277
  125.3 34.8 %collective-permute-done.11.refs_1_ = bf16[256,4096]{1,0:T(8,128)(2,1)S(1)} collective-permute-done((bf16[256,4096]{1,0:T(8,128)(2,1)S(1)}, bf16[256,4096]{1,0:T(8,128)(2,1)S(1)}, u32[]{:S(2)}, u32[]{:S(2)}) %collective-permute-start.11) | collective-permute-done | bytes 2097184 | tf_op jit(solution)/shard_map/ppermute | solution.py:415
  160.1 2.6 collective-permute-done.12.refs_7_
  163.1 2.0 collective-permute-done.14.refs_1_
  165.2 0.5 collective-permute-start.20
  165.7 4.8 %shard_map.138.refs_0_ = bf16[256,1024]{1,0:T(8,128)(2,1)S(1)} custom-call(s32[1]{0:T(128)} %dynamic_slice.26.which_ref, bf16[256,4096]{1,0:T(8,128)(2,1)S(1)} %collective-permute-done.6.refs_0_, bf16[256,4096]{1,0:T(8,128)(2,1)S(1)} %collective-permute-done.11.refs_1_, bf16[4096,1024]{1,0:T(8,128)(2,1)S(1)} %bitcast.4), custom_call_target="tpu_custom_call" | custom-call | flops 1 | bytes 1 | tf_op jit(solution)/shard_map/pallas_call | solution.py:277
  170.6 2.7 collective-permute-done.20.refs_16_
  173.3 4.0 %shard_map.140.attended_ref = bf16[256,1024]{1,0:T(8,128)(2,1)S(1)} custom-call(s32[4]{0:T(128)S(1)} %fusion.5.order_ref, s32[32]{0:T(128)S(1)} %xor.11.relative_ref, s32[32]{0:T(128)S(1)} %reshape.30.slots_ref, s32[16]{0:T(128)S(1)} %copy-done.7, bf16[256,1024]{1,0:T(8,128)(2,1)S(1)} %shard_map.138.refs_0_, bf16[8,128,1024]{2,1,0:T(8,128)(2,1)S(1)} %copy-done, ...), custom_call_target="tpu_custom_call" | custom-call | flops 1 | bytes 1 | tf_op jit(solution)/shard_map/pallas_call | solution.py:236
  177.8 1.4 collective-permute-start.21
  179.3 4.0 %shard_map.141.part_ref = f32[256,2048]{1,0:T(8,128)S(1)} custom-call(bf16[256,1024]{1,0:T(8,128)(2,1)S(1)} %shard_map.140.attended_ref, bf16[1024,4096]{1,0:T(8,128)(2,1)} %weight_ref.11), custom_call_target="tpu_custom_call" | custom-call | flops 1 | bytes 1 | tf_op jit(solution)/shard_map/pallas_call | solution.py:330
  183.3 4.8 %shard_map.142.attended_ref = bf16[256,1024]{1,0:T(8,128)(2,1)S(1)} custom-call(s32[4]{0:T(128)S(1)} %fusion.5.order_ref, s32[32]{0:T(128)S(1)} %xor.11.relative_ref, s32[32]{0:T(128)S(1)} %reshape.30.slots_ref, s32[16]{0:T(128)S(1)} %copy-done.7, bf16[256,1024]{1,0:T(8,128)(2,1)S(1)} %shard_map.139.refs_0_, bf16[8,128,1024]{2,1,0:T(8,128)(2,1)S(1)} %copy-done, ...), custom_call_target="tpu_custom_call" | custom-call | flops 1 | bytes 1 | tf_op jit(solution)/shard_map/pallas_call | solution.py:236
  188.1 5.9 %collective-permute-done.21.handed_ref = bf16[256,1024]{1,0:T(8,128)(2,1)S(1)} collective-permute-done((bf16[256,1024]{1,0:T(8,128)(2,1)S(1)}, bf16[256,1024]{1,0:T(8,128)(2,1)S(1)}, u32[]{:S(2)}, u32[]{:S(2)}) %collective-permute-start.21) | collective-permute-done | bytes 524320 | tf_op jit(solution)/shard_map/ppermute | solution.py:415
  194.1 1.3 copy-done.9
  195.4 0.8 copy-done.10
  196.2 4.0 %shard_map.143 = bf16[256,2048]{1,0:T(8,128)(2,1)S(1)} custom-call(s32[1]{0:T(128)} %bitcast.core_ref, f32[256,2048]{1,0:T(8,128)S(1)} %shard_map.141.part_ref, bf16[256,1024]{1,0:T(8,128)(2,1)S(1)} %collective-permute-done.21.handed_ref, bf16[256,4096]{1,0:T(8,128)(2,1)} %copy-done.8, bf16[256,4096]{1,0:T(8,128)(2,1)} %collective-permute-done.14.refs_1_, ...), custom_call_target="tpu_custom_call" | custom-call | flops 1 | bytes 1 | tf_op jit(solution)/shard_map/pallas_call | solution.py:330
  200.1 1.9 collective-permute-start.25
  202.1 1.3 collective-permute-start.24
  203.4 5.4 %shard_map.144 = bf16[256,2048]{1,0:T(8,128)(2,1)S(1)} custom-call(s32[1]{0:T(128)} %bitcast.core_ref, bf16[256,1024]{1,0:T(8,128)(2,1)S(1)} %shard_map.140.attended_ref, bf16[256,1024]{1,0:T(8,128)(2,1)S(1)} %collective-permute-done.21.handed_ref, bf16[1024,4096]{1,0:T(8,128)(2,1)} %weight_ref.11, bf16[256,4096]{1,0:T(8,128)(2,1)} %copy-done.8, ...), custom_call_target="tpu_custom_call" | custom-call | flops 1 | bytes 1 | tf_op jit(solution)/shard_map/pallas_call | solution.py:330
  208.8 4.1 %collective-permute-start.26 = (bf16[256,2048]{1,0:T(8,128)(2,1)S(1)}, bf16[256,2048]{1,0:T(8,128)(2,1)S(1)}, u32[]{:S(2)}, u32[]{:S(2)}) collective-permute-start(bf16[256,2048]{1,0:T(8,128)(2,1)S(1)} %shard_map.144), channel_id=1, source_target_pairs={{1,2},{2,1},{5,6},{6,5},{9,10},{10,9},{13,14},{14,13},{17,18},{18,... | collective-permute-start | bytes 3145736 | tf_op jit(solution)/shard_map/ppermute | solution.py:415
  212.9 3.0 %shard_map.145.attended_ref = bf16[256,1024]{1,0:T(8,128)(2,1)S(1)} custom-call(s32[4]{0:T(128)S(1)} %fusion.5.order_ref, s32[32]{0:T(128)S(1)} %xor.11.relative_ref, s32[32]{0:T(128)S(1)} %reshape.30.slots_ref, s32[16]{0:T(128)S(1)} %copy-done.7, bf16[256,1024]{1,0:T(8,128)(2,1)S(1)} %shard_map.137.refs_0_, bf16[8,128,1024]{2,1,0:T(8,128)(2,1)S(1)} %copy-done, ...), custom_call_target="tpu_custom_call" | custom-call | flops 1 | bytes 1 | tf_op jit(solution)/shard_map/pallas_call | solution.py:236
  216.0 3.2 %shard_map.146.attended_ref = bf16[256,1024]{1,0:T(8,128)(2,1)S(1)} custom-call(s32[4]{0:T(128)S(1)} %fusion.5.order_ref, s32[32]{0:T(128)S(1)} %xor.11.relative_ref, s32[32]{0:T(128)S(1)} %reshape.30.slots_ref, s32[16]{0:T(128)S(1)} %copy-done.7, bf16[256,1024]{1,0:T(8,128)(2,1)S(1)} %shard_map.136.refs_0_, bf16[8,128,1024]{2,1,0:T(8,128)(2,1)S(1)} %copy-done, ...), custom_call_target="tpu_custom_call" | custom-call | flops 1 | bytes 1 | tf_op jit(solution)/shard_map/pallas_call | solution.py:236
  219.2 11.3 %shard_map.147 = bf16[256,4096]{1,0:T(8,128)(2,1)} custom-call(s32[1]{0:T(128)} %bitcast.core_ref, bf16[256,1024]{1,0:T(8,128)(2,1)S(1)} %shard_map.142.attended_ref, bf16[256,1024]{1,0:T(8,128)(2,1)S(1)} %collective-permute-done.24.handed_ref, bf16[1024,4096]{1,0:T(8,128)(2,1)} %weight_ref.11, bf16[256,4096]{1,0:T(8,128)(2,1)} %copy-done.8, ...), custom_call_target="tpu_custom_call" | custom-call | flops 1 | bytes 1 | tf_op jit(solution)/shard_map/pallas_call | solution.py:330
  230.4 3.9 %shard_map.148 = bf16[256,2048]{1,0:T(8,128)(2,1)S(1)} custom-call(bf16[256,1024]{1,0:T(8,128)(2,1)S(1)} %shard_map.145.attended_ref, bf16[1024,4096]{1,0:T(8,128)(2,1)} %weight_ref.11, bf16[256,2048]{1,0:T(8,128)(2,1)S(1)} %collective-permute-done.25.plus_ref), custom_call_target="tpu_custom_call" | custom-call | flops 1 | bytes 1 | tf_op jit(solution)/shard_map/pallas_call | solution.py:330
  234.3 1.4 collective-permute-start.27
  235.8 6.5 %collective-permute-start.29 = (bf16[256,4096]{1,0:T(8,128)(2,1)}, bf16[256,4096]{1,0:T(8,128)(2,1)}, u32[]{:S(2)}, u32[]{:S(2)}) collective-permute-start(bf16[256,4096]{1,0:T(8,128)(2,1)} %shard_map.147), channel_id=1, source_target_pairs={{1,2},{2,1},{5,6},{6,5},{9,10},{10,9},{13,14},{14,13},{17,18},{18,... | collective-permute-start | bytes 6291464 | tf_op jit(solution)/shard_map/ppermute | solution.py:415
  242.3 1.3 collective-permute-start.28
  243.6 11.5 %collective-permute-done.28.handed_ref = bf16[256,1024]{1,0:T(8,128)(2,1)S(1)} collective-permute-done((bf16[256,1024]{1,0:T(8,128)(2,1)S(1)}, bf16[256,1024]{1,0:T(8,128)(2,1)S(1)}, u32[]{:S(2)}, u32[]{:S(2)}) %collective-permute-start.28) | collective-permute-done | bytes 524320 | tf_op jit(solution)/shard_map/ppermute | solution.py:415
  255.1 3.1 %collective-permute-done.27 = bf16[256,2048]{1,0:T(8,128)(2,1)S(1)} collective-permute-done((bf16[256,2048]{1,0:T(8,128)(2,1)S(1)}, bf16[256,2048]{1,0:T(8,128)(2,1)S(1)}, u32[]{:S(2)}, u32[]{:S(2)}) %collective-permute-start.27) | collective-permute-done | bytes 1048608 | tf_op jit(solution)/shard_map/ppermute | solution.py:415
  258.3 4.3 %shard_map.149 = bf16[256,2048]{1,0:T(8,128)(2,1)S(1)} custom-call(bf16[256,1024]{1,0:T(8,128)(2,1)S(1)} %shard_map.145.attended_ref, bf16[1024,4096]{1,0:T(8,128)(2,1)} %weight_ref.11, bf16[256,2048]{1,0:T(8,128)(2,1)S(1)} %collective-permute-done.26.plus_ref), custom_call_target="tpu_custom_call" | custom-call | flops 1 | bytes 1 | tf_op jit(solution)/shard_map/pallas_call | solution.py:330
  262.6 5.4 %collective-permute-start.30 = (bf16[256,2048]{1,0:T(8,128)(2,1)S(1)}, bf16[256,2048]{1,0:T(8,128)(2,1)}, u32[]{:S(2)}, u32[]{:S(2)}) collective-permute-start(bf16[256,2048]{1,0:T(8,128)(2,1)S(1)} %shard_map.149), channel_id=1, source_target_pairs={{1,0},{2,3},{5,4},{6,7},{9,8},{10,11},{13,12},{14,15},{17,16},{18,... | collective-permute-start | bytes 3145736 | tf_op jit(solution)/shard_map/ppermute | solution.py:415
  268.0 10.3 %shard_map.150 = bf16[256,4096]{1,0:T(8,128)(2,1)S(1)} custom-call(s32[1]{0:T(128)} %bitcast.core_ref, bf16[256,1024]{1,0:T(8,128)(2,1)S(1)} %shard_map.146.attended_ref, bf16[256,1024]{1,0:T(8,128)(2,1)S(1)} %collective-permute-done.28.handed_ref, bf16[1024,4096]{1,0:T(8,128)(2,1)} %weight_ref.11, bf16[256,4096]{1,0:T(8,128)(2,1)} %copy-done.8, ...), custom_call_target="tpu_custom_call" | custom-call | flops 1 | bytes 1 | tf_op jit(solution)/shard_map/pallas_call | solution.py:330
  278.3 15.9 %collective-permute-done.29 = bf16[256,4096]{1,0:T(8,128)(2,1)} collective-permute-done((bf16[256,4096]{1,0:T(8,128)(2,1)}, bf16[256,4096]{1,0:T(8,128)(2,1)}, u32[]{:S(2)}, u32[]{:S(2)}) %collective-permute-start.29) | collective-permute-done | bytes 2097184 | tf_op jit(solution)/shard_map/ppermute | solution.py:415
  294.2 3.7 %add_convert_fusion = bf16[256,4096]{1,0:T(8,128)(2,1)} fusion(bf16[256,4096]{1,0:T(8,128)(2,1)S(1)} %shard_map.150, bf16[256,2048]{1,0:T(8,128)(2,1)S(1)} %shard_map.149, bf16[256,2048]{1,0:T(8,128)(2,1)S(1)} %shard_map.148, bf16[256,4096]{1,0:T(8,128)(2,1)} %collective-permute-done.29, bf16[256,2048]{1,0:T(8,128)(2,1)} %collective-permute-done.30, ...), kind=kLoop, calls=%fused_computation.7 | loop fusion | flops 14680064 | bytes 10485761 | tf_op jit(solution)/shard_map/convert_element_type | solution.py:547
  (71 shorter events, 1.6 us)
Async XLA Ops:
  0.0 2.2 copy-start.11
  0.0 2.9 copy-start.14
  0.0 13.3 %collective-permute-start.2 = (bf16[8,128,1024]{2,1,0:T(8,128)(2,1)}, bf16[8,128,1024]{2,1,0:T(8,128)(2,1)S(1)}, u32[]{:S(2)}, u32[]{:S(2)}) collective-permute-start(bf16[8,128,1024]{2,1,0:T(8,128)(2,1)} %refs_1_.7), channel_id=1, source_target_pairs={{0,4},{4,0},{8,12},{12,8},{16,20},{20,16},{24,28},{28,24},{1,5},{5... | collective-permute-start | bytes 6291464 | tf_op jit(solution)/shard_map/ppermute | solution.py:411
  2.9 7.3 %copy-start = (bf16[8,128,1024]{2,1,0:T(8,128)(2,1)S(1)}, bf16[8,128,1024]{2,1,0:T(8,128)(2,1)}, u32[]{:S(2)}) copy-start(bf16[8,128,1024]{2,1,0:T(8,128)(2,1)} %refs_1_.7) | copy-start | bytes 6291460
  2.9 11.8 %copy-start.16 = (s32[16,2]{0,1:T(2,128)S(1)}, s32[16,2]{0,1:T(2,128)}, u32[]{:S(2)}) copy-start(s32[16,2]{0,1:T(2,128)} %param.20) | copy-start | bytes 388
  3.0 12.0 %copy-start.15 = (s32[16,2]{0,1:T(2,128)S(1)}, s32[16,2]{0,1:T(2,128)}, u32[]{:S(2)}) copy-start(s32[16,2]{0,1:T(2,128)} %param.21) | copy-start | bytes 388
  5.2 48.1 %collective-permute-start = (bf16[256,4096]{1,0:T(8,128)(2,1)}, bf16[256,4096]{1,0:T(8,128)(2,1)}, u32[]{:S(2)}, u32[]{:S(2)}) collective-permute-start(bf16[256,4096]{1,0:T(8,128)(2,1)} %fusion.4.refs_0_), channel_id=1, source_target_pairs={{0,1},{3,2},{1,0},{2,3},{4,5},{7,6},{5,4},{6,7},{8,9},{11,10},{9,8... | collective-permute-start | bytes 6291464 | tf_op jit(solution)/shard_map/ppermute | solution.py:415
  5.2 51.1 %collective-permute-start.1 = (bf16[256,4096]{1,0:T(8,128)(2,1)}, bf16[256,4096]{1,0:T(8,128)(2,1)}, u32[]{:S(2)}, u32[]{:S(2)}) collective-permute-start(bf16[256,4096]{1,0:T(8,128)(2,1)} %fusion.4.refs_0_), channel_id=1, source_target_pairs={{1,2},{2,1},{5,6},{6,5},{9,10},{10,9},{13,14},{14,13},{17,18},{18,... | collective-permute-start | bytes 6291464 | tf_op jit(solution)/shard_map/ppermute | solution.py:415
  10.2 47.4 %collective-permute-start.4 = (bf16[8,128,1024]{2,1,0:T(8,128)(2,1)S(1)}, bf16[8,128,1024]{2,1,0:T(8,128)(2,1)}, u32[]{:S(2)}, u32[]{:S(2)}) collective-permute-start(bf16[8,128,1024]{2,1,0:T(8,128)(2,1)S(1)} %copy-done), channel_id=1, source_target_pairs={{0,8},{4,12},{8,0},{12,4},{16,24},{20,28},{24,16},{28,20},{1,9},{5... | collective-permute-start | bytes 6291464 | tf_op jit(solution)/shard_map/ppermute | solution.py:411
  11.8 47.3 %collective-permute-start.5 = (bf16[8,128,1024]{2,1,0:T(8,128)(2,1)}, bf16[8,128,1024]{2,1,0:T(8,128)(2,1)}, u32[]{:S(2)}, u32[]{:S(2)}) collective-permute-start(bf16[8,128,1024]{2,1,0:T(8,128)(2,1)} %refs_9_.7), channel_id=1, source_target_pairs={{0,16},{4,20},{8,24},{12,28},{16,0},{20,4},{24,8},{28,12},{1,17},{... | collective-permute-start | bytes 6291464 | tf_op jit(solution)/shard_map/ppermute | solution.py:411
  13.3 1.4 copy-start.1
  14.7 44.3 %collective-permute-start.3 = (bf16[8,128,1024]{2,1,0:T(8,128)(2,1)}, bf16[8,128,1024]{2,1,0:T(8,128)(2,1)}, u32[]{:S(2)}, u32[]{:S(2)}) collective-permute-start(bf16[8,128,1024]{2,1,0:T(8,128)(2,1)} %refs_9_.7), channel_id=1, source_target_pairs={{0,4},{4,0},{8,12},{12,8},{16,20},{20,16},{24,28},{28,24},{1,5},{5... | collective-permute-start | bytes 6291464 | tf_op jit(solution)/shard_map/ppermute | solution.py:411
  15.8 52.3 %copy-start.18 = (s32[4]{0:T(128)S(1)}, s32[4]{0:T(128)}, u32[]{:S(2)}) copy-start(s32[4]{0:T(128)} %constant.62.clone) | copy-start | bytes 52
  15.8 52.9 %copy-start.17 = (s32[4]{0:T(128)S(1)}, s32[4]{0:T(128)}, u32[]{:S(2)}) copy-start(s32[4]{0:T(128)} %constant.63.clone) | copy-start | bytes 52
  59.1 47.9 %collective-permute-start.10 = (bf16[256,4096]{1,0:T(8,128)(2,1)S(1)}, bf16[256,4096]{1,0:T(8,128)(2,1)S(1)}, u32[]{:S(2)}, u32[]{:S(2)}) collective-permute-start(bf16[256,4096]{1,0:T(8,128)(2,1)S(1)} %get-tuple-element.77), channel_id=1, source_target_pairs={{0,1},{3,2},{4,5},{7,6},{8,9},{11,10},{12,13},{15,14},{16,17},{19,... | collective-permute-start | bytes 6291464 | tf_op jit(solution)/shard_map/ppermute | solution.py:415
  60.4 48.1 %collective-permute-start.6 = (bf16[256,4096]{1,0:T(8,128)(2,1)}, bf16[256,4096]{1,0:T(8,128)(2,1)S(1)}, u32[]{:S(2)}, u32[]{:S(2)}) collective-permute-start(bf16[256,4096]{1,0:T(8,128)(2,1)} %collective-permute-done.refs_1_), channel_id=1, source_target_pairs={{1,2},{2,1},{5,6},{6,5},{9,10},{10,9},{13,14},{14,13},{17,18},{18,... | collective-permute-start | bytes 6291464 | tf_op jit(solution)/shard_map/ppermute | solution.py:415
  62.6 46.8 %collective-permute-start.7 = (bf16[256,4096]{1,0:T(8,128)(2,1)}, bf16[256,4096]{1,0:T(8,128)(2,1)S(1)}, u32[]{:S(2)}, u32[]{:S(2)}) collective-permute-start(bf16[256,4096]{1,0:T(8,128)(2,1)} %collective-permute-done.1.refs_1_), channel_id=1, source_target_pairs={{1,0},{2,3},{5,4},{6,7},{9,8},{10,11},{13,12},{14,15},{17,16},{18,... | collective-permute-start | bytes 6291464 | tf_op jit(solution)/shard_map/ppermute | solution.py:415
  66.0 45.5 %collective-permute-start.8 = (bf16[8,128,1024]{2,1,0:T(8,128)(2,1)S(1)}, bf16[8,128,1024]{2,1,0:T(8,128)(2,1)S(1)}, u32[]{:S(2)}, u32[]{:S(2)}) collective-permute-start(bf16[8,128,1024]{2,1,0:T(8,128)(2,1)S(1)} %copy-done), channel_id=1, source_target_pairs={{0,16},{4,20},{8,24},{12,28},{16,0},{20,4},{24,8},{28,12},{1,17},{... | collective-permute-start | bytes 6291464 | tf_op jit(solution)/shard_map/ppermute | solution.py:411
  67.6 45.4 %collective-permute-start.9 = (bf16[8,128,1024]{2,1,0:T(8,128)(2,1)}, bf16[8,128,1024]{2,1,0:T(8,128)(2,1)S(1)}, u32[]{:S(2)}, u32[]{:S(2)}) collective-permute-start(bf16[8,128,1024]{2,1,0:T(8,128)(2,1)} %refs_9_.7), channel_id=1, source_target_pairs={{0,8},{4,12},{8,0},{12,4},{16,24},{20,28},{24,16},{28,20},{1,9},{5... | collective-permute-start | bytes 6291464 | tf_op jit(solution)/shard_map/ppermute | solution.py:411
  69.4 96.3 %slice-start = ((s8[8388608]{0:T(1024)(128)(4,1)}), s8[4194304]{0:T(1024)(128)(4,1)S(1)}, s32[]{:S(2)}) async-start(s8[8388608]{0:T(1024)(128)(4,1)} %bitcast.3), calls=%async_computation | async-start | bytes 8388608
  77.6 88.0 %slice-start.1 = ((s8[8388608]{0:T(1024)(128)(4,1)}), s8[4194304]{0:T(1024)(128)(4,1)S(1)}, s32[]{:S(2)}) async-start(s8[8388608]{0:T(1024)(128)(4,1)} %bitcast.3), calls=%async_computation.1 | async-start | bytes 8388608
  107.0 70.2 %copy-start.8 = (bf16[256,4096]{1,0:T(8,128)(2,1)}, bf16[256,4096]{1,0:T(8,128)(2,1)S(1)}, u32[]{:S(2)}) copy-start(bf16[256,4096]{1,0:T(8,128)(2,1)S(1)} %collective-permute-done.10.refs_0_) | copy-start | bytes 6291460
  113.0 12.3 %collective-permute-start.15 = (bf16[8,128,1024]{2,1,0:T(8,128)(2,1)}, bf16[8,128,1024]{2,1,0:T(8,128)(2,1)S(1)}, u32[]{:S(2)}, u32[]{:S(2)}) collective-permute-start(bf16[8,128,1024]{2,1,0:T(8,128)(2,1)} %collective-permute-done.4.refs_3_), channel_id=1, source_target_pairs={{0,4},{4,0},{8,12},{12,8},{16,20},{20,16},{24,28},{28,24},{1,5},{5... | collective-permute-start | bytes 6291464 | tf_op jit(solution)/shard_map/ppermute | solution.py:411
  113.0 47.1 %collective-permute-start.11 = (bf16[256,4096]{1,0:T(8,128)(2,1)S(1)}, bf16[256,4096]{1,0:T(8,128)(2,1)S(1)}, u32[]{:S(2)}, u32[]{:S(2)}) collective-permute-start(bf16[256,4096]{1,0:T(8,128)(2,1)S(1)} %collective-permute-done.6.refs_0_), channel_id=1, source_target_pairs={{1,0},{2,3},{5,4},{6,7},{9,8},{10,11},{13,12},{14,15},{17,16},{18,... | collective-permute-start | bytes 6291464 | tf_op jit(solution)/shard_map/ppermute | solution.py:415
  114.6 48.2 %collective-permute-start.12 = (bf16[8,128,1024]{2,1,0:T(8,128)(2,1)}, bf16[8,128,1024]{2,1,0:T(8,128)(2,1)S(1)}, u32[]{:S(2)}, u32[]{:S(2)}) collective-permute-start(bf16[8,128,1024]{2,1,0:T(8,128)(2,1)} %collective-permute-done.4.refs_3_), channel_id=1, source_target_pairs={{0,16},{4,20},{8,24},{12,28},{16,0},{20,4},{24,8},{28,12},{1,17},{... | collective-permute-start | bytes 6291464 | tf_op jit(solution)/shard_map/ppermute | solution.py:411
  115.5 47.7 %collective-permute-start.13 = (bf16[8,128,1024]{2,1,0:T(8,128)(2,1)}, bf16[8,128,1024]{2,1,0:T(8,128)(2,1)S(1)}, u32[]{:S(2)}, u32[]{:S(2)}) collective-permute-start(bf16[8,128,1024]{2,1,0:T(8,128)(2,1)} %collective-permute-done.5.refs_13_), channel_id=1, source_target_pairs={{0,8},{4,12},{8,0},{12,4},{16,24},{20,28},{24,16},{28,20},{1,9},{5... | collective-permute-start | bytes 6291464 | tf_op jit(solution)/shard_map/ppermute | solution.py:411
  116.0 49.2 %collective-permute-start.14 = (bf16[256,4096]{1,0:T(8,128)(2,1)S(1)}, bf16[256,4096]{1,0:T(8,128)(2,1)}, u32[]{:S(2)}, u32[]{:S(2)}) collective-permute-start(bf16[256,4096]{1,0:T(8,128)(2,1)S(1)} %get-tuple-element.83), channel_id=1, source_target_pairs={{0,1},{3,2},{4,5},{7,6},{8,9},{11,10},{12,13},{15,14},{16,17},{19,... | collective-permute-start | bytes 6291464 | tf_op jit(solution)/shard_map/ppermute | solution.py:415
  125.2 48.0 %copy-start.2 = (bf16[8,128,1024]{2,1,0:T(8,128)(2,1)S(1)}, bf16[8,128,1024]{2,1,0:T(8,128)(2,1)}, u32[]{:S(2)}) copy-start(bf16[8,128,1024]{2,1,0:T(8,128)(2,1)} %copy-done.1) | copy-start | bytes 6291460
  125.2 48.0 %copy-start.7 = (s32[16]{0:T(128)S(1)}, s32[16]{0:T(128)}, u32[]{:S(2)}) copy-start(s32[16]{0:T(128)} %counts_ref.7) | copy-start | bytes 196
  125.2 45.3 %collective-permute-start.19 = (bf16[8,128,1024]{2,1,0:T(8,128)(2,1)}, bf16[8,128,1024]{2,1,0:T(8,128)(2,1)S(1)}, u32[]{:S(2)}, u32[]{:S(2)}) collective-permute-start(bf16[8,128,1024]{2,1,0:T(8,128)(2,1)} %collective-permute-done.5.refs_13_), channel_id=1, source_target_pairs={{0,4},{4,0},{8,12},{12,8},{16,20},{20,16},{24,28},{28,24},{1,5},{5... | collective-permute-start | bytes 6291464 | tf_op jit(solution)/shard_map/ppermute | solution.py:411
  160.1 10.5 %collective-permute-start.16 = (bf16[8,128,1024]{2,1,0:T(8,128)(2,1)S(1)}, bf16[8,128,1024]{2,1,0:T(8,128)(2,1)S(1)}, u32[]{:S(2)}, u32[]{:S(2)}) collective-permute-start(bf16[8,128,1024]{2,1,0:T(8,128)(2,1)S(1)} %collective-permute-done.8.refs_5_), channel_id=1, source_target_pairs={{0,4},{4,0},{8,12},{12,8},{16,20},{20,16},{24,28},{28,24},{1,5},{5... | collective-permute-start | bytes 6291464 | tf_op jit(solution)/shard_map/ppermute | solution.py:411
  162.7 7.8 %collective-permute-start.18 = (bf16[8,128,1024]{2,1,0:T(8,128)(2,1)S(1)}, bf16[8,128,1024]{2,1,0:T(8,128)(2,1)S(1)}, u32[]{:S(2)}, u32[]{:S(2)}) collective-permute-start(bf16[8,128,1024]{2,1,0:T(8,128)(2,1)S(1)} %collective-permute-done.9.refs_11_), channel_id=1, source_target_pairs={{0,4},{4,0},{8,12},{12,8},{16,20},{20,16},{24,28},{28,24},{1,5},{5... | collective-permute-start | bytes 6291464 | tf_op jit(solution)/shard_map/ppermute | solution.py:411
  165.2 5.4 %collective-permute-start.17 = (bf16[8,128,1024]{2,1,0:T(8,128)(2,1)S(1)}, bf16[8,128,1024]{2,1,0:T(8,128)(2,1)S(1)}, u32[]{:S(2)}, u32[]{:S(2)}) collective-permute-start(bf16[8,128,1024]{2,1,0:T(8,128)(2,1)S(1)} %collective-permute-done.12.refs_7_), channel_id=1, source_target_pairs={{0,4},{4,0},{8,12},{12,8},{16,20},{20,16},{24,28},{28,24},{1,5},{5... | collective-permute-start | bytes 6291464 | tf_op jit(solution)/shard_map/ppermute | solution.py:411
  165.2 8.1 %collective-permute-start.20 = (bf16[8,128,1024]{2,1,0:T(8,128)(2,1)S(1)}, bf16[8,128,1024]{2,1,0:T(8,128)(2,1)S(1)}, u32[]{:S(2)}, u32[]{:S(2)}) collective-permute-start(bf16[8,128,1024]{2,1,0:T(8,128)(2,1)S(1)} %collective-permute-done.13.refs_15_), channel_id=1, source_target_pairs={{0,4},{4,0},{8,12},{12,8},{16,20},{20,16},{24,28},{28,24},{1,5},{5... | collective-permute-start | bytes 6291464 | tf_op jit(solution)/shard_map/ppermute | solution.py:411
  170.6 6.7 %copy-start.3 = (bf16[8,128,1024]{2,1,0:T(8,128)(2,1)}, bf16[8,128,1024]{2,1,0:T(8,128)(2,1)S(1)}, u32[]{:S(2)}) copy-start(bf16[8,128,1024]{2,1,0:T(8,128)(2,1)S(1)} %collective-permute-done.18.refs_12_) | copy-start | bytes 6291460
  173.3 4.0 %copy-start.5 = (bf16[8,128,1024]{2,1,0:T(8,128)(2,1)}, bf16[8,128,1024]{2,1,0:T(8,128)(2,1)S(1)}, u32[]{:S(2)}) copy-start(bf16[8,128,1024]{2,1,0:T(8,128)(2,1)S(1)} %collective-permute-done.20.refs_16_) | copy-start | bytes 6291460
  177.3 16.8 %collective-permute-start.22 = (bf16[256,4096]{1,0:T(8,128)(2,1)S(1)}, bf16[256,4096]{1,0:T(8,128)(2,1)S(1)}, u32[]{:S(2)}, u32[]{:S(2)}) collective-permute-start(bf16[256,4096]{1,0:T(8,128)(2,1)S(1)} %collective-permute-done.10.refs_0_), channel_id=1, source_target_pairs={{0,4},{4,0},{8,12},{12,8},{16,20},{20,16},{24,28},{28,24},{1,5},{5... | collective-permute-start | bytes 6291464 | tf_op jit(solution)/shard_map/ppermute | solution.py:411
  177.3 5.9 %copy-start.4 = (bf16[8,128,1024]{2,1,0:T(8,128)(2,1)S(1)}, bf16[8,128,1024]{2,1,0:T(8,128)(2,1)}, u32[]{:S(2)}) copy-start(bf16[8,128,1024]{2,1,0:T(8,128)(2,1)} %copy-done.3) | copy-start | bytes 6291460
  177.4 5.9 %copy-start.6 = (bf16[8,128,1024]{2,1,0:T(8,128)(2,1)S(1)}, bf16[8,128,1024]{2,1,0:T(8,128)(2,1)}, u32[]{:S(2)}) copy-start(bf16[8,128,1024]{2,1,0:T(8,128)(2,1)} %copy-done.5) | copy-start | bytes 6291460
  177.4 16.7 %collective-permute-start.23 = (bf16[256,4096]{1,0:T(8,128)(2,1)}, bf16[256,4096]{1,0:T(8,128)(2,1)S(1)}, u32[]{:S(2)}, u32[]{:S(2)}) collective-permute-start(bf16[256,4096]{1,0:T(8,128)(2,1)} %collective-permute-done.14.refs_1_), channel_id=1, source_target_pairs={{0,4},{4,0},{8,12},{12,8},{16,20},{20,16},{24,28},{28,24},{1,5},{5... | collective-permute-start | bytes 6291464 | tf_op jit(solution)/shard_map/ppermute | solution.py:411
  177.8 16.2 %collective-permute-start.21 = (bf16[256,1024]{1,0:T(8,128)(2,1)S(1)}, bf16[256,1024]{1,0:T(8,128)(2,1)S(1)}, u32[]{:S(2)}, u32[]{:S(2)}) collective-permute-start(bf16[256,1024]{1,0:T(8,128)(2,1)S(1)} %shard_map.140.attended_ref), channel_id=1, source_target_pairs={{0,1},{3,2},{4,5},{7,6},{8,9},{11,10},{12,13},{15,14},{16,17},{19,... | collective-permute-start | bytes 1572872 | tf_op jit(solution)/shard_map/ppermute | solution.py:415
  194.1 1.3 copy-start.9
  194.1 2.1 copy-start.10
  200.1 30.3 %collective-permute-start.25 = (bf16[256,2048]{1,0:T(8,128)(2,1)S(1)}, bf16[256,2048]{1,0:T(8,128)(2,1)S(1)}, u32[]{:S(2)}, u32[]{:S(2)}) collective-permute-start(bf16[256,2048]{1,0:T(8,128)(2,1)S(1)} %shard_map.143), channel_id=1, source_target_pairs={{1,2},{2,1},{5,6},{6,5},{9,10},{10,9},{13,14},{14,13},{17,18},{18,... | collective-permute-start | bytes 3145736 | tf_op jit(solution)/shard_map/ppermute | solution.py:415
  202.1 17.1 %collective-permute-start.24 = (bf16[256,1024]{1,0:T(8,128)(2,1)S(1)}, bf16[256,1024]{1,0:T(8,128)(2,1)S(1)}, u32[]{:S(2)}, u32[]{:S(2)}) collective-permute-start(bf16[256,1024]{1,0:T(8,128)(2,1)S(1)} %shard_map.142.attended_ref), channel_id=1, source_target_pairs={{0,1},{3,2},{4,5},{7,6},{8,9},{11,10},{12,13},{15,14},{16,17},{19,... | collective-permute-start | bytes 1572872 | tf_op jit(solution)/shard_map/ppermute | solution.py:415
  208.8 46.3 %collective-permute-start.26 = (bf16[256,2048]{1,0:T(8,128)(2,1)S(1)}, bf16[256,2048]{1,0:T(8,128)(2,1)S(1)}, u32[]{:S(2)}, u32[]{:S(2)}) collective-permute-start(bf16[256,2048]{1,0:T(8,128)(2,1)S(1)} %shard_map.144), channel_id=1, source_target_pairs={{1,2},{2,1},{5,6},{6,5},{9,10},{10,9},{13,14},{14,13},{17,18},{18,... | collective-permute-start | bytes 3145736 | tf_op jit(solution)/shard_map/ppermute | solution.py:415
  234.3 23.9 %collective-permute-start.27 = (bf16[256,2048]{1,0:T(8,128)(2,1)S(1)}, bf16[256,2048]{1,0:T(8,128)(2,1)S(1)}, u32[]{:S(2)}, u32[]{:S(2)}) collective-permute-start(bf16[256,2048]{1,0:T(8,128)(2,1)S(1)} %shard_map.148), channel_id=1, source_target_pairs={{1,0},{2,3},{5,4},{6,7},{9,8},{10,11},{13,12},{14,15},{17,16},{18,... | collective-permute-start | bytes 3145736 | tf_op jit(solution)/shard_map/ppermute | solution.py:415
  235.8 58.4 %collective-permute-start.29 = (bf16[256,4096]{1,0:T(8,128)(2,1)}, bf16[256,4096]{1,0:T(8,128)(2,1)}, u32[]{:S(2)}, u32[]{:S(2)}) collective-permute-start(bf16[256,4096]{1,0:T(8,128)(2,1)} %shard_map.147), channel_id=1, source_target_pairs={{1,2},{2,1},{5,6},{6,5},{9,10},{10,9},{13,14},{14,13},{17,18},{18,... | collective-permute-start | bytes 6291464 | tf_op jit(solution)/shard_map/ppermute | solution.py:415
  242.3 12.8 %collective-permute-start.28 = (bf16[256,1024]{1,0:T(8,128)(2,1)S(1)}, bf16[256,1024]{1,0:T(8,128)(2,1)S(1)}, u32[]{:S(2)}, u32[]{:S(2)}) collective-permute-start(bf16[256,1024]{1,0:T(8,128)(2,1)S(1)} %shard_map.146.attended_ref), channel_id=1, source_target_pairs={{0,1},{3,2},{4,5},{7,6},{8,9},{11,10},{12,13},{15,14},{16,17},{19,... | collective-permute-start | bytes 1572872 | tf_op jit(solution)/shard_map/ppermute | solution.py:415
  258.3 4.3 %copy-start.12 = (bf16[256,2048]{1,0:T(8,128)(2,1)}, bf16[256,2048]{1,0:T(8,128)(2,1)S(1)}, u32[]{:S(2)}) copy-start(bf16[256,2048]{1,0:T(8,128)(2,1)S(1)} %collective-permute-done.27) | copy-start | bytes 3145732
  262.6 31.6 %collective-permute-start.30 = (bf16[256,2048]{1,0:T(8,128)(2,1)S(1)}, bf16[256,2048]{1,0:T(8,128)(2,1)}, u32[]{:S(2)}, u32[]{:S(2)}) collective-permute-start(bf16[256,2048]{1,0:T(8,128)(2,1)S(1)} %shard_map.149), channel_id=1, source_target_pairs={{1,0},{2,3},{5,4},{6,7},{9,8},{10,11},{13,12},{14,15},{17,16},{18,... | collective-permute-start | bytes 3145736 | tf_op jit(solution)/shard_map/ppermute | solution.py:415
  268.0 26.2 %copy-start.13 = (bf16[256,2048]{1,0:T(8,128)(2,1)S(1)}, bf16[256,2048]{1,0:T(8,128)(2,1)}, u32[]{:S(2)}) copy-start(bf16[256,2048]{1,0:T(8,128)(2,1)} %copy-done.12) | copy-start | bytes 3145732
